TPU v7x, 32 devices: a whole 2x2x4 slice. The times are simulated.
32 devices in a mesh: fsdp: 8 (over y, x, core), tensor: 4 (over z).
Axes of the slice: x: 2, y: 2, z: 4, core: 2. Of those that a mesh axis runs over, the one named last changes fastest.
Arguments:
- tokens: bfloat16 [8192, 768], P(('fsdp', 'tensor')), may hold values from -6 to 6
- ln_attn: bfloat16 [768], P('fsdp'), may hold values from 0.25 to 1.75
- ln_ff: bfloat16 [768], P('fsdp'), may hold values from 0.25 to 1.75
- ln_global: bfloat16 [768], P('fsdp'), may hold values from 0.25 to 1.75
- w_query: bfloat16 [768, 768], P('fsdp', 'tensor'), may hold values from -0.02734375 to 0.02734375
- w_key: bfloat16 [768, 768], P('fsdp', 'tensor'), may hold values from -0.21875 to 0.21875
- w_value: bfloat16 [768, 768], P('fsdp', 'tensor'), may hold values from -0.21875 to 0.21875
- w_out: bfloat16 [768, 768], P('tensor', 'fsdp'), may hold values from -1.25 to 1.25
- wi_gate: bfloat16 [768, 2048], P('fsdp', 'tensor'), may hold values from -0.21875 to 0.21875
- wi_up: bfloat16 [768, 2048], P('fsdp', 'tensor'), may hold values from -0.21875 to 0.21875
- wo_ff: bfloat16 [2048, 768], P('tensor', 'fsdp'), may hold values from -0.1875 to 0.1875
- table_local: bfloat16 [32, 12], P(None, 'tensor'), may hold values from -4 to 4
- table_global: bfloat16 [32, 12], P(None, 'tensor'), may hold values from -4 to 4
- local_onehot: int32 [128, 384, 32], replicated, may hold values from 0 to 1, as said below
- global_onehot: int32 [64, 64, 32], replicated, may hold values from 0 to 1, as said below
- segment: int32 [8, 1024], P('fsdp'), may hold values from 0 to 7, never falling along the last dimension, each value on 1 to 512 neighbouring positions
- grad_out: bfloat16 [8192, 768], P(('fsdp', 'tensor')), may hold values from -6 to 6
Outputs:
- output: bfloat16 [8192, 768], P(('fsdp', 'tensor'))
- grad_tokens: float32 [8192, 768], P(('fsdp', 'tensor'))
- grad_ln_attn: float32 [768], P('fsdp')
- grad_ln_ff: float32 [768], P('fsdp')
- grad_ln_global: float32 [768], P('fsdp')
- grad_w_query: float32 [768, 768], P('fsdp', 'tensor')
- grad_w_key: float32 [768, 768], P('fsdp', 'tensor')
- grad_w_value: float32 [768, 768], P('fsdp', 'tensor')
- grad_w_out: float32 [768, 768], P('tensor', 'fsdp')
- grad_wi_gate: float32 [768, 2048], P('fsdp', 'tensor')
- grad_wi_up: float32 [768, 2048], P('fsdp', 'tensor')
- grad_wo_ff: float32 [2048, 768], P('tensor', 'fsdp')
- grad_table_local: float32 [32, 12], P(None, 'tensor')
- grad_table_global: float32 [32, 12], P(None, 'tensor')
Inputs may be any that keep to these rules, and one draw needn't show every extreme that they name: `local_onehot`: each row of the last dimension holds exactly one 1; the bucket depends only on the offset j - 128 - i. `global_onehot`: each row of the last dimension holds exactly one 1; the bucket depends only on the offset a - b. `segment`: in each sequence document numbers never fall; each of the 8 documents holds 1 to 512 positions, and one holds exactly 512.
All inputs are finite; a program needn't handle non-finite values.
Results may differ from a plain program's by a relative error of at most 0.017.
Values may be sent and summed in bfloat16 or wider, within the bound.
No kernel may reach another device: no remote copies, remote signals or barrier semaphores. Data moves between devices by JAX's collectives and lax.ppermute only.
A program may use at most 128 MiB of HBM per device.

v0:
```python
import jax
import jax.numpy as jnp
from jax import lax
from jax.experimental import pallas as pl
from jax.experimental.pallas import tpu as pltpu
from jax.sharding import PartitionSpec as P


D = 768
HEADS = 12
BUCKETS = 32
BLOCK = 128
GBLOCK = 16
SLOTS = 64
ROWS = 256
FAR = 32
EXT = ROWS + 2 * BLOCK
ALL = EXT + 4 * FAR
KEYS = 3 * BLOCK + 4 * FAR
HALF = D // 2
FFS = 512
WIDE = 3 * FFS + D

f32 = jnp.float32
bf16 = jnp.bfloat16
tiny_eps = 1e-06
masked_score = -1e30
highest = lax.Precision.HIGHEST


def dot(a, b):
    return lax.dot_general(a, b, (((1,), (0,)), ((), ())), preferred_element_type=f32)


def dot_nt(a, b):
    return lax.dot_general(a, b, (((1,), (1,)), ((), ())), preferred_element_type=f32)


def dot_tn(a, b):
    return lax.dot_general(a, b, (((0,), (0,)), ((), ())), preferred_element_type=f32)


def whole_spec(shape):
    return pl.BlockSpec(shape, lambda i: (0,) * len(shape))


def slab_spec(shape):
    return pl.BlockSpec((1,) + shape, lambda i: (i,) + (0,) * len(shape))


def shape_of(shape, dtype):
    return jax.ShapeDtypeStruct(shape, dtype)


def rsqrt_mean(v):
    return lax.rsqrt(jnp.mean(v * v, axis=-1, keepdims=True) + tiny_eps)


def row_term(v, r, gain, e):
    eg = e * gain
    return r * eg - v * (r * r * r) * jnp.mean(eg * v, axis=-1, keepdims=True)


def eye(rows, cols):
    at = lax.broadcasted_iota(jnp.int32, (rows, cols), 0)
    return (at == lax.broadcasted_iota(jnp.int32, (rows, cols), 1)).astype(bf16)


def pack_kernel(wq, wk, wv, wo, gate, up, down_t, out):
    rows = wq.shape[0]
    out_t = dot_nt(eye(rows, rows), wo[...]).astype(bf16)
    out[:, 0:FFS] = gate[...]
    out[:, FFS : 2 * FFS] = up[...]
    out[:, 2 * FFS : 3 * FFS] = down_t[...]
    at = 3 * FFS
    out[:, at : at + 128] = wq[:, 0:128]
    out[:, at + 128 : at + 256] = wk[:, 0:128]
    out[:, at + 256 : at + 384] = wv[:, 0:128]
    out[:, at + 384 : at + 512] = jnp.concatenate([wq[:, 128:192], wv[:, 128:192]], axis=1)
    out[:, at + 512 : at + 640] = jnp.concatenate([wk[:, 128:192], out_t[:, 128:192]], axis=1)
    out[:, at + 640 : at + 768] = out_t[:, 0:128]


def pack(*shards):
    return pl.pallas_call(
        pack_kernel, out_shape=shape_of((shards[0].shape[0], WIDE), bf16), name="pack"
    )(*shards)


def prep_kernel(left, tok, right, grad, order, gains, mem, tables, x, tokp, gop, pooled_ref, far):
    turn = order[...]
    gain = gains[0:1]
    for base, ref in ((0, left), (BLOCK, tok), (BLOCK + ROWS, right)):
        v = dot(ref[...], turn)
        x[base : base + ref.shape[0]] = (v * rsqrt_mean(v) * gain).astype(bf16)
        if ref is tok:
            tokp[...] = v.astype(bf16)
    gop[...] = dot(grad[...], turn).astype(bf16)
    pooled = dot(mem[...], x[BLOCK : BLOCK + ROWS])
    pooled_ref[...] = pooled
    rows = (pooled * rsqrt_mean(pooled) * gains[2:3]).astype(bf16)
    at = lax.broadcasted_iota(jnp.int32, rows.shape, 0)
    far[...] = jnp.where(at == FAR - 1, jnp.broadcast_to(tables[...], rows.shape), rows)


def prep(*args):
    return pl.pallas_call(
        prep_kernel,
        out_shape=[
            shape_of((EXT, D), bf16),
            shape_of((ROWS, D), bf16),
            shape_of((ROWS, D), bf16),
            shape_of((FAR, D), f32),
            shape_of((FAR, D), bf16),
        ],
        name="prep",
    )(*args)


def join(w_s, halves, step):
    for n in range(2):

        @pl.when(step == n)
        def _(n=n):
            w_s[0:HALF, :] = halves[2 * n][...]
            w_s[HALF:D, :] = halves[2 * n + 1][...]


attn_specs = [pl.BlockSpec((HALF, D), lambda i: (0, 2))] * 4
ff_specs = [pl.BlockSpec((HALF, 3 * FFS), lambda i: (0, 0))] * 4


def keys_of(tile, c):
    return jnp.concatenate([tile[c * BLOCK : c * BLOCK + 3 * BLOCK], tile[EXT:ALL]], axis=0)


def fill_x(x_s, x, fars):
    x_s[0:EXT] = x[...]
    for n, ref in enumerate(fars):
        x_s[EXT + n * FAR : EXT + n * FAR + FAR] = ref[...]


def turned(value, back):
    at = lax.broadcasted_iota(jnp.int32, value.shape, 0)
    size = value.shape[1]
    for bit in range(7):
        step = 1 << bit
        moved = pltpu.roll(value, size - step if back else step, 1)
        value = jnp.where((at >> bit) & 1 == 1, moved, value)
    return value


def attn_fwd_kernel(base, last, *refs):
    x, f0, f1, f2, f3 = refs[:5]
    halves = refs[5:9]
    near_at, far_at, tables, mask = refs[9:13]
    refs = refs[13:]
    if last:
        before, tok, gains = refs[:3]
        refs = refs[3:]
        res, nf, p_ref, r_ref, a_ref, acc, x_s, w_s = refs
    else:
        acc, p_ref, r_ref, a_ref, x_s, w_s = refs
    step = pl.program_id(0)

    @pl.when(step == 0)
    def _():
        fill_x(x_s, x, (f0, f1, f2, f3))

    join(w_s, halves, step)
    r = dot(x_s[...], w_s[:, 0:640]).astype(bf16)
    r_ref[0] = r
    low = lax.broadcasted_iota(jnp.int32, (BLOCK, 128), 1) < 64
    zero = jnp.zeros((BLOCK, 128), bf16)
    near_index = near_at[...]
    far_index = far_at[...]
    parts = [[None] * 3, [None] * 3]
    for j in range(3):
        head = (base + step) * 3 + j
        diagonal = jnp.zeros((1, 3 * BLOCK), f32)
        slots = jnp.zeros((16, 128), f32)
        for n in range(BUCKETS):
            diagonal = jnp.where(near_index == n, tables[head, n], diagonal)
            slots = jnp.where(far_index == n, tables[HEADS + head, n], slots)
        near = turned(jnp.broadcast_to(diagonal, (BLOCK, 3 * BLOCK)), False)
        q_all = r[:, 0:128] if j < 2 else r[:, 384:512]
        k_all = r[:, 128:256] if j < 2 else r[:, 512:640]
        v_all = r[:, 256:384] if j < 2 else r[:, 384:512]
        for c in range(2):
            q = q_all[BLOCK + c * BLOCK : 2 * BLOCK + c * BLOCK]
            q = jnp.where(low, zero, q) if j == 1 else jnp.where(low, q, zero)
            far = jnp.broadcast_to(slots[c * 8 : c * 8 + 8][:, None], (8, GBLOCK, 128)).reshape(BLOCK, 128)
            s = dot_nt(q, keys_of(k_all, c)) + jnp.concatenate([near, far], axis=1) + mask[c]
            e = jnp.exp(s - jnp.max(s, axis=-1, keepdims=True))
            p = (e * (1.0 / jnp.sum(e, axis=-1, keepdims=True))).astype(bf16)
            p_ref[0, c * 3 + j] = p
            parts[c][j] = dot(p, keys_of(v_all, c))
    for c in range(2):
        a_ref[0, c * BLOCK : c * BLOCK + BLOCK] = jnp.concatenate(
            [jnp.where(low, 0.0, parts[c][2]), jnp.where(low, parts[c][0], parts[c][1])], axis=1
        ).astype(bf16)
    part = dot_nt(a_ref[0], w_s[:, 512:768])

    @pl.when(step == 0)
    def _():
        acc[...] = before[...] + part if last else part

    @pl.when(step > 0)
    def _():
        acc[...] += part

    if last:

        @pl.when(step == pl.num_programs(0) - 1)
        def _():
            v = tok[...].astype(f32) + acc[...]
            res[...] = v
            nf[...] = (v * rsqrt_mean(v) * gains[1:2]).astype(bf16)


x_specs = [whole_spec((EXT, D))] + [whole_spec((FAR, D))] * 4


def attn_fwd(base, x, fars, halves, near_at, far_at, tables, mask, *rest):
    last = len(rest) > 0
    outs = [
        (slab_spec((6, BLOCK, KEYS)), shape_of((2, 6, BLOCK, KEYS), bf16)),
        (slab_spec((ALL, 640)), shape_of((2, ALL, 640), bf16)),
        (slab_spec((ROWS, 256)), shape_of((2, ROWS, 256), bf16)),
    ]
    wide = (whole_spec((ROWS, D)), shape_of((ROWS, D), f32))
    if last:
        outs = [wide, (whole_spec((ROWS, D)), shape_of((ROWS, D), bf16))] + outs
    else:
        outs = [wide] + outs
    return pl.pallas_call(
        lambda *refs: attn_fwd_kernel(base, last, *refs),
        grid=(2,),
        in_specs=x_specs
        + attn_specs
        + [
            whole_spec((1, 3 * BLOCK)),
            whole_spec((16, 128)),
            pl.BlockSpec(memory_space=pltpu.SMEM),
            whole_spec((2, BLOCK, KEYS)),
        ]
        + ([whole_spec((ROWS, D)), whole_spec((ROWS, D)), whole_spec((8, D))] if last else []),
        out_specs=[o[0] for o in outs],
        out_shape=[o[1] for o in outs],
        scratch_shapes=([pltpu.VMEM((ROWS, D), f32)] if last else [])
        + [pltpu.VMEM((ALL, D), bf16), pltpu.VMEM((D, D), bf16)],
        name="attn_fwd_b" if last else "attn_fwd_a",
    )(x, *fars, *halves, near_at, far_at, tables, mask, *rest)


def attn_bwd_kernel(last, *refs):
    x, f0, f1, f2, f3, rl = refs[:6]
    halves = refs[6:10]
    r_ref, p_ref, a_ref = refs[10:13]
    refs = refs[13:]
    if last:
        before = refs[0]
        down, doth, near_ref, far_ref, own, lo, hi, fown, s1, s2, s3, xg, x_s, w_s, dr_s = refs[1:]
    else:
        down, doth, near_ref, far_ref, xg, x_s, w_s, dr_s = refs
    step = pl.program_id(0)

    @pl.when(step == 0)
    def _():
        fill_x(x_s, x, (f0, f1, f2, f3))

    join(w_s, halves, step)
    da = dot(rl[...], w_s[:, 512:768]).astype(bf16)
    low = lax.broadcasted_iota(jnp.int32, (BLOCK, 128), 1) < 64
    zero = jnp.zeros((BLOCK, 128), bf16)
    r = r_ref[0]
    dr_s[...] = jnp.zeros((ALL, 640), f32)

    def add_keys(n, c, value):
        lanes = slice(n * 128, n * 128 + 128)
        dr_s[c * BLOCK : c * BLOCK + 3 * BLOCK, lanes] += value[: 3 * BLOCK]
        dr_s[EXT:ALL, lanes] += value[3 * BLOCK :]

    near = [None, None, None]
    for c in range(2):
        rows = slice(BLOCK + c * BLOCK, 2 * BLOCK + c * BLOCK)
        held = None
        for j in range(3):
            p = p_ref[0, c * 3 + j]
            q = r[rows, 0:128] if j < 2 else r[rows, 384:512]
            q = jnp.where(low, zero, q) if j == 1 else jnp.where(low, q, zero)
            k = keys_of(r[:, 128:256] if j < 2 else r[:, 512:640], c)
            v = keys_of(r[:, 256:384] if j < 2 else r[:, 384:512], c)
            do = da[c * BLOCK : c * BLOCK + BLOCK, (128 if j < 2 else 0) : (256 if j < 2 else 128)]
            do = jnp.where(low, do, zero) if j == 0 else jnp.where(low, zero, do)
            wide = p.astype(f32)
            dp = dot_nt(do, v)
            ds = wide * (dp - jnp.sum(wide * dp, axis=-1, keepdims=True))
            near[j] = ds[:, : 3 * BLOCK] if c == 0 else near[j] + ds[:, : 3 * BLOCK]
            far_ref[0, j, c * 8 : c * 8 + 8] = jnp.sum(
                ds[:, 3 * BLOCK :].reshape(8, GBLOCK, 128), axis=1
            )
            dl = ds.astype(bf16)
            dq = dot(dl, k)
            add_keys(1 if j < 2 else 4, c, dot_tn(dl, q))
            add_keys(2 if j < 2 else 3, c, dot_tn(p, do))
            if j == 0:
                held = dq
            elif j == 1:
                dr_s[rows, 0:128] = jnp.where(low, held, dq)
            else:
                dr_s[rows, 384:512] += jnp.where(low, dq, 0.0)
    for j in range(3):
        near_ref[0, j : j + 1] = jnp.sum(turned(near[j], True), axis=0, keepdims=True)
    dr = dr_s[...].astype(bf16)
    part = dot_nt(dr, w_s[:, 0:640])

    @pl.when(step == 0)
    def _():
        xg[...] = before[...] + part if last else part

    @pl.when(step > 0)
    def _():
        xg[...] += part

    for ref, base in ((down, 0), (doth, HALF)):
        g = dot_tn(x_s[:, base : base + HALF], dr)
        go = dot_tn(rl[:, base : base + HALF], a_ref[0])
        ref[0, :, 0:512] = g[:, 0:512].astype(bf16)
        ref[0, :, 512:640] = (g[:, 512:640] + go[:, 0:128]).astype(bf16)
        ref[0, :, 640:768] = go[:, 128:256].astype(bf16)
    if last:

        @pl.when(step == pl.num_programs(0) - 1)
        def _():
            lo[...] = xg[0:BLOCK].astype(bf16)
            own[...] = xg[BLOCK : BLOCK + ROWS]
            hi[...] = xg[BLOCK + ROWS : EXT].astype(bf16)
            fown[...] = xg[EXT : EXT + FAR]
            for n, ref in enumerate((s1, s2, s3)):
                ref[...] = xg[EXT + FAR + n * FAR : EXT + 2 * FAR + n * FAR].astype(bf16)


def attn_bwd(x, fars, rl, halves, r, p, a, *rest):
    last = len(rest) > 0
    outs = [
        (slab_spec((HALF, D)), shape_of((2, HALF, D), bf16)),
        (slab_spec((HALF, D)), shape_of((2, HALF, D), bf16)),
        (slab_spec((3, 3 * BLOCK)), shape_of((2, 3, 3 * BLOCK), f32)),
        (slab_spec((3, 16, 128)), shape_of((2, 3, 16, 128), f32)),
    ]
    if last:
        for rows, dtype in ((ROWS, f32), (BLOCK, bf16), (BLOCK, bf16), (FAR, f32)) + ((FAR, bf16),) * 3:
            outs.append((whole_spec((rows, D)), shape_of((rows, D), dtype)))
    else:
        outs.append((whole_spec((ALL, D)), shape_of((ALL, D), f32)))
    return pl.pallas_call(
        lambda *refs: attn_bwd_kernel(last, *refs),
        grid=(2,),
        in_specs=x_specs
        + [whole_spec((ROWS, D))]
        + attn_specs
        + [slab_spec((ALL, 640)), slab_spec((6, BLOCK, KEYS)), slab_spec((ROWS, 256))]
        + ([whole_spec((ALL, D))] if last else []),
        out_specs=[o[0] for o in outs],
        out_shape=[o[1] for o in outs],
        scratch_shapes=([pltpu.VMEM((ALL, D), f32)] if last else [])
        + [pltpu.VMEM((ALL, D), bf16), pltpu.VMEM((D, D), bf16), pltpu.VMEM((ALL, 640), f32)],
        name="attn_bwd_b" if last else "attn_bwd_a",
    )(x, *fars, rl, *halves, r, p, a, *rest)


def ff_kernel(last, *refs):
    nf, go = refs[:2]
    halves = refs[2:6]
    refs = refs[6:]
    if last:
        out_a, ng_a, res, gains, order = refs[:5]
        down, doth, output, res_grad, rl, gain_grad, out_acc, ng_acc, w_s = refs[5:]
    else:
        down, doth, out_acc, ng_acc, w_s = refs
    step = pl.program_id(0)
    join(w_s, halves, step)
    gate = dot(nf[...], w_s[:, 0:FFS])
    up = dot(nf[...], w_s[:, FFS : 2 * FFS])
    hg = dot(go[...], w_s[:, 2 * FFS : 3 * FFS])
    root = 0.7978845608028654
    t = jnp.tanh(root * (gate + 0.044715 * gate * gate * gate))
    cdf = 0.5 * (1.0 + t)
    act = gate * cdf
    slope = cdf + 0.5 * gate * (1.0 - t * t) * (root * (1.0 + 3.0 * 0.044715 * gate * gate))
    hidden = (act * up).astype(bf16)
    both = jnp.concatenate([(hg * up * slope).astype(bf16), (hg * act).astype(bf16)], axis=1)
    out = dot_nt(hidden, w_s[:, 2 * FFS : 3 * FFS])
    ng = dot_nt(both, w_s[:, 0 : 2 * FFS])

    @pl.when(step == 0)
    def _():
        out_acc[...] = out_a[...] + out if last else out
        ng_acc[...] = ng_a[...] + ng if last else ng

    @pl.when(step > 0)
    def _():
        out_acc[...] += out
        ng_acc[...] += ng

    for ref, base in ((down, 0), (doth, HALF)):
        ref[0, :, 0 : 2 * FFS] = dot_tn(nf[:, base : base + HALF], both).astype(bf16)
        ref[0, :, 2 * FFS : 3 * FFS] = dot_tn(go[:, base : base + HALF], hidden).astype(bf16)
    if last:

        @pl.when(step == pl.num_programs(0) - 1)
        def _():
            v = res[...]
            r = rsqrt_mean(v)
            e = ng_acc[...]
            output[...] = dot_nt((v + out_acc[...]).astype(bf16), order[...]).astype(bf16)
            total = go[...].astype(f32) + row_term(v, r, gains[1:2], e)
            res_grad[...] = total
            rl[...] = total.astype(bf16)
            gain_grad[...] = jnp.sum(e * v * r, axis=0, keepdims=True)


def ff_both(nf, go, halves, *rest):
    last = len(rest) > 0
    wide = (whole_spec((ROWS, D)), shape_of((ROWS, D), f32))
    narrow = (whole_spec((ROWS, D)), shape_of((ROWS, D), bf16))
    outs = [(slab_spec((HALF, 3 * FFS)), shape_of((2, HALF, 3 * FFS), bf16))] * 2
    if last:
        outs = outs + [narrow, wide, narrow, (whole_spec((1, D)), shape_of((1, D), f32))]
    else:
        outs = outs + [wide, wide]
    return pl.pallas_call(
        lambda *refs: ff_kernel(last, *refs),
        grid=(2,),
        in_specs=[whole_spec((ROWS, D))] * 2
        + ff_specs
        + ([whole_spec((ROWS, D))] * 3 + [whole_spec((8, D)), whole_spec((D, D))] if last else []),
        out_specs=[o[0] for o in outs],
        out_shape=[o[1] for o in outs],
        scratch_shapes=([pltpu.VMEM((ROWS, D), f32)] * 2 if last else []) + [pltpu.VMEM((D, 3 * FFS), bf16)],
        name="ff_b" if last else "ff_a",
    )(nf, go, *halves, *rest)


def post_kernel(own, lo, hi, f0, f1, f2, f3, res_grad, tok, pooled, mem, gains, order, grad, gain_grad):
    e = f0[...] + f1[...].astype(f32) + f2[...].astype(f32) + f3[...].astype(f32)
    v = pooled[...]
    r = rsqrt_mean(v)
    spread = row_term(v, r, gains[2:3], e)
    gain_grad[1:2] = jnp.sum(e * v * r, axis=0, keepdims=True)
    wide = own[...] + jnp.concatenate([lo[...], hi[...]], axis=0).astype(f32)
    for _ in range(3):
        part = spread.astype(bf16)
        wide = wide + dot_tn(mem[...], part)
        spread = spread - part.astype(f32)
    v = tok[...].astype(f32)
    r = rsqrt_mean(v)
    gain_grad[0:1] = jnp.sum(wide * v * r, axis=0, keepdims=True)
    rest = res_grad[...] + row_term(v, r, gains[0:1], wide)
    total = jnp.zeros((ROWS, D), f32)
    for _ in range(3):
        part = rest.astype(bf16)
        total = total + dot_nt(part, order[...])
        rest = rest - part.astype(f32)
    grad[...] = total


def post(*args):
    return pl.pallas_call(
        post_kernel, out_shape=[shape_of((ROWS, D), f32), shape_of((2, D), f32)], name="post"
    )(*args)


def swap(x, axis, mask):
    size = lax.axis_size(axis)
    return lax.ppermute(x, axis, [(i, i ^ mask) for i in range(size)])


def high_bits():
    return list(range(3, lax.axis_size("fsdp").bit_length() - 1))


def gather_own(slab, bits):
    first, second = bits
    one = swap(slab, "fsdp", 1 << first)
    two = swap(slab, "fsdp", 1 << second)
    both = swap(one, "fsdp", 1 << second)
    middle = [one, two] if first == 1 else [two, one]
    return jnp.concatenate([slab] + middle + [both])


def gather_high(shard):
    for bit in high_bits():
        shard = jnp.concatenate([shard, swap(shard, "fsdp", 1 << bit)], axis=0)
    return shard


def gather_tensor(x):
    got = []
    for k in (1, 2, 3):
        got.append(swap(x, "tensor", k))
    return got


def scatter_pair(own, oth, bits):
    first, second = bits
    came = swap(oth, "fsdp", 1)

    def piece(n):
        rows = slice(n * 96, n * 96 + 96)
        return own[:, rows].astype(f32) + came[:, rows].astype(f32)

    at = {1: 1, 2: 2}
    send = jnp.concatenate([piece(at[first]), piece(3)], axis=1).astype(own.dtype)
    got = swap(send, "fsdp", 1 << first)
    send = (piece(at[second]) + got[:, 96:].astype(f32)).astype(own.dtype)
    more = swap(send, "fsdp", 1 << second)
    total = (piece(0) + got[:, :96].astype(f32) + more.astype(f32)).astype(own.dtype)
    for bit in high_bits()[::-1]:
        half = total.shape[1] // 2
        total = total[:, :half] + swap(total[:, half:], "fsdp", 1 << bit)
    return total


def scatter_tensor(slabs):
    total = slabs[0].astype(f32)
    for k in (1, 2, 3):
        got = swap(slabs[k], "tensor", k)
        total = total + got.astype(f32)
    return total


def inner(
    tokens, ln_attn, ln_ff, ln_global, w_query, w_key, w_value, w_out, wi_gate, wi_up, wo_ff,
    table_local, table_global, local_onehot, global_onehot, segment, grad_out,
):
    count = lax.axis_size("fsdp")
    width = D // count
    f = lax.axis_index("fsdp")
    z = lax.axis_index("tensor")
    last = lax.axis_size("tensor") - 1
    up_one = [(i, i + 1) for i in range(last)]
    down_one = [(i + 1, i) for i in range(last)]

    gains = jnp.stack([ln_attn, ln_ff, ln_global])[:, None, :]
    for bit in high_bits() + [1, 2, 0]:
        gains = jnp.concatenate([gains, swap(gains, "fsdp", 1 << bit)], axis=1)
    gains = jnp.pad(gains.reshape(3, D).astype(f32), ((0, 5), (0, 0)))
    left = lax.ppermute(tokens[ROWS - BLOCK :], "tensor", up_one)
    right = lax.ppermute(tokens[:BLOCK], "tensor", down_one)

    shard = gather_high(pack(w_query, w_key, w_value, w_out, wi_gate, wi_up, wo_ff.T))
    slabs = [shard] + gather_tensor(shard)
    tables = jnp.concatenate([table_local.T.reshape(1, -1), table_global.T.reshape(1, -1)], axis=1)
    tables = jnp.pad(tables, ((0, 0), (0, D - tables.shape[1])))

    true_at = jnp.arange(D, dtype=jnp.int32)
    piece = true_at // 96
    high = (true_at % 96) // width
    relative = (piece // 4) | ((piece & 3) << 1) | (high << 3)
    source = (f ^ relative) * width + true_at % width
    order = (true_at[:, None] == source[None, :]).astype(bf16)

    seg_row = segment[0]
    parts = seg_row.reshape(4, ROWS)
    rel = jnp.arange(4, dtype=jnp.int32) ^ z
    seg_rel = jnp.take(parts, rel, axis=0)
    here = jnp.arange(ROWS, dtype=jnp.int32)
    starts = (here % GBLOCK == 0)[None] | (
        seg_rel != jnp.concatenate([seg_rel[:, :1], seg_rel[:, :-1]], axis=1)
    )
    triangle = (here[:, None] <= here[None, :]).astype(bf16)
    piece_rel = dot(starts.astype(bf16), triangle).astype(jnp.int32) - 1
    is_in = piece_rel[:, None, :] == jnp.arange(FAR, dtype=jnp.int32)[:, None]
    slot_rel = rel[:, None] * (ROWS // GBLOCK) + here[None] // GBLOCK
    piece_doc = jnp.max(jnp.where(is_in, seg_rel[:, None, :], -1), axis=2).reshape(4 * FAR)
    piece_slot = jnp.max(jnp.where(is_in, slot_rel[:, None, :], -1), axis=2).reshape(4 * FAR)
    member = is_in[0].astype(bf16)

    x, tok, go, pooled, far_rows = prep(left, tokens, right, grad_out, order, gains, member, tables)
    fars = [far_rows] + gather_tensor(far_rows)

    tables = jnp.stack([far[FAR - 1, : 6 * BUCKETS] for far in fars])
    tables = tables.reshape(4, 2, 3, BUCKETS).transpose(1, 0, 2, 3).reshape(2 * HEADS, BUCKETS).astype(f32)

    padded = jnp.concatenate([jnp.full((BLOCK,), -1, jnp.int32), seg_row, jnp.full((BLOCK,), -1, jnp.int32)])
    seg_ext = lax.dynamic_slice(padded, (z * ROWS,), (EXT,))
    seg_own = seg_ext[BLOCK : BLOCK + ROWS].reshape(2, BLOCK)
    seg_keys = jnp.stack([seg_ext[: 3 * BLOCK], seg_ext[BLOCK:]])
    offset = jnp.arange(3 * BLOCK, dtype=jnp.int32)[None] - BLOCK - jnp.arange(BLOCK, dtype=jnp.int32)[:, None]
    near_ok = (jnp.abs(offset) < BLOCK)[None] & (seg_own[:, :, None] == seg_keys[:, None, :])
    far_ok = seg_own[:, :, None] == piece_doc[None, None, :]
    mask = jnp.where(jnp.concatenate([near_ok, far_ok], axis=2), 0.0, masked_score).astype(f32)
    bucket = jnp.arange(BUCKETS, dtype=jnp.int32)
    near_at = jnp.sum(local_onehot[0] * bucket, axis=1)[None]
    own_hot = lax.dynamic_slice(global_onehot, (z * 16, 0, 0), (16, SLOTS, BUCKETS))
    slot_at = jnp.sum(own_hot * bucket, axis=2)
    slot_is = piece_slot[None, :] == jnp.arange(SLOTS, dtype=jnp.int32)[:, None]
    far_at = dot(slot_at.astype(bf16), slot_is.astype(bf16)).astype(jnp.int32)

    small_work = (mask, near_at, far_at, tables)
    pairs = []
    for n, slab in enumerate(slabs):
        own_half = gather_own(slab, ((1, 2), (2, 1))[n % 2])
        if n == 1:
            own_half, (mask, near_at, far_at, tables) = lax.optimization_barrier(
                (own_half, small_work)
            )
        pairs.append([own_half, swap(own_half, "fsdp", 1)])
    pair_a = pairs[0] + pairs[1]
    pair_b = pairs[2] + pairs[3]

    acc, p_a, r_a, at_a = attn_fwd(0, x, fars, pair_a, near_at, far_at, tables, mask)
    residual, nf, p_b, r_b, at_b = attn_fwd(
        2, x, fars, pair_b, near_at, far_at, tables, mask, acc, tok, gains
    )
    fo_a, ft_a, out_a, ng_a = ff_both(nf, go, pair_a)
    fo_b, ft_b, output, res_grad, rl, gain_ff_grad = ff_both(
        nf, go, pair_b, out_a, ng_a, residual, gains, order
    )
    sum_fa = scatter_pair(fo_a, ft_a, (1, 2))
    sum_fb = scatter_pair(fo_b, ft_b, (2, 1))
    do_a, dt_a, nb_a, fb_a, xg = attn_bwd(x, fars, rl, pair_a, r_a, p_a, at_a)
    do_b, dt_b, nb_b, fb_b, own, lo, hi, f0, s1, s2, s3 = attn_bwd(
        x, fars, rl, pair_b, r_b, p_b, at_b, xg
    )
    sum_aa = scatter_pair(do_a, dt_a, (1, 2))
    sum_ab = scatter_pair(do_b, dt_b, (2, 1))
    to_left = lax.ppermute(lo, "tensor", down_one)
    to_right = lax.ppermute(hi, "tensor", up_one)
    f1, f2, f3 = [swap(s, "tensor", k) for s, k in ((s1, 1), (s2, 2), (s3, 3))]
    late = lax.optimization_barrier((nb_a, nb_b, fb_a, fb_b, f1, f2, f3))
    grad_tokens, gain_grads = post(
        own, to_right, to_left, f0, f1, f2, f3, res_grad, tok, pooled, member, gains, order
    )

    nb_a, nb_b, fb_a, fb_b, f1, f2, f3 = late
    near_table = jnp.dot(
        jnp.concatenate([nb_a, nb_b]).reshape(HEADS, 3 * BLOCK), local_onehot[0].astype(f32), precision=highest
    )
    far_hot = (far_at.reshape(-1)[:, None] == bucket).astype(f32)
    far_table = jnp.dot(
        jnp.concatenate([fb_a, fb_b]).reshape(HEADS, 16 * 128), far_hot, precision=highest
    )
    table_part = jnp.concatenate(
        [near_table.reshape(4, 3 * BUCKETS), far_table.reshape(4, 3 * BUCKETS)], axis=1
    )
    gain_part = jnp.stack([gain_grads[0], gain_ff_grad[0], gain_grads[1]])
    gain_part = gain_part.reshape(3, count, width).transpose(1, 0, 2).reshape(count, 3 * width)
    small = jnp.concatenate(
        [
            jnp.broadcast_to(gain_part[None], (4, count, 3 * width)),
            jnp.broadcast_to(table_part[:, None], (4, count, 6 * BUCKETS)),
        ],
        axis=2,
    )
    for bit in [0, 2, 1] + high_bits()[::-1]:
        half = small.shape[1] // 2
        small = small[:, :half] + swap(small[:, half:], "fsdp", 1 << bit)
    small = scatter_tensor(small)[0]
    gain_sum = small[: 3 * width].reshape(3, width)
    table_sum = small[3 * width :].reshape(2, 3, BUCKETS).transpose(0, 2, 1)

    ff_sum = scatter_tensor([sum_fa[0], sum_fa[1], sum_fb[0], sum_fb[1]])
    at_sum = scatter_tensor([sum_aa[0], sum_aa[1], sum_ab[0], sum_ab[1]])
    col = lambda n: at_sum[:, n * 64 : n * 64 + 64]
    grad_query = jnp.concatenate([at_sum[:, 0:128], col(6)], axis=1)
    grad_key = jnp.concatenate([at_sum[:, 128:256], col(8)], axis=1)
    grad_value = jnp.concatenate([at_sum[:, 256:384], col(7)], axis=1)
    grad_out_w = jnp.concatenate([at_sum[:, 640:768], col(9)], axis=1).T
    return (
        output,
        grad_tokens,
        gain_sum[0],
        gain_sum[1],
        gain_sum[2],
        grad_query,
        grad_key,
        grad_value,
        grad_out_w,
        ff_sum[:, 0:FFS],
        ff_sum[:, FFS : 2 * FFS],
        ff_sum[:, 2 * FFS : 3 * FFS].T,
        table_sum[0],
        table_sum[1],
    )


def solution(mesh):
    return jax.shard_map(
        inner,
        mesh=mesh,
        in_specs=(
            P(("fsdp", "tensor"), None),
            P("fsdp"),
            P("fsdp"),
            P("fsdp"),
            P("fsdp", "tensor"),
            P("fsdp", "tensor"),
            P("fsdp", "tensor"),
            P("tensor", "fsdp"),
            P("fsdp", "tensor"),
            P("fsdp", "tensor"),
            P("tensor", "fsdp"),
            P(None, "tensor"),
            P(None, "tensor"),
            P(),
            P(),
            P("fsdp", None),
            P(("fsdp", "tensor"), None),
        ),
        out_specs=(
            P(("fsdp", "tensor"), None),
            P(("fsdp", "tensor"), None),
            P("fsdp"),
            P("fsdp"),
            P("fsdp"),
            P("fsdp", "tensor"),
            P("fsdp", "tensor"),
            P("fsdp", "tensor"),
            P("tensor", "fsdp"),
            P("fsdp", "tensor"),
            P("fsdp", "tensor"),
            P("tensor", "fsdp"),
            P(None, "tensor"),
            P(None, "tensor"),
        ),
        check_vma=False,
    )
```

profile of v0, /device:TPU:0, one launch (start us, length us, event | category | flops | bytes accessed | tf_op | source)
XLA Modules:
  0.0 336.7 jit_solution(13696265214974648843)
XLA Ops:
  2.8 3.1 collective-permute-start.18
  7.3 2.6 collective-permute-start.8
  12.3 2.4 collective-permute-start
  29.2 6.0 %collective-permute-done.1.right = bf16[128,768]{1,0:T(8,128)(2,1)S(1)} collective-permute-done((bf16[128,768]{1,0:T(8,128)(2,1)S(1)}, bf16[128,768]{1,0:T(8,128)(2,1)S(1)}, u32[]{:S(2)}, u32[]{:S(2)}) %collective-permute-start.1) | collective-permute-done | bytes 196640 | tf_op jit(solution)/shard_map/ppermute | solution.py:551
  35.9 3.8 %prep.1 = (bf16[512,768]{1,0:T(8,128)(2,1)}, bf16[256,768]{1,0:T(8,128)(2,1)}, bf16[256,768]{1,0:T(8,128)(2,1)}, f32[32,768]{1,0:T(8,128)}, bf16[32,768]{1,0:T(8,128)(2,1)}) custom-call(bf16[128,768]{1,0:T(8,128)(2,1)} %copy-done.15, bf16[256,768]{1,0:T(8,128)(2,1)} %tok.1, bf16[128,768]{1,0:T(8,128)(2,1)} %copy-done.16, bf16[256,768]{1,0:T(8,128)(2,1)} %grad.1, ...), custom_call_target="tpu_custom_call" | custom-call | tf_op jit(solution)/shard_map/prep/pallas_call | solution.py:107
  41.2 3.4 %collective-permute-done.5.refs_2_ = bf16[32,768]{1,0:T(8,128)(2,1)S(1)} collective-permute-done((bf16[32,768]{1,0:T(8,128)(2,1)}, bf16[32,768]{1,0:T(8,128)(2,1)S(1)}, u32[]{:S(2)}, u32[]{:S(2)}) %collective-permute-start.5) | collective-permute-done | bytes 49184 | tf_op jit(solution)/shard_map/ppermute | solution.py:477
  57.3 4.4 %collective-permute-done.13 = bf16[96,2304]{1,0:T(8,128)(2,1)S(1)} collective-permute-done((bf16[96,2304]{1,0:T(8,128)(2,1)S(1)}, bf16[96,2304]{1,0:T(8,128)(2,1)S(1)}, u32[]{:S(2)}, u32[]{:S(2)}) %collective-permute-start.13) | collective-permute-done | bytes 442400 | tf_op jit(solution)/shard_map/ppermute | solution.py:477
  65.5 13.7 %collective-permute-done.24 = bf16[96,2304]{1,0:T(8,128)(2,1)S(1)} collective-permute-done((bf16[96,2304]{1,0:T(8,128)(2,1)S(1)}, bf16[96,2304]{1,0:T(8,128)(2,1)S(1)}, u32[]{:S(2)}, u32[]{:S(2)}) %collective-permute-start.24) | collective-permute-done | bytes 442400 | tf_op jit(solution)/shard_map/ppermute | solution.py:477
  83.3 4.2 %collective-permute-done.14 = bf16[96,2304]{1,0:T(8,128)(2,1)S(1)} collective-permute-done((bf16[96,2304]{1,0:T(8,128)(2,1)S(1)}, bf16[96,2304]{1,0:T(8,128)(2,1)S(1)}, u32[]{:S(2)}, u32[]{:S(2)}) %collective-permute-start.14) | collective-permute-done | bytes 442400 | tf_op jit(solution)/shard_map/ppermute | solution.py:477
  89.8 8.3 %collective-permute-done.15 = bf16[96,2304]{1,0:T(8,128)(2,1)S(1)} collective-permute-done((bf16[96,2304]{1,0:T(8,128)(2,1)S(1)}, bf16[96,2304]{1,0:T(8,128)(2,1)S(1)}, u32[]{:S(2)}, u32[]{:S(2)}) %collective-permute-start.15) | collective-permute-done | bytes 442400 | tf_op jit(solution)/shard_map/ppermute | solution.py:477
  101.8 8.3 %collective-permute-done.21 = bf16[96,2304]{1,0:T(8,128)(2,1)S(1)} collective-permute-done((bf16[96,2304]{1,0:T(8,128)(2,1)S(1)}, bf16[96,2304]{1,0:T(8,128)(2,1)S(1)}, u32[]{:S(2)}, u32[]{:S(2)}) %collective-permute-start.21) | collective-permute-done | bytes 442400 | tf_op jit(solution)/shard_map/ppermute | solution.py:477
  111.6 3.2 collective-permute-done.16
  118.2 12.1 %attn_fwd_a.1 = (f32[256,768]{1,0:T(8,128)}, bf16[2,6,128,512]{3,2,1,0:T(8,128)(2,1)}, bf16[2,640,640]{2,1,0:T(8,128)(2,1)}, bf16[2,256,256]{2,1,0:T(8,128)(2,1)}) custom-call(bf16[512,768]{1,0:T(8,128)(2,1)} %get-tuple-element.65.refs_0_, bf16[32,768]{1,0:T(8,128)(2,1)} %get-tuple-element.66.refs_1_, bf16[32,768]{1,0:T(8,128)(2,1)} %copy-done.12, ...), custom_call_target="tpu_custom_call" | custom-call | tf_op jit(solution)/shard_map/attn_fwd_a/pallas_call | solution.py:236
  130.3 12.6 %attn_fwd_b.1 = (f32[256,768]{1,0:T(8,128)}, bf16[256,768]{1,0:T(8,128)(2,1)}, bf16[2,6,128,512]{3,2,1,0:T(8,128)(2,1)}, bf16[2,640,640]{2,1,0:T(8,128)(2,1)}, bf16[2,256,256]{2,1,0:T(8,128)(2,1)}) custom-call(bf16[512,768]{1,0:T(8,128)(2,1)} %get-tuple-element.65.refs_0_, bf16[32,768]{1,0:T(8,128)(2,1)} %get-tuple-element.66.refs_1_, ...), custom_call_target="tpu_custom_call" | custom-call | tf_op jit(solution)/shard_map/attn_fwd_b/pallas_call | solution.py:236
  142.9 9.3 %ff_a.1 = (bf16[2,384,1536]{2,1,0:T(8,128)(2,1)}, bf16[2,384,1536]{2,1,0:T(8,128)(2,1)}, f32[256,768]{1,0:T(8,128)}, f32[256,768]{1,0:T(8,128)}) custom-call(bf16[256,768]{1,0:T(8,128)(2,1)} %get-tuple-element.74.refs_0_, bf16[256,768]{1,0:T(8,128)(2,1)} %get-tuple-element.75.refs_1_, bf16[384,2304]{1,0:T(8,128)(2,1)} %copy-done, ...), custom_call_target="tpu_custom_call" | custom-call | tf_op jit(solution)/shard_map/ff_a/pallas_call | solution.py:433
  152.1 12.5 %ff_b.1 = (bf16[2,384,1536]{2,1,0:T(8,128)(2,1)}, bf16[2,384,1536]{2,1,0:T(8,128)(2,1)}, bf16[256,768]{1,0:T(8,128)(2,1)}, f32[256,768]{1,0:T(8,128)}, bf16[256,768]{1,0:T(8,128)(2,1)}, /*index=5*/f32[1,768]{1,0:T(1,128)}) custom-call(bf16[256,768]{1,0:T(8,128)(2,1)} %get-tuple-element.74.refs_0_, bf16[256,768]{1,0:T(8,128)(2,1)} %get-tuple-element.75.refs_1_, ...), custom_call_target="tpu_custom_call" | custom-call | tf_op jit(solution)/shard_map/ff_b/pallas_call | solution.py:433
  164.6 15.8 %attn_bwd_a.1 = (bf16[2,384,768]{2,1,0:T(8,128)(2,1)}, bf16[2,384,768]{2,1,0:T(8,128)(2,1)}, f32[2,3,384]{2,1,0:T(4,128)}, f32[2,3,16,128]{3,2,1,0:T(8,128)}, f32[640,768]{1,0:T(8,128)}) custom-call(bf16[512,768]{1,0:T(8,128)(2,1)} %get-tuple-element.65.refs_0_, bf16[32,768]{1,0:T(8,128)(2,1)} %get-tuple-element.66.refs_1_, bf16[32,768]{1,0:T(8,128)(2,1)} %copy-done.12, ...), custom_call_target="tpu_custom_call" | custom-call | tf_op jit(solution)/shard_map/attn_bwd_a/pallas_call | solution.py:357
  180.5 17.2 %attn_bwd_b.1 = (bf16[2,384,768]{2,1,0:T(8,128)(2,1)}, bf16[2,384,768]{2,1,0:T(8,128)(2,1)}, f32[2,3,384]{2,1,0:T(4,128)}, f32[2,3,16,128]{3,2,1,0:T(8,128)}, f3...) custom-call(bf16[512,768]{1,0:T(8,128)(2,1)} %get-tuple-element.65.r, ...), custom_call_target="tpu_custom_call" | custom-call | tf_op jit(solution)/shard_map/attn_bwd_b/pallas_call | solution.py:357
  199.4 2.7 collective-permute-start.31
  209.1 2.9 collective-permute-done.28.hi
  212.7 5.5 %post.1 = (f32[256,768]{1,0:T(8,128)}, f32[2,768]{1,0:T(2,128)}) custom-call(f32[256,768]{1,0:T(8,128)} %get-tuple-element.88.own, bf16[128,768]{1,0:T(8,128)(2,1)} %copy-done.23, bf16[128,768]{1,0:T(8,128)(2,1)} %copy-done.24, f32[32,768]{1,0:T(8,128)} %get-tuple-element.91.f0, bf16[32,768]{1,0:T(8,128)(2,1)} %copy-done.26, bf16[32,768]{1,0:T(8,128)(2,1)} %copy-done.27, ...), custom_call_target="tpu_custom_call" | custom-call | tf_op jit(solution)/shard_map/post/pallas_call | solution.py:470
  222.1 2.2 collective-permute-done.33
  225.9 2.2 collective-permute-done.34
  230.3 2.3 collective-permute-start.37
  242.2 8.7 %collective-permute-done.39 = bf16[2,192,768]{2,1,0:T(8,128)(2,1)S(1)} collective-permute-done((bf16[2,192,768]{2,1,0:T(8,128)(2,1)S(1)}, bf16[2,192,768]{2,1,0:T(8,128)(2,1)S(1)}, u32[]{:S(2)}, u32[]{:S(2)}) %collective-permute-start.39) | collective-permute-done | bytes 589856 | tf_op jit(solution)/shard_map/ppermute | solution.py:477
  256.8 2.9 collective-permute-done.40
  273.1 2.4 collective-permute-done.45
  276.9 16.8 %collective-permute-done.48 = bf16[2,192,1536]{2,1,0:T(8,128)(2,1)S(1)} collective-permute-done((bf16[2,192,1536]{2,1,0:T(8,128)(2,1)S(1)}, bf16[2,192,1536]{2,1,0:T(8,128)(2,1)S(1)}, u32[]{:S(2)}, u32[]{:S(2)}) %collective-permute-start.48) | collective-permute-done | bytes 1179680 | tf_op jit(solution)/shard_map/ppermute | solution.py:477
  293.7 2.5 add_convert_fusion.5
  302.1 7.5 %collective-permute-done.49 = bf16[2,96,1536]{2,1,0:T(8,128)(2,1)} collective-permute-done((bf16[2,96,1536]{2,1,0:T(8,128)(2,1)}, bf16[2,96,1536]{2,1,0:T(8,128)(2,1)}, u32[]{:S(2)}, u32[]{:S(2)}) %collective-permute-start.49) | collective-permute-done | bytes 589856 | tf_op jit(solution)/shard_map/ppermute | solution.py:477
  319.5 2.5 collective-permute-done.50
  321.9 13.5 %collective-permute-done.54 = bf16[96,1536]{1,0:T(8,128)(2,1)S(1)} collective-permute-done((bf16[96,1536]{1,0:T(8,128)(2,1)S(1)}, bf16[96,1536]{1,0:T(8,128)(2,1)S(1)}, u32[]{:S(2)}, u32[]{:S(2)}) %collective-permute-start.54) | collective-permute-done | bytes 294944 | tf_op jit(solution)/shard_map/ppermute | solution.py:477
  (283 shorter events, 117.6 us)
Async XLA Ops:
  2.8 50.1 %collective-permute-start.18 = (bf16[96,2304]{1,0:T(8,128)(2,1)}, bf16[96,2304]{1,0:T(8,128)(2,1)S(1)}, u32[]{:S(2)}, u32[]{:S(2)}) collective-permute-start(bf16[96,2304]{1,0:T(8,128)(2,1)} %pack.1), channel_id=1, source_target_pairs={{0,1},{1,0},{2,3},{3,2},{4,5},{5,4},{6,7},{7,6},{8,9},{9,8},{10,11... | collective-permute-start | bytes 1327112 | tf_op jit(solution)/shard_map/ppermute | solution.py:477
  5.8 47.6 %collective-permute-start.22 = (bf16[96,2304]{1,0:T(8,128)(2,1)}, bf16[96,2304]{1,0:T(8,128)(2,1)S(1)}, u32[]{:S(2)}, u32[]{:S(2)}) collective-permute-start(bf16[96,2304]{1,0:T(8,128)(2,1)} %pack.1), channel_id=1, source_target_pairs={{0,8},{4,12},{8,0},{12,4},{16,24},{20,28},{24,16},{28,20},{1,9},{5... | collective-permute-start | bytes 1327112 | tf_op jit(solution)/shard_map/ppermute | solution.py:477
  7.3 47.6 %collective-permute-start.8 = (bf16[96,2304]{1,0:T(8,128)(2,1)}, bf16[96,2304]{1,0:T(8,128)(2,1)S(1)}, u32[]{:S(2)}, u32[]{:S(2)}) collective-permute-start(bf16[96,2304]{1,0:T(8,128)(2,1)} %pack.1), channel_id=1, source_target_pairs={{0,2},{1,3},{2,0},{3,1},{4,6},{5,7},{6,4},{7,5},{8,10},{9,11},{10,... | collective-permute-start | bytes 1327112 | tf_op jit(solution)/shard_map/ppermute | solution.py:477
  10.6 10.8 %collective-permute-start.2 = (bf16[3,1,96]{2,0,1:T(4,128)(2,1)S(1)}, bf16[3,1,96]{2,0,1:T(4,128)(2,1)S(1)}, u32[]{:S(2)}, u32[]{:S(2)}) collective-permute-start(bf16[3,1,96]{2,0,1:T(4,128)(2,1)S(1)} %maximum_bitcast_fusion.1), channel_id=1, source_target_pairs={{0,8},{4,12},{8,0},{12,4},{16,24},{20,28},{24,16},{28,20},{1,9},{5... | collective-permute-start | bytes 1736 | tf_op jit(solution)/shard_map/ppermute | solution.py:477
  12.3 17.0 %collective-permute-start = (bf16[128,768]{1,0:T(8,128)(2,1)S(1)}, bf16[128,768]{1,0:T(8,128)(2,1)S(1)}, u32[]{:S(2)}, u32[]{:S(2)}) collective-permute-start(bf16[128,768]{1,0:T(8,128)(2,1)S(1)} %get-tuple-element.160), channel_id=1, source_target_pairs={{0,1},{1,2},{2,3},{4,5},{5,6},{6,7},{8,9},{9,10},{10,11},{12,13},{... | collective-permute-start | bytes 589832 | tf_op jit(solution)/shard_map/ppermute | solution.py:550
  47.1 16.8 %collective-permute-start.23 = (bf16[96,2304]{1,0:T(8,128)(2,1)S(1)}, bf16[96,2304]{1,0:T(8,128)(2,1)S(1)}, u32[]{:S(2)}, u32[]{:S(2)}) collective-permute-start(bf16[96,2304]{1,0:T(8,128)(2,1)S(1)} %copy-done.7), channel_id=1, source_target_pairs={{0,16},{4,20},{8,24},{12,28},{16,0},{20,4},{24,8},{28,12},{1,17},{... | collective-permute-start | bytes 1327112 | tf_op jit(solution)/shard_map/ppermute | solution.py:477
  52.9 35.4 %collective-permute-start.20 = (bf16[96,2304]{1,0:T(8,128)(2,1)S(1)}, bf16[96,2304]{1,0:T(8,128)(2,1)S(1)}, u32[]{:S(2)}, u32[]{:S(2)}) collective-permute-start(bf16[96,2304]{1,0:T(8,128)(2,1)S(1)} %collective-permute-done.18), channel_id=1, source_target_pairs={{0,16},{4,20},{8,24},{12,28},{16,0},{20,4},{24,8},{28,12},{1,17},{... | collective-permute-start | bytes 1327112 | tf_op jit(solution)/shard_map/ppermute | solution.py:477
  53.5 48.3 %collective-permute-start.19 = (bf16[96,2304]{1,0:T(8,128)(2,1)S(1)}, bf16[96,2304]{1,0:T(8,128)(2,1)S(1)}, u32[]{:S(2)}, u32[]{:S(2)}) collective-permute-start(bf16[96,2304]{1,0:T(8,128)(2,1)S(1)} %collective-permute-done.18), channel_id=1, source_target_pairs={{0,8},{4,12},{8,0},{12,4},{16,24},{20,28},{24,16},{28,20},{1,9},{5... | collective-permute-start | bytes 1327112 | tf_op jit(solution)/shard_map/ppermute | solution.py:477
  55.0 24.2 %collective-permute-start.24 = (bf16[96,2304]{1,0:T(8,128)(2,1)S(1)}, bf16[96,2304]{1,0:T(8,128)(2,1)S(1)}, u32[]{:S(2)}, u32[]{:S(2)}) collective-permute-start(bf16[96,2304]{1,0:T(8,128)(2,1)S(1)} %collective-permute-done.22), channel_id=1, source_target_pairs={{0,16},{4,20},{8,24},{12,28},{16,0},{20,4},{24,8},{28,12},{1,17},{... | collective-permute-start | bytes 1327112 | tf_op jit(solution)/shard_map/ppermute | solution.py:477
  61.6 19.2 %collective-permute-start.9 = (bf16[96,2304]{1,0:T(8,128)(2,1)S(1)}, bf16[96,2304]{1,0:T(8,128)(2,1)S(1)}, u32[]{:S(2)}, u32[]{:S(2)}) collective-permute-start(bf16[96,2304]{1,0:T(8,128)(2,1)S(1)} %collective-permute-done.8), channel_id=1, source_target_pairs={{0,8},{4,12},{8,0},{12,4},{16,24},{20,28},{24,16},{28,20},{1,9},{5... | collective-permute-start | bytes 1327112 | tf_op jit(solution)/shard_map/ppermute | solution.py:477
  63.9 36.5 %collective-permute-start.10 = (bf16[96,2304]{1,0:T(8,128)(2,1)S(1)}, bf16[96,2304]{1,0:T(8,128)(2,1)S(1)}, u32[]{:S(2)}, u32[]{:S(2)}) collective-permute-start(bf16[96,2304]{1,0:T(8,128)(2,1)S(1)} %collective-permute-done.8), channel_id=1, source_target_pairs={{0,16},{4,20},{8,24},{12,28},{16,0},{20,4},{24,8},{28,12},{1,17},{... | collective-permute-start | bytes 1327112 | tf_op jit(solution)/shard_map/ppermute | solution.py:477
  80.9 17.3 %collective-permute-start.15 = (bf16[96,2304]{1,0:T(8,128)(2,1)S(1)}, bf16[96,2304]{1,0:T(8,128)(2,1)S(1)}, u32[]{:S(2)}, u32[]{:S(2)}) collective-permute-start(bf16[96,2304]{1,0:T(8,128)(2,1)S(1)} %collective-permute-done.13), channel_id=1, source_target_pairs={{0,16},{4,20},{8,24},{12,28},{16,0},{20,4},{24,8},{28,12},{1,17},{... | collective-permute-start | bytes 1327112 | tf_op jit(solution)/shard_map/ppermute | solution.py:477
  87.5 28.2 %collective-permute-start.25 = (bf16[384,2304]{1,0:T(8,128)(2,1)S(1)}, bf16[384,2304]{1,0:T(8,128)(2,1)S(1)}, u32[]{:S(2)}, u32[]{:S(2)}) collective-permute-start(bf16[384,2304]{1,0:T(8,128)(2,1)S(1)} %pad_maximum_fusion.1.refs_5_.refs_2_.refs_6_), channel_id=1, source_target_pairs={{0,4},{4,0},{8,12},{12,8},{16,20},{20,16},{24,28},{28,24},{1,5},{5... | collective-permute-start | bytes 5308424 | tf_op jit(solution)/shard_map/ppermute | solution.py:477
  88.3 22.0 %collective-permute-start.11 = (bf16[96,2304]{1,0:T(8,128)(2,1)S(1)}, bf16[96,2304]{1,0:T(8,128)(2,1)S(1)}, u32[]{:S(2)}, u32[]{:S(2)}) collective-permute-start(bf16[96,2304]{1,0:T(8,128)(2,1)S(1)} %collective-permute-done.9), channel_id=1, source_target_pairs={{0,16},{4,20},{8,24},{12,28},{16,0},{20,4},{24,8},{28,12},{1,17},{... | collective-permute-start | bytes 1327112 | tf_op jit(solution)/shard_map/ppermute | solution.py:477
  98.2 11.9 %collective-permute-start.21 = (bf16[96,2304]{1,0:T(8,128)(2,1)S(1)}, bf16[96,2304]{1,0:T(8,128)(2,1)S(1)}, u32[]{:S(2)}, u32[]{:S(2)}) collective-permute-start(bf16[96,2304]{1,0:T(8,128)(2,1)S(1)} %collective-permute-done.20), channel_id=1, source_target_pairs={{0,8},{4,12},{8,0},{12,4},{16,24},{20,28},{24,16},{28,20},{1,9},{5... | collective-permute-start | bytes 1327112 | tf_op jit(solution)/shard_map/ppermute | solution.py:477
  100.5 14.4 %collective-permute-start.16 = (bf16[96,2304]{1,0:T(8,128)(2,1)S(1)}, bf16[96,2304]{1,0:T(8,128)(2,1)S(1)}, u32[]{:S(2)}, u32[]{:S(2)}) collective-permute-start(bf16[96,2304]{1,0:T(8,128)(2,1)S(1)} %collective-permute-done.15), channel_id=1, source_target_pairs={{0,8},{4,12},{8,0},{12,4},{16,24},{20,28},{24,16},{28,20},{1,9},{5... | collective-permute-start | bytes 1327112 | tf_op jit(solution)/shard_map/ppermute | solution.py:477
  111.2 19.0 %collective-permute-start.12 = (bf16[384,2304]{1,0:T(8,128)(2,1)}, bf16[384,2304]{1,0:T(8,128)(2,1)}, u32[]{:S(2)}, u32[]{:S(2)}) collective-permute-start(bf16[384,2304]{1,0:T(8,128)(2,1)} %constant_dynamic-update-slice_fusion.refs_5_.refs_2_.refs_6_), channel_id=1, source_target_pairs={{0,4},{4,0},{8,12},{12,8},{16,20},{20,16},{24,28},{28,24},{1,5},{5... | collective-permute-start | bytes 5308424 | tf_op jit(solution)/shard_map/ppermute | solution.py:477
  115.7 14.6 %collective-permute-start.17 = (bf16[384,2304]{1,0:T(8,128)(2,1)}, bf16[384,2304]{1,0:T(8,128)(2,1)}, u32[]{:S(2)}, u32[]{:S(2)}) collective-permute-start(bf16[384,2304]{1,0:T(8,128)(2,1)} %constant_dynamic-update-slice_fusion.4.refs_7_.refs_4_.refs_8_), channel_id=1, source_target_pairs={{0,4},{4,0},{8,12},{12,8},{16,20},{20,16},{24,28},{28,24},{1,5},{5... | collective-permute-start | bytes 5308424 | tf_op jit(solution)/shard_map/ppermute | solution.py:477
  219.2 16.6 %collective-permute-start.38 = (bf16[2,384,768]{2,1,0:T(8,128)(2,1)}, bf16[2,384,768]{2,1,0:T(8,128)(2,1)}, u32[]{:S(2)}, u32[]{:S(2)}) collective-permute-start(bf16[2,384,768]{2,1,0:T(8,128)(2,1)} %get-tuple-element.109), channel_id=1, source_target_pairs={{0,4},{4,0},{8,12},{12,8},{16,20},{20,16},{24,28},{28,24},{1,5},{5... | collective-permute-start | bytes 3538952 | tf_op jit(solution)/shard_map/ppermute | solution.py:477
  222.1 16.7 %collective-permute-start.42 = (bf16[2,384,768]{2,1,0:T(8,128)(2,1)}, bf16[2,384,768]{2,1,0:T(8,128)(2,1)}, u32[]{:S(2)}, u32[]{:S(2)}) collective-permute-start(bf16[2,384,768]{2,1,0:T(8,128)(2,1)} %get-tuple-element.111), channel_id=1, source_target_pairs={{0,4},{4,0},{8,12},{12,8},{16,20},{20,16},{24,28},{28,24},{1,5},{5... | collective-permute-start | bytes 3538952 | tf_op jit(solution)/shard_map/ppermute | solution.py:477
  232.6 34.6 %collective-permute-start.47 = (bf16[2,384,1536]{2,1,0:T(8,128)(2,1)}, bf16[2,384,1536]{2,1,0:T(8,128)(2,1)S(1)}, u32[]{:S(2)}, u32[]{:S(2)}) collective-permute-start(bf16[2,384,1536]{2,1,0:T(8,128)(2,1)} %get-tuple-element.113), channel_id=1, source_target_pairs={{0,4},{4,0},{8,12},{12,8},{16,20},{20,16},{24,28},{28,24},{1,5},{5... | collective-permute-start | bytes 7077896 | tf_op jit(solution)/shard_map/ppermute | solution.py:477
  233.5 37.0 %collective-permute-start.51 = (bf16[2,384,1536]{2,1,0:T(8,128)(2,1)}, bf16[2,384,1536]{2,1,0:T(8,128)(2,1)}, u32[]{:S(2)}, u32[]{:S(2)}) collective-permute-start(bf16[2,384,1536]{2,1,0:T(8,128)(2,1)} %get-tuple-element.115), channel_id=1, source_target_pairs={{0,4},{4,0},{8,12},{12,8},{16,20},{20,16},{24,28},{28,24},{1,5},{5... | collective-permute-start | bytes 7077896 | tf_op jit(solution)/shard_map/ppermute | solution.py:477
  237.2 13.7 %collective-permute-start.39 = (bf16[2,192,768]{2,1,0:T(8,128)(2,1)S(1)}, bf16[2,192,768]{2,1,0:T(8,128)(2,1)S(1)}, u32[]{:S(2)}, u32[]{:S(2)}) collective-permute-start(bf16[2,192,768]{2,1,0:T(8,128)(2,1)S(1)} %pad_maximum_fusion.4), channel_id=1, source_target_pairs={{0,8},{4,12},{8,0},{12,4},{16,24},{20,28},{24,16},{28,20},{1,9},{5... | collective-permute-start | bytes 1769480 | tf_op jit(solution)/shard_map/ppermute | solution.py:477
  240.0 14.7 %collective-permute-start.43 = (bf16[2,192,768]{2,1,0:T(8,128)(2,1)S(1)}, bf16[2,192,768]{2,1,0:T(8,128)(2,1)S(1)}, u32[]{:S(2)}, u32[]{:S(2)}) collective-permute-start(bf16[2,192,768]{2,1,0:T(8,128)(2,1)S(1)} %pad_maximum_fusion.5), channel_id=1, source_target_pairs={{0,16},{4,20},{8,24},{12,28},{16,0},{20,4},{24,8},{28,12},{1,17},{... | collective-permute-start | bytes 1769480 | tf_op jit(solution)/shard_map/ppermute | solution.py:477
  260.9 12.2 %collective-permute-start.41 = (bf16[96,768]{1,0:T(8,128)(2,1)S(1)}, bf16[96,768]{1,0:T(8,128)(2,1)S(1)}, u32[]{:S(2)}, u32[]{:S(2)}) collective-permute-start(bf16[96,768]{1,0:T(8,128)(2,1)S(1)} %slice_bitcast_fusion.7), channel_id=1, source_target_pairs={{0,1},{1,0},{2,3},{3,2},{4,5},{5,4},{6,7},{7,6},{8,9},{9,8},{10,11... | collective-permute-start | bytes 442376 | tf_op jit(solution)/shard_map/ppermute | solution.py:477
  263.7 11.8 %collective-permute-start.45 = (bf16[96,768]{1,0:T(8,128)(2,1)S(1)}, bf16[96,768]{1,0:T(8,128)(2,1)S(1)}, u32[]{:S(2)}, u32[]{:S(2)}) collective-permute-start(bf16[96,768]{1,0:T(8,128)(2,1)S(1)} %get-tuple-element.169), channel_id=1, source_target_pairs={{0,2},{1,3},{2,0},{3,1},{4,6},{5,7},{6,4},{7,5},{8,10},{9,11},{10,... | collective-permute-start | bytes 442376 | tf_op jit(solution)/shard_map/ppermute | solution.py:477
  268.9 24.8 %collective-permute-start.48 = (bf16[2,192,1536]{2,1,0:T(8,128)(2,1)S(1)}, bf16[2,192,1536]{2,1,0:T(8,128)(2,1)S(1)}, u32[]{:S(2)}, u32[]{:S(2)}) collective-permute-start(bf16[2,192,1536]{2,1,0:T(8,128)(2,1)S(1)} %pad_maximum_fusion.2), channel_id=1, source_target_pairs={{0,8},{4,12},{8,0},{12,4},{16,24},{20,28},{24,16},{28,20},{1,9},{5... | collective-permute-start | bytes 3538952 | tf_op jit(solution)/shard_map/ppermute | solution.py:477
  272.1 27.6 %collective-permute-start.52 = (bf16[2,192,1536]{2,1,0:T(8,128)(2,1)S(1)}, bf16[2,192,1536]{2,1,0:T(8,128)(2,1)}, u32[]{:S(2)}, u32[]{:S(2)}) collective-permute-start(bf16[2,192,1536]{2,1,0:T(8,128)(2,1)S(1)} %pad_maximum_fusion.3), channel_id=1, source_target_pairs={{0,16},{4,20},{8,24},{12,28},{16,0},{20,4},{24,8},{28,12},{1,17},{... | collective-permute-start | bytes 3538952 | tf_op jit(solution)/shard_map/ppermute | solution.py:477
  296.2 13.4 %collective-permute-start.49 = (bf16[2,96,1536]{2,1,0:T(8,128)(2,1)}, bf16[2,96,1536]{2,1,0:T(8,128)(2,1)}, u32[]{:S(2)}, u32[]{:S(2)}) collective-permute-start(bf16[2,96,1536]{2,1,0:T(8,128)(2,1)} %add_convert_fusion.5), channel_id=1, source_target_pairs={{0,16},{4,20},{8,24},{12,28},{16,0},{20,4},{24,8},{28,12},{1,17},{... | collective-permute-start | bytes 1769480 | tf_op jit(solution)/shard_map/ppermute | solution.py:477
  301.2 11.4 %collective-permute-start.53 = (bf16[2,96,1536]{2,1,0:T(8,128)(2,1)S(1)}, bf16[2,96,1536]{2,1,0:T(8,128)(2,1)S(1)}, u32[]{:S(2)}, u32[]{:S(2)}) collective-permute-start(bf16[2,96,1536]{2,1,0:T(8,128)(2,1)S(1)} %add_convert_fusion.1), channel_id=1, source_target_pairs={{0,8},{4,12},{8,0},{12,4},{16,24},{20,28},{24,16},{28,20},{1,9},{5... | collective-permute-start | bytes 1769480 | tf_op jit(solution)/shard_map/ppermute | solution.py:477
  314.2 21.3 %collective-permute-start.54 = (bf16[96,1536]{1,0:T(8,128)(2,1)S(1)}, bf16[96,1536]{1,0:T(8,128)(2,1)S(1)}, u32[]{:S(2)}, u32[]{:S(2)}) collective-permute-start(bf16[96,1536]{1,0:T(8,128)(2,1)S(1)} %get-tuple-element.157), channel_id=1, source_target_pairs={{0,2},{1,3},{2,0},{3,1},{4,6},{5,7},{6,4},{7,5},{8,10},{9,11},{10,... | collective-permute-start | bytes 884744 | tf_op jit(solution)/shard_map/ppermute | solution.py:477
  316.0 19.5 %collective-permute-start.55 = (bf16[96,1536]{1,0:T(8,128)(2,1)S(1)}, bf16[96,1536]{1,0:T(8,128)(2,1)S(1)}, u32[]{:S(2)}, u32[]{:S(2)}) collective-permute-start(bf16[96,1536]{1,0:T(8,128)(2,1)S(1)} %get-tuple-element.158), channel_id=1, source_target_pairs={{0,3},{1,2},{2,1},{3,0},{4,7},{5,6},{6,5},{7,4},{8,11},{9,10},{10,... | collective-permute-start | bytes 884744 | tf_op jit(solution)/shard_map/ppermute | solution.py:477
  (59 other events, 580.1 us)
where the time goes:
time: 343 us; the launch traced here: 337 us
  waiting for transfers between devices  125 us (36%)
  Pallas kernels  90.8 us (26%)
  starting transfers between devices  64.3 us (19%)
  other arithmetic  30 us (9%)
  local copies, waits for them, and re-layouts  22.9 us (7%)
    ppermute x52, waiting for transfers between devices, swap(): return lax.ppermute(x, axis, [(i, i ^ mask) for i in range(size)])  115 us
    ppermute x52, starting transfers between devices, swap(): return lax.ppermute(x, axis, [(i, i ^ mask) for i in range(size)])  57.9 us
    pallas_call x2, Pallas kernels, attn_bwd(): pl.pallas_call(lambda *refs: attn_bwd_kernel(last, *refs), grid=(2,), in_...  33 us
    pallas_call x2, Pallas kernels, attn_fwd(): pl.pallas_call(lambda *refs: attn_fwd_kernel(base, last, *refs), grid=(2,...  24.7 us
    pallas_call x2, Pallas kernels, ff_both(): pl.pallas_call(lambda *refs: ff_kernel(last, *refs), grid=(2,), in_specs=...  21.8 us
    unnamed x80, local copies, waits for them, and re-layouts  12.4 us
  transfers between devices with their start and end apart: 56, of which 29 were waited for; matrix products, arithmetic and copies ran while one was open for 14% of the time, Pallas kernels for 5%

commit v1 on v0

--- a/solution.py
+++ b/solution.py
@@ -25,7 +25,6 @@
 bf16 = jnp.bfloat16
 tiny_eps = 1e-06
 masked_score = -1e30
-highest = lax.Precision.HIGHEST
 
 
 def dot(a, b):
@@ -117,17 +116,17 @@
     )(*args)
 
 
-def join(w_s, halves, step):
-    for n in range(2):
+def join(w_s, pieces, step):
+    for n in range(len(pieces) // 8):
 
         @pl.when(step == n)
         def _(n=n):
-            w_s[0:HALF, :] = halves[2 * n][...]
-            w_s[HALF:D, :] = halves[2 * n + 1][...]
-
-
-attn_specs = [pl.BlockSpec((HALF, D), lambda i: (0, 2))] * 4
-ff_specs = [pl.BlockSpec((HALF, 3 * FFS), lambda i: (0, 0))] * 4
+            for k in range(8):
+                w_s[k * 96 : k * 96 + 96, :] = pieces[8 * n + k][...]
+
+
+attn_spec = pl.BlockSpec((96, D), lambda i: (0, 2))
+ff_specs = [pl.BlockSpec((96, 3 * FFS), lambda i: (0, 0))] * 16
 
 
 def keys_of(tile, c):
@@ -152,9 +151,9 @@
 
 def attn_fwd_kernel(base, last, *refs):
     x, f0, f1, f2, f3 = refs[:5]
-    halves = refs[5:9]
-    near_at, far_at, tables, mask = refs[9:13]
-    refs = refs[13:]
+    pieces = refs[5:21]
+    near_at, far_at, tables, mask = refs[21:25]
+    refs = refs[25:]
     if last:
         before, tok, gains = refs[:3]
         refs = refs[3:]
@@ -167,7 +166,7 @@
     def _():
         fill_x(x_s, x, (f0, f1, f2, f3))
 
-    join(w_s, halves, step)
+    join(w_s, pieces, step)
     r = dot(x_s[...], w_s[:, 0:640]).astype(bf16)
     r_ref[0] = r
     low = lax.broadcasted_iota(jnp.int32, (BLOCK, 128), 1) < 64
@@ -221,7 +220,7 @@
 x_specs = [whole_spec((EXT, D))] + [whole_spec((FAR, D))] * 4
 
 
-def attn_fwd(base, x, fars, halves, near_at, far_at, tables, mask, *rest):
+def attn_fwd(base, x, fars, pieces, near_at, far_at, tables, mask, *rest):
     last = len(rest) > 0
     outs = [
         (slab_spec((6, BLOCK, KEYS)), shape_of((2, 6, BLOCK, KEYS), bf16)),
@@ -237,7 +236,7 @@
         lambda *refs: attn_fwd_kernel(base, last, *refs),
         grid=(2,),
         in_specs=x_specs
-        + attn_specs
+        + [attn_spec] * 16
         + [
             whole_spec((1, 3 * BLOCK)),
             whole_spec((16, 128)),
@@ -250,17 +249,21 @@
         scratch_shapes=([pltpu.VMEM((ROWS, D), f32)] if last else [])
         + [pltpu.VMEM((ALL, D), bf16), pltpu.VMEM((D, D), bf16)],
         name="attn_fwd_b" if last else "attn_fwd_a",
-    )(x, *fars, *halves, near_at, far_at, tables, mask, *rest)
-
-
-def attn_bwd_kernel(last, *refs):
+    )(x, *fars, *pieces, near_at, far_at, tables, mask, *rest)
+
+
+def attn_bwd_kernel(slabs, more, last, *refs):
     x, f0, f1, f2, f3, rl = refs[:6]
-    halves = refs[6:10]
-    r_ref, p_ref, a_ref = refs[10:13]
-    refs = refs[13:]
-    if last:
+    pieces = refs[6 : 6 + 8 * slabs]
+    refs = refs[6 + 8 * slabs :]
+    r_ref, p_ref, a_ref = refs[:3]
+    refs = refs[3:]
+    if more:
         before = refs[0]
-        down, doth, near_ref, far_ref, own, lo, hi, fown, s1, s2, s3, xg, x_s, w_s, dr_s = refs[1:]
+        refs = refs[1:]
+    if last:
+        where_ref = refs[0]
+        down, doth, near_ref, far_ref, own, fown, s1, s2, s3, s4, xg, x_s, w_s, dr_s = refs[1:]
     else:
         down, doth, near_ref, far_ref, xg, x_s, w_s, dr_s = refs
     step = pl.program_id(0)
@@ -269,7 +272,7 @@
     def _():
         fill_x(x_s, x, (f0, f1, f2, f3))
 
-    join(w_s, halves, step)
+    join(w_s, pieces, step)
     da = dot(rl[...], w_s[:, 512:768]).astype(bf16)
     low = lax.broadcasted_iota(jnp.int32, (BLOCK, 128), 1) < 64
     zero = jnp.zeros((BLOCK, 128), bf16)
@@ -317,7 +320,7 @@
 
     @pl.when(step == 0)
     def _():
-        xg[...] = before[...] + part if last else part
+        xg[...] = before[...] + part if more else part
 
     @pl.when(step > 0)
     def _():
@@ -333,54 +336,66 @@
 
         @pl.when(step == pl.num_programs(0) - 1)
         def _():
-            lo[...] = xg[0:BLOCK].astype(bf16)
             own[...] = xg[BLOCK : BLOCK + ROWS]
-            hi[...] = xg[BLOCK + ROWS : EXT].astype(bf16)
             fown[...] = xg[EXT : EXT + FAR]
-            for n, ref in enumerate((s1, s2, s3)):
-                ref[...] = xg[EXT + FAR + n * FAR : EXT + 2 * FAR + n * FAR].astype(bf16)
-
-
-def attn_bwd(x, fars, rl, halves, r, p, a, *rest):
-    last = len(rest) > 0
+            lo = xg[0:BLOCK].astype(bf16)
+            hi = xg[BLOCK + ROWS : EXT].astype(bf16)
+            odd = where_ref[0] > 0
+            s1[0:BLOCK] = jnp.where(odd, lo, hi)
+            s4[...] = jnp.where(odd, hi, lo)
+            s1[BLOCK:] = xg[EXT + FAR : EXT + 2 * FAR].astype(bf16)
+            s2[...] = xg[EXT + 2 * FAR : EXT + 3 * FAR].astype(bf16)
+            s3[...] = xg[EXT + 3 * FAR : EXT + 4 * FAR].astype(bf16)
+
+
+def attn_bwd(x, fars, rl, pieces, offset, r, p, a, *rest):
+    slabs = len(pieces) // 8
+    more = len(rest) > 0
+    last = len(rest) > 1
+
+    def part_spec(shape):
+        return pl.BlockSpec((1,) + shape, lambda i: (i + offset,) + (0,) * len(shape))
+
     outs = [
-        (slab_spec((HALF, D)), shape_of((2, HALF, D), bf16)),
-        (slab_spec((HALF, D)), shape_of((2, HALF, D), bf16)),
-        (slab_spec((3, 3 * BLOCK)), shape_of((2, 3, 3 * BLOCK), f32)),
-        (slab_spec((3, 16, 128)), shape_of((2, 3, 16, 128), f32)),
+        (slab_spec((HALF, D)), shape_of((slabs, HALF, D), bf16)),
+        (slab_spec((HALF, D)), shape_of((slabs, HALF, D), bf16)),
+        (slab_spec((3, 3 * BLOCK)), shape_of((slabs, 3, 3 * BLOCK), f32)),
+        (slab_spec((3, 16, 128)), shape_of((slabs, 3, 16, 128), f32)),
     ]
     if last:
-        for rows, dtype in ((ROWS, f32), (BLOCK, bf16), (BLOCK, bf16), (FAR, f32)) + ((FAR, bf16),) * 3:
+        for rows, dtype in (
+            (ROWS, f32), (FAR, f32), (BLOCK + FAR, bf16), (FAR, bf16), (FAR, bf16), (BLOCK, bf16),
+        ):
             outs.append((whole_spec((rows, D)), shape_of((rows, D), dtype)))
     else:
         outs.append((whole_spec((ALL, D)), shape_of((ALL, D), f32)))
     return pl.pallas_call(
-        lambda *refs: attn_bwd_kernel(last, *refs),
-        grid=(2,),
+        lambda *refs: attn_bwd_kernel(slabs, more, last, *refs),
+        grid=(slabs,),
         in_specs=x_specs
         + [whole_spec((ROWS, D))]
-        + attn_specs
-        + [slab_spec((ALL, 640)), slab_spec((6, BLOCK, KEYS)), slab_spec((ROWS, 256))]
-        + ([whole_spec((ALL, D))] if last else []),
+        + [attn_spec] * (8 * slabs)
+        + [part_spec((ALL, 640)), part_spec((6, BLOCK, KEYS)), part_spec((ROWS, 256))]
+        + ([whole_spec((ALL, D))] if more else [])
+        + ([pl.BlockSpec(memory_space=pltpu.SMEM)] if last else []),
         out_specs=[o[0] for o in outs],
         out_shape=[o[1] for o in outs],
         scratch_shapes=([pltpu.VMEM((ALL, D), f32)] if last else [])
         + [pltpu.VMEM((ALL, D), bf16), pltpu.VMEM((D, D), bf16), pltpu.VMEM((ALL, 640), f32)],
-        name="attn_bwd_b" if last else "attn_bwd_a",
-    )(x, *fars, rl, *halves, r, p, a, *rest)
+    )(x, *fars, rl, *pieces, r, p, a, *rest)
 
 
 def ff_kernel(last, *refs):
     nf, go = refs[:2]
-    halves = refs[2:6]
-    refs = refs[6:]
+    pieces = refs[2:18]
+    refs = refs[18:]
     if last:
         out_a, ng_a, res, gains, order = refs[:5]
         down, doth, output, res_grad, rl, gain_grad, out_acc, ng_acc, w_s = refs[5:]
     else:
         down, doth, out_acc, ng_acc, w_s = refs
     step = pl.program_id(0)
-    join(w_s, halves, step)
+    join(w_s, pieces, step)
     gate = dot(nf[...], w_s[:, 0:FFS])
     up = dot(nf[...], w_s[:, FFS : 2 * FFS])
     hg = dot(go[...], w_s[:, 2 * FFS : 3 * FFS])
@@ -421,7 +436,7 @@
             gain_grad[...] = jnp.sum(e * v * r, axis=0, keepdims=True)
 
 
-def ff_both(nf, go, halves, *rest):
+def ff_both(nf, go, pieces, *rest):
     last = len(rest) > 0
     wide = (whole_spec((ROWS, D)), shape_of((ROWS, D), f32))
     narrow = (whole_spec((ROWS, D)), shape_of((ROWS, D), bf16))
@@ -439,37 +454,99 @@
         out_specs=[o[0] for o in outs],
         out_shape=[o[1] for o in outs],
         scratch_shapes=([pltpu.VMEM((ROWS, D), f32)] * 2 if last else []) + [pltpu.VMEM((D, 3 * FFS), bf16)],
-        name="ff_b" if last else "ff_a",
-    )(nf, go, *halves, *rest)
-
-
-def post_kernel(own, lo, hi, f0, f1, f2, f3, res_grad, tok, pooled, mem, gains, order, grad, gain_grad):
-    e = f0[...] + f1[...].astype(f32) + f2[...].astype(f32) + f3[...].astype(f32)
+        name="ff_a" if last else "ff_b",
+    )(nf, go, *pieces, *rest)
+
+
+def split3(value):
+    parts = []
+    for _ in range(3):
+        parts.append(value.astype(bf16))
+        value = value - parts[-1].astype(f32)
+    return parts
+
+
+def post_kernel(
+    where_ref, own, f0, r1, r2, r3, r4, res_grad, tok, pooled, mem, gains, order, gain_ff,
+    near_0, near_1, near_b, far_0, far_1, far_b, near_at, far_at, grad, small,
+):
+    e = f0[...] + r1[BLOCK:].astype(f32) + r2[...].astype(f32) + r3[...].astype(f32)
     v = pooled[...]
     r = rsqrt_mean(v)
     spread = row_term(v, r, gains[2:3], e)
-    gain_grad[1:2] = jnp.sum(e * v * r, axis=0, keepdims=True)
-    wide = own[...] + jnp.concatenate([lo[...], hi[...]], axis=0).astype(f32)
-    for _ in range(3):
-        part = spread.astype(bf16)
+    gain_global = jnp.sum(e * v * r, axis=0, keepdims=True)
+    odd = where_ref[0] > 0
+    near = r1[0:BLOCK].astype(f32)
+    other = jnp.where(where_ref[1] > 0, r4[...].astype(f32), 0.0)
+    wide = own[...] + jnp.concatenate(
+        [jnp.where(odd, near, other), jnp.where(odd, other, near)], axis=0
+    )
+    for part in split3(spread):
         wide = wide + dot_tn(mem[...], part)
-        spread = spread - part.astype(f32)
     v = tok[...].astype(f32)
     r = rsqrt_mean(v)
-    gain_grad[0:1] = jnp.sum(wide * v * r, axis=0, keepdims=True)
     rest = res_grad[...] + row_term(v, r, gains[0:1], wide)
+    sums = jnp.concatenate(
+        [jnp.sum(wide * v * r, axis=0, keepdims=True), gain_ff[...], gain_global, jnp.zeros((5, D), f32)]
+    )
     total = jnp.zeros((ROWS, D), f32)
-    for _ in range(3):
-        part = rest.astype(bf16)
+    gain_sums = jnp.zeros((8, D), f32)
+    for part, gain_part in zip(split3(rest), split3(sums)):
         total = total + dot_nt(part, order[...])
-        rest = rest - part.astype(f32)
+        gain_sums = gain_sums + dot_nt(gain_part, order[...])
     grad[...] = total
+    small[0:8] = gain_sums
+    bucket = lax.broadcasted_iota(jnp.int32, (BUCKETS, 3 * BLOCK), 0)
+    near_hot = (jnp.broadcast_to(near_at[...], bucket.shape) == bucket).astype(bf16)
+    far_hot = [
+        (jnp.broadcast_to(far_at[a : a + 1], (BUCKETS, 128)) == bucket[:, 0:128]).astype(bf16) for a in range(16)
+    ]
+    at = lax.broadcasted_iota(jnp.int32, (16, 3), 0)
+    col = lax.broadcasted_iota(jnp.int32, (16, 3), 1)
+    near_of = (near_0[0], near_1[0], near_b[0], near_b[1])
+    far_of = ((far_0, 0), (far_1, 0), (far_b, 0), (far_b, 1))
+    near_sum = jnp.zeros((16, BUCKETS), f32)
+    far_sum = jnp.zeros((16, BUCKETS), f32)
+    for k in range(4):
+        place = (at == col + 3 * (where_ref[2] ^ k)).astype(bf16)
+        near_table = sum(dot_nt(part, near_hot) for part in split3(near_of[k]))
+        far_table = jnp.zeros((3, BUCKETS), f32)
+        for a in range(16):
+            far_grad = far_of[k][0][far_of[k][1], :, a]
+            far_table = far_table + sum(dot_nt(part, far_hot[a]) for part in split3(far_grad))
+        near_sum = near_sum + sum(dot(place, part) for part in split3(near_table))
+        far_sum = far_sum + sum(dot(place, part) for part in split3(far_table))
+    small[8:24] = jnp.zeros((16, D), f32)
+    small[8:24, 0:BUCKETS] = near_sum
+    small[8:24, 128 : 128 + BUCKETS] = far_sum
 
 
 def post(*args):
+    in_vmem = pl.BlockSpec(memory_space=pltpu.VMEM)
     return pl.pallas_call(
-        post_kernel, out_shape=[shape_of((ROWS, D), f32), shape_of((2, D), f32)], name="post"
+        post_kernel,
+        in_specs=[pl.BlockSpec(memory_space=pltpu.SMEM)] + [in_vmem] * (len(args) - 1),
+        out_shape=[shape_of((ROWS, D), f32), shape_of((24, D), f32)],
+        name="post",
     )(*args)
+
+
+def unpack_kernel(s0, s1, s2, s3, q, k, v, o):
+    wide = s0[...].astype(f32) + s1[...].astype(f32) + s2[...].astype(f32) + s3[...].astype(f32)
+    q[:, 0:128] = wide[:, 0:128]
+    k[:, 0:128] = wide[:, 128:256]
+    v[:, 0:128] = wide[:, 256:384]
+    q[:, 128:192] = wide[:, 384:448]
+    v[:, 128:192] = wide[:, 448:512]
+    k[:, 128:192] = wide[:, 512:576]
+    o[:, 128:192] = wide[:, 576:640]
+    o[:, 0:128] = wide[:, 640:768]
+
+
+def unpack(*slabs):
+    return pl.pallas_call(
+        unpack_kernel, out_shape=[shape_of((slabs[0].shape[0], 192), f32)] * 4, name="unpack"
+    )(*slabs)
 
 
 def swap(x, axis, mask):
@@ -481,13 +558,11 @@
     return list(range(3, lax.axis_size("fsdp").bit_length() - 1))
 
 
-def gather_own(slab, bits):
-    first, second = bits
-    one = swap(slab, "fsdp", 1 << first)
-    two = swap(slab, "fsdp", 1 << second)
-    both = swap(one, "fsdp", 1 << second)
-    middle = [one, two] if first == 1 else [two, one]
-    return jnp.concatenate([slab] + middle + [both])
+def near_swaps(x):
+    got = [x]
+    for n in (1, 2, 3):
+        got.append(swap(x, "fsdp", n << 1))
+    return got
 
 
 def gather_high(shard):
@@ -503,20 +578,22 @@
     return got
 
 
-def scatter_pair(own, oth, bits):
-    first, second = bits
-    came = swap(oth, "fsdp", 1)
+def scatter_pair(sources):
+    dtype = sources[0][0].dtype
+    came = []
+    for _, oth in sources:
+        came.append(swap(oth, "fsdp", 1))
 
     def piece(n):
         rows = slice(n * 96, n * 96 + 96)
-        return own[:, rows].astype(f32) + came[:, rows].astype(f32)
-
-    at = {1: 1, 2: 2}
-    send = jnp.concatenate([piece(at[first]), piece(3)], axis=1).astype(own.dtype)
-    got = swap(send, "fsdp", 1 << first)
-    send = (piece(at[second]) + got[:, 96:].astype(f32)).astype(own.dtype)
-    more = swap(send, "fsdp", 1 << second)
-    total = (piece(0) + got[:, :96].astype(f32) + more.astype(f32)).astype(own.dtype)
+        return jnp.concatenate(
+            [own[:, rows].astype(f32) + got[:, rows].astype(f32) for (own, _), got in zip(sources, came)]
+        )
+
+    total = piece(0)
+    for n in (1, 2, 3):
+        total = total + swap(piece(n).astype(dtype), "fsdp", n << 1).astype(f32)
+    total = total.astype(dtype)
     for bit in high_bits()[::-1]:
         half = total.shape[1] // 2
         total = total[:, :half] + swap(total[:, half:], "fsdp", 1 << bit)
@@ -524,11 +601,10 @@
 
 
 def scatter_tensor(slabs):
-    total = slabs[0].astype(f32)
+    got = [slabs[0]]
     for k in (1, 2, 3):
-        got = swap(slabs[k], "tensor", k)
-        total = total + got.astype(f32)
-    return total
+        got.append(swap(slabs[k], "tensor", k))
+    return got
 
 
 def inner(
@@ -544,8 +620,10 @@
     down_one = [(i + 1, i) for i in range(last)]
 
     gains = jnp.stack([ln_attn, ln_ff, ln_global])[:, None, :]
-    for bit in high_bits() + [1, 2, 0]:
+    for bit in high_bits():
         gains = jnp.concatenate([gains, swap(gains, "fsdp", 1 << bit)], axis=1)
+    gains = jnp.concatenate(near_swaps(gains), axis=1)
+    gains = jnp.concatenate([gains, swap(gains, "fsdp", 1)], axis=1)
     gains = jnp.pad(gains.reshape(3, D).astype(f32), ((0, 5), (0, 0)))
     left = lax.ppermute(tokens[ROWS - BLOCK :], "tensor", up_one)
     right = lax.ppermute(tokens[:BLOCK], "tensor", down_one)
@@ -600,75 +678,52 @@
     far_at = dot(slot_at.astype(bf16), slot_is.astype(bf16)).astype(jnp.int32)
 
     small_work = (mask, near_at, far_at, tables)
-    pairs = []
+    whole = []
     for n, slab in enumerate(slabs):
-        own_half = gather_own(slab, ((1, 2), (2, 1))[n % 2])
+        own_pieces = near_swaps(slab)
         if n == 1:
-            own_half, (mask, near_at, far_at, tables) = lax.optimization_barrier(
-                (own_half, small_work)
-            )
-        pairs.append([own_half, swap(own_half, "fsdp", 1)])
-    pair_a = pairs[0] + pairs[1]
-    pair_b = pairs[2] + pairs[3]
+            own_pieces, (mask, near_at, far_at, tables) = lax.optimization_barrier((own_pieces, small_work))
+        whole.append(own_pieces + [swap(piece, "fsdp", 1) for piece in own_pieces])
+    pair_a = whole[0] + whole[1]
+    pair_b = whole[2] + whole[3]
 
     acc, p_a, r_a, at_a = attn_fwd(0, x, fars, pair_a, near_at, far_at, tables, mask)
     residual, nf, p_b, r_b, at_b = attn_fwd(
         2, x, fars, pair_b, near_at, far_at, tables, mask, acc, tok, gains
     )
-    fo_a, ft_a, out_a, ng_a = ff_both(nf, go, pair_a)
-    fo_b, ft_b, output, res_grad, rl, gain_ff_grad = ff_both(
-        nf, go, pair_b, out_a, ng_a, residual, gains, order
+    fo_b, ft_b, out_b, ng_b = ff_both(nf, go, pair_b)
+    fo_a, ft_a, output, res_grad, rl, gain_ff = ff_both(
+        nf, go, pair_a, out_b, ng_b, residual, gains, order
     )
-    sum_fa = scatter_pair(fo_a, ft_a, (1, 2))
-    sum_fb = scatter_pair(fo_b, ft_b, (2, 1))
-    do_a, dt_a, nb_a, fb_a, xg = attn_bwd(x, fars, rl, pair_a, r_a, p_a, at_a)
-    do_b, dt_b, nb_b, fb_b, own, lo, hi, f0, s1, s2, s3 = attn_bwd(
-        x, fars, rl, pair_b, r_b, p_b, at_b, xg
+    sum_fb = scatter_pair([(fo_b, ft_b)])
+    sum_fa = scatter_pair([(fo_a, ft_a)])
+    where = jnp.stack([z & 1, ((z == 1) | (z == 2)).astype(jnp.int32), z]).astype(jnp.int32)
+    do_b, dt_b, nb_b, fb_b, xg = attn_bwd(x, fars, rl, pair_b, 0, r_b, p_b, at_b)
+    do_1, dt_1, nb_1, fb_1, xg = attn_bwd(x, fars, rl, whole[1], 1, r_a, p_a, at_a, xg)
+    do_0, dt_0, nb_0, fb_0, own, f0, s1, s2, s3, s4 = attn_bwd(x, fars, rl, whole[0], 0, r_a, p_a, at_a, xg, where)
+    sum_ab = scatter_pair([(do_b, dt_b)])
+    sum_aa = scatter_pair([(do_0, dt_0), (do_1, dt_1)])
+    got = []
+    for k, sent in ((1, s1), (2, s2), (3, s3)):
+        got.append(swap(sent, "tensor", k))
+    got.append(lax.ppermute(s4, "tensor", [(1, 2), (2, 1)]))
+    grad_tokens, small = post(
+        where, own, f0, *got, res_grad, tok, pooled, member, gains, order, gain_ff,
+        nb_0, nb_1, nb_b, fb_0, fb_1, fb_b, near_at, far_at,
     )
-    sum_aa = scatter_pair(do_a, dt_a, (1, 2))
-    sum_ab = scatter_pair(do_b, dt_b, (2, 1))
-    to_left = lax.ppermute(lo, "tensor", down_one)
-    to_right = lax.ppermute(hi, "tensor", up_one)
-    f1, f2, f3 = [swap(s, "tensor", k) for s, k in ((s1, 1), (s2, 2), (s3, 3))]
-    late = lax.optimization_barrier((nb_a, nb_b, fb_a, fb_b, f1, f2, f3))
-    grad_tokens, gain_grads = post(
-        own, to_right, to_left, f0, f1, f2, f3, res_grad, tok, pooled, member, gains, order
-    )
-
-    nb_a, nb_b, fb_a, fb_b, f1, f2, f3 = late
-    near_table = jnp.dot(
-        jnp.concatenate([nb_a, nb_b]).reshape(HEADS, 3 * BLOCK), local_onehot[0].astype(f32), precision=highest
-    )
-    far_hot = (far_at.reshape(-1)[:, None] == bucket).astype(f32)
-    far_table = jnp.dot(
-        jnp.concatenate([fb_a, fb_b]).reshape(HEADS, 16 * 128), far_hot, precision=highest
-    )
-    table_part = jnp.concatenate(
-        [near_table.reshape(4, 3 * BUCKETS), far_table.reshape(4, 3 * BUCKETS)], axis=1
-    )
-    gain_part = jnp.stack([gain_grads[0], gain_ff_grad[0], gain_grads[1]])
-    gain_part = gain_part.reshape(3, count, width).transpose(1, 0, 2).reshape(count, 3 * width)
-    small = jnp.concatenate(
-        [
-            jnp.broadcast_to(gain_part[None], (4, count, 3 * width)),
-            jnp.broadcast_to(table_part[:, None], (4, count, 6 * BUCKETS)),
-        ],
-        axis=2,
-    )
-    for bit in [0, 2, 1] + high_bits()[::-1]:
-        half = small.shape[1] // 2
-        small = small[:, :half] + swap(small[:, half:], "fsdp", 1 << bit)
-    small = scatter_tensor(small)[0]
-    gain_sum = small[: 3 * width].reshape(3, width)
-    table_sum = small[3 * width :].reshape(2, 3, BUCKETS).transpose(0, 2, 1)
-
-    ff_sum = scatter_tensor([sum_fa[0], sum_fa[1], sum_fb[0], sum_fb[1]])
-    at_sum = scatter_tensor([sum_aa[0], sum_aa[1], sum_ab[0], sum_ab[1]])
-    col = lambda n: at_sum[:, n * 64 : n * 64 + 64]
-    grad_query = jnp.concatenate([at_sum[:, 0:128], col(6)], axis=1)
-    grad_key = jnp.concatenate([at_sum[:, 128:256], col(8)], axis=1)
-    grad_value = jnp.concatenate([at_sum[:, 256:384], col(7)], axis=1)
-    grad_out_w = jnp.concatenate([at_sum[:, 640:768], col(9)], axis=1).T
+    got = [small] + gather_tensor(small)
+    small = (got[0] + got[1]) + (got[2] + got[3])
+    small = small + swap(small, "fsdp", 1)
+    got = near_swaps(small)
+    small = (got[0] + got[1]) + (got[2] + got[3])
+    for bit in high_bits():
+        small = small + swap(small, "fsdp", 1 << bit)
+    gain_sum = lax.dynamic_slice(small, (0, f * width), (3, width))
+    table_sum = lax.dynamic_slice(small, (8 + 3 * z, 0), (3, 256))
+
+    parts = scatter_tensor([sum_fa[0], sum_fa[1], sum_fb[0], sum_fb[1]])
+    ff_sum = sum(part.astype(f32) for part in parts)
+    grad_query, grad_key, grad_value, grad_out_t = unpack(*scatter_tensor([sum_aa[0], sum_aa[1], sum_ab[0], sum_ab[1]]))
     return (
         output,
         grad_tokens,
@@ -678,12 +733,12 @@
         grad_query,
         grad_key,
         grad_value,
-        grad_out_w,
+        grad_out_t.T,
         ff_sum[:, 0:FFS],
         ff_sum[:, FFS : 2 * FFS],
         ff_sum[:, 2 * FFS : 3 * FFS].T,
-        table_sum[0],
-        table_sum[1],
+        table_sum[:, 0:BUCKETS].T,
+        table_sum[:, 128 : 128 + BUCKETS].T,
     )
 
 

time: 343 us -> 379 us (1.10)
  the two profiles are of different devices: /device:TPU:0 before, /device:TPU:9 now
where the time goes in v1:
time: 379 us; the launch traced here: 373 us
  waiting for transfers between devices  133 us (35%)
  starting transfers between devices  108 us (28%)
  Pallas kernels  95.3 us (25%)
  other arithmetic  17.9 us (5%)
  local copies, waits for them, and re-layouts  16.4 us (4%)
    ppermute x71, waiting for transfers between devices, swap(): return lax.ppermute(x, axis, [(i, i ^ mask) for i in range(size)])  131 us
    ppermute x71, starting transfers between devices, swap(): return lax.ppermute(x, axis, [(i, i ^ mask) for i in range(size)])  99.5 us
    pallas_call x3, Pallas kernels, attn_bwd(): pl.pallas_call(lambda *refs: attn_bwd_kernel(slabs, more, last, *refs), g...  33.4 us
    pallas_call x2, Pallas kernels, attn_fwd(): pl.pallas_call(lambda *refs: attn_fwd_kernel(base, last, *refs), grid=(2,...  24.9 us
    pallas_call x2, Pallas kernels, ff_both(): pl.pallas_call(lambda *refs: ff_kernel(last, *refs), grid=(2,), in_specs=...  21.8 us
  transfers between devices with their start and end apart: 74, of which 28 were waited for; matrix products, arithmetic and copies ran while one was open for 8% of the time, Pallas kernels for 5%

profile of v1, /device:TPU:9, one launch (start us, length us, event | category | flops | bytes accessed | tf_op | source)
XLA Modules:
  0.0 373.0 jit_solution(10776976759863703787)
XLA Ops:
  1.4 2.2 collective-permute-start.4
  19.2 3.2 collective-permute-start
  27.7 3.8 %prep.1 = (bf16[512,768]{1,0:T(8,128)(2,1)}, bf16[256,768]{1,0:T(8,128)(2,1)}, bf16[256,768]{1,0:T(8,128)(2,1)}, f32[32,768]{1,0:T(8,128)}, bf16[32,768]{1,0:T(8,128)(2,1)}) custom-call(bf16[128,768]{1,0:T(8,128)(2,1)} %copy-done.31, bf16[256,768]{1,0:T(8,128)(2,1)} %tok.1, bf16[128,768]{1,0:T(8,128)(2,1)} %copy-done.30, bf16[256,768]{1,0:T(8,128)(2,1)} %grad.1, ...), custom_call_target="tpu_custom_call" | custom-call | tf_op jit(solution)/shard_map/prep/pallas_call | solution.py:106
  44.9 3.2 collective-permute-start.35
  49.8 8.9 %collective-permute-start.33 = (bf16[96,2304]{1,0:T(8,128)(2,1)S(1)}, bf16[96,2304]{1,0:T(8,128)(2,1)S(1)}, u32[]{:S(2)}, u32[]{:S(2)}) collective-permute-start(bf16[96,2304]{1,0:T(8,128)(2,1)S(1)} %collective-permute-done.29.refs_6_.refs_3_.refs_7_), channel_id=1, source_target_pairs={{0,4},{4,0},{8,12},{12,8},{16,20},{20,16},{24,28},{28,24},{1,5},{5... | collective-permute-start | bytes 1327112 | tf_op jit(solution)/shard_map/ppermute | solution.py:554
  59.7 15.5 %collective-permute-done.9.refs_5_.refs_2_.refs_6_ = bf16[96,2304]{1,0:T(8,128)(2,1)S(1)} collective-permute-done((bf16[96,2304]{1,0:T(8,128)(2,1)S(1)}, bf16[96,2304]{1,0:T(8,128)(2,1)S(1)}, u32[]{:S(2)}, u32[]{:S(2)}) %collective-permute-start.9) | collective-permute-done | bytes 442400 | tf_op jit(solution)/shard_map/ppermute | solution.py:554
  76.9 4.8 %collective-permute-start.21 = (bf16[96,2304]{1,0:T(8,128)(2,1)S(1)}, bf16[96,2304]{1,0:T(8,128)(2,1)S(1)}, u32[]{:S(2)}, u32[]{:S(2)}) collective-permute-start(bf16[96,2304]{1,0:T(8,128)(2,1)S(1)} %collective-permute-done.17.refs_13_.refs_10_.refs_14_), channel_id=1, source_target_pairs={{0,4},{4,0},{8,12},{12,8},{16,20},{20,16},{24,28},{28,24},{1,5},{5... | collective-permute-start | bytes 1327112 | tf_op jit(solution)/shard_map/ppermute | solution.py:554
  83.4 7.1 %collective-permute-done.27.refs_15_.refs_12_.refs_8_ = bf16[96,2304]{1,0:T(8,128)(2,1)S(1)} collective-permute-done((bf16[96,2304]{1,0:T(8,128)(2,1)S(1)}, bf16[96,2304]{1,0:T(8,128)(2,1)S(1)}, u32[]{:S(2)}, u32[]{:S(2)}) %collective-permute-start.27) | collective-permute-done | bytes 442400 | tf_op jit(solution)/shard_map/ppermute | solution.py:554
  90.5 12.1 %collective-permute-start.13 = (bf16[96,2304]{1,0:T(8,128)(2,1)S(1)}, bf16[96,2304]{1,0:T(8,128)(2,1)}, u32[]{:S(2)}, u32[]{:S(2)}) collective-permute-start(bf16[96,2304]{1,0:T(8,128)(2,1)S(1)} %collective-permute-done.9.refs_5_.refs_2_.refs_6_), channel_id=1, source_target_pairs={{0,4},{4,0},{8,12},{12,8},{16,20},{20,16},{24,28},{28,24},{1,5},{5... | collective-permute-start | bytes 1327112 | tf_op jit(solution)/shard_map/ppermute | solution.py:554
  104.6 4.9 %collective-permute-done.19.refs_15_.refs_12_.refs_16_ = bf16[96,2304]{1,0:T(8,128)(2,1)S(1)} collective-permute-done((bf16[96,2304]{1,0:T(8,128)(2,1)S(1)}, bf16[96,2304]{1,0:T(8,128)(2,1)S(1)}, u32[]{:S(2)}, u32[]{:S(2)}) %collective-permute-start.19) | collective-permute-done | bytes 442400 | tf_op jit(solution)/shard_map/ppermute | solution.py:554
  117.3 11.9 %collective-permute-start.36 = (bf16[96,2304]{1,0:T(8,128)(2,1)S(1)}, bf16[96,2304]{1,0:T(8,128)(2,1)S(1)}, u32[]{:S(2)}, u32[]{:S(2)}) collective-permute-start(bf16[96,2304]{1,0:T(8,128)(2,1)S(1)} %collective-permute-done.25.refs_13_.refs_10_.refs_6_), channel_id=1, source_target_pairs={{0,4},{4,0},{8,12},{12,8},{16,20},{20,16},{24,28},{28,24},{1,5},{5... | collective-permute-start | bytes 1327112 | tf_op jit(solution)/shard_map/ppermute | solution.py:554
  134.1 12.2 %attn_fwd_a.1 = (f32[256,768]{1,0:T(8,128)}, bf16[2,6,128,512]{3,2,1,0:T(8,128)(2,1)}, bf16[2,640,640]{2,1,0:T(8,128)(2,1)}, bf16[2,256,256]{2,1,0:T(8,128)(2,1)}) custom-call(bf16[512,768]{1,0:T(8,128)(2,1)} %get-tuple-element.72.refs_0_, bf16[32,768]{1,0:T(8,128)(2,1)} %get-tuple-element.73.refs_1_, bf16[32,768]{1,0:T(8,128)(2,1)} %collective-permute-done.6.refs_2_, ...), custom_call_target="tpu_custom_call" | custom-call | tf_op jit(solution)/shard_map/attn_fwd_a/pallas_call | solution.py:235
  146.4 12.7 %attn_fwd_b.1 = (f32[256,768]{1,0:T(8,128)}, bf16[256,768]{1,0:T(8,128)(2,1)}, bf16[2,6,128,512]{3,2,1,0:T(8,128)(2,1)}, bf16[2,640,640]{2,1,0:T(8,128)(2,1)}, bf16[2,256,256]{2,1,0:T(8,128)(2,1)}) custom-call(bf16[512,768]{1,0:T(8,128)(2,1)} %get-tuple-element.72.refs_0_, bf16[32,768]{1,0:T(8,128)(2,1)} %get-tuple-element.73.refs_1_, ...), custom_call_target="tpu_custom_call" | custom-call | tf_op jit(solution)/shard_map/attn_fwd_b/pallas_call | solution.py:235
  159.1 9.2 %ff_b.1 = (bf16[2,384,1536]{2,1,0:T(8,128)(2,1)}, bf16[2,384,1536]{2,1,0:T(8,128)(2,1)}, f32[256,768]{1,0:T(8,128)}, f32[256,768]{1,0:T(8,128)}) custom-call(bf16[256,768]{1,0:T(8,128)(2,1)} %get-tuple-element.84.refs_0_, bf16[256,768]{1,0:T(8,128)(2,1)} %get-tuple-element.85.refs_1_, bf16[96,2304]{1,0:T(8,128)(2,1)} %copy-done.17, ...), custom_call_target="tpu_custom_call" | custom-call | tf_op jit(solution)/shard_map/ff_b/pallas_call | solution.py:448
  168.3 12.6 %ff_a.1 = (bf16[2,384,1536]{2,1,0:T(8,128)(2,1)}, bf16[2,384,1536]{2,1,0:T(8,128)(2,1)}, bf16[256,768]{1,0:T(8,128)(2,1)}, f32[256,768]{1,0:T(8,128)}, bf16[256,768]{1,0:T(8,128)(2,1)}, /*index=5*/f32[1,768]{1,0:T(1,128)}) custom-call(bf16[256,768]{1,0:T(8,128)(2,1)} %get-tuple-element.84.refs_0_, bf16[256,768]{1,0:T(8,128)(2,1)} %get-tuple-element.85.refs_1_, ...), custom_call_target="tpu_custom_call" | custom-call | tf_op jit(solution)/shard_map/ff_a/pallas_call | solution.py:448
  180.9 15.6 %shard_map.272 = (bf16[2,384,768]{2,1,0:T(8,128)(2,1)}, bf16[2,384,768]{2,1,0:T(8,128)(2,1)}, f32[2,3,384]{2,1,0:T(4,128)}, f32[2,3,16,128]{3,2,1,0:T(8,128)}, f32[640,768]{1,0:T(8,128)}) custom-call(bf16[512,768]{1,0:T(8,128)(2,1)} %get-tuple-element.72.refs_0_, bf16[32,768]{1,0:T(8,128)(2,1)} %get-tuple-element.73.refs_1_, ...), custom_call_target="tpu_custom_call" | custom-call | tf_op jit(solution)/shard_map/pallas_call | solution.py:372
  196.5 9.1 %shard_map.273 = (bf16[1,384,768]{2,1,0:T(8,128)(2,1)}, bf16[1,384,768]{2,1,0:T(8,128)(2,1)}, f32[1,3,384]{2,1,0:T(4,128)}, f32[1,3,16,128]{3,2,1,0:T(8,128)}, f32[640,768]{1,0:T(8,128)}) custom-call(bf16[512,768]{1,0:T(8,128)(2,1)} %get-tuple-element.72.refs_0_, bf16[32,768]{1,0:T(8,128)(2,1)} %get-tuple-element.73.refs_1_, ...), custom_call_target="tpu_custom_call" | custom-call | tf_op jit(solution)/shard_map/pallas_call | solution.py:372
  205.6 8.6 %shard_map.274 = (bf16[1,384,768]{2,1,0:T(8,128)(2,1)}, bf16[1,384,768]{2,1,0:T(8,128)(2,1)}, f32[1,3,384]{2,1,0:T(4,128)}, f32[1,3,16,128]{3,2,1,0:T(8,128)}, f...) custom-call(bf16[512,768]{1,0:T(8,128)(2,1)} %get-tuple-element.72.r, ...), custom_call_target="tpu_custom_call" | custom-call | tf_op jit(solution)/shard_map/pallas_call | solution.py:372
  214.3 3.5 collective-permute-start.43
  218.1 7.1 %collective-permute-done.41.r2 = bf16[32,768]{1,0:T(8,128)(2,1)S(1)} collective-permute-done((bf16[32,768]{1,0:T(8,128)(2,1)}, bf16[32,768]{1,0:T(8,128)(2,1)S(1)}, u32[]{:S(2)}, u32[]{:S(2)}) %collective-permute-start.41) | collective-permute-done | bytes 49184 | tf_op jit(solution)/shard_map/ppermute | solution.py:554
  227.5 7.4 %post.1 = (f32[256,768]{1,0:T(8,128)}, f32[24,768]{1,0:T(8,128)}) custom-call(s32[3]{0:T(128)} %pad_add_fusion.1.refs_18_.where_ref, f32[256,768]{1,0:T(8,128)} %get-tuple-element.99.own, f32[32,768]{1,0:T(8,128)} %get-tuple-element.100.f0, bf16[160,768]{1,0:T(8,128)(2,1)} %copy-done.29, bf16[32,768]{1,0:T(8,128)(2,1)} %copy-done.37, ...), custom_call_target="tpu_custom_call" | custom-call | tf_op jit(solution)/shard_map/post/pallas_call | solution.py:526
  239.6 2.7 collective-permute-done.45
  254.1 2.9 collective-permute-done.48
  265.7 11.7 %collective-permute-done.54 = bf16[2,96,768]{2,1,0:T(8,128)(2,1)S(1)} collective-permute-done((bf16[2,96,768]{2,1,0:T(8,128)(2,1)S(1)}, bf16[2,96,768]{2,1,0:T(8,128)(2,1)S(1)}, u32[]{:S(2)}, u32[]{:S(2)}) %collective-permute-start.54) | collective-permute-done | bytes 294944 | tf_op jit(solution)/shard_map/ppermute | solution.py:554
  280.9 4.2 %collective-permute-done.58 = bf16[2,96,768]{2,1,0:T(8,128)(2,1)S(1)} collective-permute-done((bf16[2,96,768]{2,1,0:T(8,128)(2,1)S(1)}, bf16[2,96,768]{2,1,0:T(8,128)(2,1)S(1)}, u32[]{:S(2)}, u32[]{:S(2)}) %collective-permute-start.58) | collective-permute-done | bytes 294944 | tf_op jit(solution)/shard_map/ppermute | solution.py:554
  287.0 5.4 %collective-permute-done.60 = bf16[2,96,768]{2,1,0:T(8,128)(2,1)S(1)} collective-permute-done((bf16[2,96,768]{2,1,0:T(8,128)(2,1)S(1)}, bf16[2,96,768]{2,1,0:T(8,128)(2,1)S(1)}, u32[]{:S(2)}, u32[]{:S(2)}) %collective-permute-start.60) | collective-permute-done | bytes 294944 | tf_op jit(solution)/shard_map/ppermute | solution.py:554
  297.0 7.9 %collective-permute-done.69 = bf16[2,96,1536]{2,1,0:T(8,128)(2,1)S(1)} collective-permute-done((bf16[2,96,1536]{2,1,0:T(8,128)(2,1)S(1)}, bf16[2,96,1536]{2,1,0:T(8,128)(2,1)S(1)}, u32[]{:S(2)}, u32[]{:S(2)}) %collective-permute-start.69) | collective-permute-done | bytes 589856 | tf_op jit(solution)/shard_map/ppermute | solution.py:554
  305.4 12.3 %collective-permute-done.71 = bf16[2,96,1536]{2,1,0:T(8,128)(2,1)S(1)} collective-permute-done((bf16[2,96,1536]{2,1,0:T(8,128)(2,1)S(1)}, bf16[2,96,1536]{2,1,0:T(8,128)(2,1)S(1)}, u32[]{:S(2)}, u32[]{:S(2)}) %collective-permute-start.71) | collective-permute-done | bytes 589856 | tf_op jit(solution)/shard_map/ppermute | solution.py:554
  320.1 10.1 %collective-permute-done.64 = bf16[2,96,1536]{2,1,0:T(8,128)(2,1)S(1)} collective-permute-done((bf16[2,96,1536]{2,1,0:T(8,128)(2,1)S(1)}, bf16[2,96,1536]{2,1,0:T(8,128)(2,1)S(1)}, u32[]{:S(2)}, u32[]{:S(2)}) %collective-permute-start.64) | collective-permute-done | bytes 589856 | tf_op jit(solution)/shard_map/ppermute | solution.py:554
  332.3 10.6 %collective-permute-done.66 = bf16[2,96,1536]{2,1,0:T(8,128)(2,1)S(1)} collective-permute-done((bf16[2,96,1536]{2,1,0:T(8,128)(2,1)S(1)}, bf16[2,96,1536]{2,1,0:T(8,128)(2,1)S(1)}, u32[]{:S(2)}, u32[]{:S(2)}) %collective-permute-start.66) | collective-permute-done | bytes 589856 | tf_op jit(solution)/shard_map/ppermute | solution.py:554
  352.5 11.6 %collective-permute-done.72 = bf16[96,1536]{1,0:T(8,128)(2,1)S(1)} collective-permute-done((bf16[96,1536]{1,0:T(8,128)(2,1)S(1)}, bf16[96,1536]{1,0:T(8,128)(2,1)S(1)}, u32[]{:S(2)}, u32[]{:S(2)}) %collective-permute-start.72) | collective-permute-done | bytes 294944 | tf_op jit(solution)/shard_map/ppermute | solution.py:554
  364.0 7.8 %collective-permute-done.73 = bf16[96,1536]{1,0:T(8,128)(2,1)S(1)} collective-permute-done((bf16[96,1536]{1,0:T(8,128)(2,1)S(1)}, bf16[96,1536]{1,0:T(8,128)(2,1)S(1)}, u32[]{:S(2)}, u32[]{:S(2)}) %collective-permute-start.73) | collective-permute-done | bytes 294944 | tf_op jit(solution)/shard_map/ppermute | solution.py:554
  (290 shorter events, 108.6 us)
Async XLA Ops:
  1.4 15.7 %collective-permute-start.4 = (bf16[3,1,96]{2,0,1:T(4,128)(2,1)S(1)}, bf16[3,1,96]{2,0,1:T(4,128)(2,1)S(1)}, u32[]{:S(2)}, u32[]{:S(2)}) collective-permute-start(bf16[3,1,96]{2,0,1:T(4,128)(2,1)S(1)} %get-tuple-element.161), channel_id=1, source_target_pairs={{0,24},{4,28},{8,16},{12,20},{16,8},{20,12},{24,0},{28,4},{1,25},{... | collective-permute-start | bytes 1736 | tf_op jit(solution)/shard_map/ppermute | solution.py:554
  3.9 18.5 %collective-permute-start.2 = (bf16[3,1,96]{2,0,1:T(4,128)(2,1)S(1)}, bf16[3,1,96]{2,0,1:T(4,128)(2,1)S(1)}, u32[]{:S(2)}, u32[]{:S(2)}) collective-permute-start(bf16[3,1,96]{2,0,1:T(4,128)(2,1)S(1)} %get-tuple-element.161), channel_id=1, source_target_pairs={{0,8},{4,12},{8,0},{12,4},{16,24},{20,28},{24,16},{28,20},{1,9},{5... | collective-permute-start | bytes 1736 | tf_op jit(solution)/shard_map/ppermute | solution.py:554
  6.2 33.3 %collective-permute-start.32 = (bf16[96,2304]{1,0:T(8,128)(2,1)}, bf16[96,2304]{1,0:T(8,128)(2,1)S(1)}, u32[]{:S(2)}, u32[]{:S(2)}) collective-permute-start(bf16[96,2304]{1,0:T(8,128)(2,1)} %pack.1.refs_5_.refs_2_.refs_6_), channel_id=1, source_target_pairs={{0,4},{4,0},{8,12},{12,8},{16,20},{20,16},{24,28},{28,24},{1,5},{5... | collective-permute-start | bytes 1327112 | tf_op jit(solution)/shard_map/ppermute | solution.py:554
  7.7 35.3 %collective-permute-start.31 = (bf16[96,2304]{1,0:T(8,128)(2,1)}, bf16[96,2304]{1,0:T(8,128)(2,1)S(1)}, u32[]{:S(2)}, u32[]{:S(2)}) collective-permute-start(bf16[96,2304]{1,0:T(8,128)(2,1)} %pack.1.refs_5_.refs_2_.refs_6_), channel_id=1, source_target_pairs={{0,24},{4,28},{8,16},{12,20},{16,8},{20,12},{24,0},{28,4},{1,25},{... | collective-permute-start | bytes 1327112 | tf_op jit(solution)/shard_map/ppermute | solution.py:554
  39.6 19.2 %collective-permute-start.17 = (bf16[96,2304]{1,0:T(8,128)(2,1)S(1)}, bf16[96,2304]{1,0:T(8,128)(2,1)S(1)}, u32[]{:S(2)}, u32[]{:S(2)}) collective-permute-start(bf16[96,2304]{1,0:T(8,128)(2,1)S(1)} %copy-done), channel_id=1, source_target_pairs={{0,3},{1,2},{2,1},{3,0},{4,7},{5,6},{6,5},{7,4},{8,11},{9,10},{10,... | collective-permute-start | bytes 1327112 | tf_op jit(solution)/shard_map/ppermute | solution.py:554
  43.0 32.1 %collective-permute-start.9 = (bf16[96,2304]{1,0:T(8,128)(2,1)S(1)}, bf16[96,2304]{1,0:T(8,128)(2,1)S(1)}, u32[]{:S(2)}, u32[]{:S(2)}) collective-permute-start(bf16[96,2304]{1,0:T(8,128)(2,1)S(1)} %copy-done), channel_id=1, source_target_pairs={{0,2},{1,3},{2,0},{3,1},{4,6},{5,7},{6,4},{7,5},{8,10},{9,11},{10,... | collective-permute-start | bytes 1327112 | tf_op jit(solution)/shard_map/ppermute | solution.py:554
  44.9 30.7 %collective-permute-start.35 = (bf16[96,2304]{1,0:T(8,128)(2,1)S(1)}, bf16[96,2304]{1,0:T(8,128)(2,1)S(1)}, u32[]{:S(2)}, u32[]{:S(2)}) collective-permute-start(bf16[96,2304]{1,0:T(8,128)(2,1)S(1)} %collective-permute-done.31.refs_8_.refs_5_.refs_9_), channel_id=1, source_target_pairs={{0,4},{4,0},{8,12},{12,8},{16,20},{20,16},{24,28},{28,24},{1,5},{5... | collective-permute-start | bytes 1327112 | tf_op jit(solution)/shard_map/ppermute | solution.py:554
  48.1 28.8 %collective-permute-start.34 = (bf16[96,2304]{1,0:T(8,128)(2,1)S(1)}, bf16[96,2304]{1,0:T(8,128)(2,1)S(1)}, u32[]{:S(2)}, u32[]{:S(2)}) collective-permute-start(bf16[96,2304]{1,0:T(8,128)(2,1)S(1)} %collective-permute-done.30.refs_7_.refs_4_.refs_8_), channel_id=1, source_target_pairs={{0,4},{4,0},{8,12},{12,8},{16,20},{20,16},{24,28},{28,24},{1,5},{5... | collective-permute-start | bytes 1327112 | tf_op jit(solution)/shard_map/ppermute | solution.py:554
  49.8 31.9 %collective-permute-start.33 = (bf16[96,2304]{1,0:T(8,128)(2,1)S(1)}, bf16[96,2304]{1,0:T(8,128)(2,1)S(1)}, u32[]{:S(2)}, u32[]{:S(2)}) collective-permute-start(bf16[96,2304]{1,0:T(8,128)(2,1)S(1)} %collective-permute-done.29.refs_6_.refs_3_.refs_7_), channel_id=1, source_target_pairs={{0,4},{4,0},{8,12},{12,8},{16,20},{20,16},{24,28},{28,24},{1,5},{5... | collective-permute-start | bytes 1327112 | tf_op jit(solution)/shard_map/ppermute | solution.py:554
  58.7 23.6 %collective-permute-start.28 = (bf16[96,2304]{1,0:T(8,128)(2,1)S(1)}, bf16[96,2304]{1,0:T(8,128)(2,1)S(1)}, u32[]{:S(2)}, u32[]{:S(2)}) collective-permute-start(bf16[96,2304]{1,0:T(8,128)(2,1)S(1)} %collective-permute-done.25.refs_13_.refs_10_.refs_6_), channel_id=1, source_target_pairs={{0,24},{4,28},{8,16},{12,20},{16,8},{20,12},{24,0},{28,4},{1,25},{... | collective-permute-start | bytes 1327112 | tf_op jit(solution)/shard_map/ppermute | solution.py:554
  76.9 25.7 %collective-permute-start.21 = (bf16[96,2304]{1,0:T(8,128)(2,1)S(1)}, bf16[96,2304]{1,0:T(8,128)(2,1)S(1)}, u32[]{:S(2)}, u32[]{:S(2)}) collective-permute-start(bf16[96,2304]{1,0:T(8,128)(2,1)S(1)} %collective-permute-done.17.refs_13_.refs_10_.refs_14_), channel_id=1, source_target_pairs={{0,4},{4,0},{8,12},{12,8},{16,20},{20,16},{24,28},{28,24},{1,5},{5... | collective-permute-start | bytes 1327112 | tf_op jit(solution)/shard_map/ppermute | solution.py:554
  81.7 22.3 %collective-permute-start.20 = (bf16[96,2304]{1,0:T(8,128)(2,1)S(1)}, bf16[96,2304]{1,0:T(8,128)(2,1)S(1)}, u32[]{:S(2)}, u32[]{:S(2)}) collective-permute-start(bf16[96,2304]{1,0:T(8,128)(2,1)S(1)} %collective-permute-done.17.refs_13_.refs_10_.refs_14_), channel_id=1, source_target_pairs={{0,24},{4,28},{8,16},{12,20},{16,8},{20,12},{24,0},{28,4},{1,25},{... | collective-permute-start | bytes 1327112 | tf_op jit(solution)/shard_map/ppermute | solution.py:554
  82.3 27.2 %collective-permute-start.19 = (bf16[96,2304]{1,0:T(8,128)(2,1)S(1)}, bf16[96,2304]{1,0:T(8,128)(2,1)S(1)}, u32[]{:S(2)}, u32[]{:S(2)}) collective-permute-start(bf16[96,2304]{1,0:T(8,128)(2,1)S(1)} %collective-permute-done.17.refs_13_.refs_10_.refs_14_), channel_id=1, source_target_pairs={{0,16},{4,20},{8,24},{12,28},{16,0},{20,4},{24,8},{28,12},{1,17},{... | collective-permute-start | bytes 1327112 | tf_op jit(solution)/shard_map/ppermute | solution.py:554
  90.4 26.8 %collective-permute-start.18 = (bf16[96,2304]{1,0:T(8,128)(2,1)S(1)}, bf16[96,2304]{1,0:T(8,128)(2,1)}, u32[]{:S(2)}, u32[]{:S(2)}) collective-permute-start(bf16[96,2304]{1,0:T(8,128)(2,1)S(1)} %collective-permute-done.17.refs_13_.refs_10_.refs_14_), channel_id=1, source_target_pairs={{0,8},{4,12},{8,0},{12,4},{16,24},{20,28},{24,16},{28,20},{1,9},{5... | collective-permute-start | bytes 1327112 | tf_op jit(solution)/shard_map/ppermute | solution.py:554
  90.5 38.7 %collective-permute-start.13 = (bf16[96,2304]{1,0:T(8,128)(2,1)S(1)}, bf16[96,2304]{1,0:T(8,128)(2,1)}, u32[]{:S(2)}, u32[]{:S(2)}) collective-permute-start(bf16[96,2304]{1,0:T(8,128)(2,1)S(1)} %collective-permute-done.9.refs_5_.refs_2_.refs_6_), channel_id=1, source_target_pairs={{0,4},{4,0},{8,12},{12,8},{16,20},{20,16},{24,28},{28,24},{1,5},{5... | collective-permute-start | bytes 1327112 | tf_op jit(solution)/shard_map/ppermute | solution.py:554
  102.6 26.6 %collective-permute-start.12 = (bf16[96,2304]{1,0:T(8,128)(2,1)S(1)}, bf16[96,2304]{1,0:T(8,128)(2,1)}, u32[]{:S(2)}, u32[]{:S(2)}) collective-permute-start(bf16[96,2304]{1,0:T(8,128)(2,1)S(1)} %collective-permute-done.9.refs_5_.refs_2_.refs_6_), channel_id=1, source_target_pairs={{0,24},{4,28},{8,16},{12,20},{16,8},{20,12},{24,0},{28,4},{1,25},{... | collective-permute-start | bytes 1327112 | tf_op jit(solution)/shard_map/ppermute | solution.py:554
  103.9 25.7 %collective-permute-start.11 = (bf16[96,2304]{1,0:T(8,128)(2,1)S(1)}, bf16[96,2304]{1,0:T(8,128)(2,1)}, u32[]{:S(2)}, u32[]{:S(2)}) collective-permute-start(bf16[96,2304]{1,0:T(8,128)(2,1)S(1)} %collective-permute-done.9.refs_5_.refs_2_.refs_6_), channel_id=1, source_target_pairs={{0,16},{4,20},{8,24},{12,28},{16,0},{20,4},{24,8},{28,12},{1,17},{... | collective-permute-start | bytes 1327112 | tf_op jit(solution)/shard_map/ppermute | solution.py:554
  109.5 21.0 %collective-permute-start.10 = (bf16[96,2304]{1,0:T(8,128)(2,1)S(1)}, bf16[96,2304]{1,0:T(8,128)(2,1)}, u32[]{:S(2)}, u32[]{:S(2)}) collective-permute-start(bf16[96,2304]{1,0:T(8,128)(2,1)S(1)} %collective-permute-done.9.refs_5_.refs_2_.refs_6_), channel_id=1, source_target_pairs={{0,8},{4,12},{8,0},{12,4},{16,24},{20,28},{24,16},{28,20},{1,9},{5... | collective-permute-start | bytes 1327112 | tf_op jit(solution)/shard_map/ppermute | solution.py:554
  237.5 22.2 %collective-permute-start.51 = (bf16[1,384,768]{2,1,0:T(8,128)(2,1)}, bf16[1,384,768]{2,1,0:T(8,128)(2,1)}, u32[]{:S(2)}, u32[]{:S(2)}) collective-permute-start(bf16[1,384,768]{2,1,0:T(8,128)(2,1)} %get-tuple-element.117), channel_id=1, source_target_pairs={{0,4},{4,0},{8,12},{12,8},{16,20},{20,16},{24,28},{28,24},{1,5},{5... | collective-permute-start | bytes 1769480 | tf_op jit(solution)/shard_map/ppermute | solution.py:554
  248.5 44.0 %collective-permute-start.68 = (bf16[2,384,1536]{2,1,0:T(8,128)(2,1)}, bf16[2,384,1536]{2,1,0:T(8,128)(2,1)S(1)}, u32[]{:S(2)}, u32[]{:S(2)}) collective-permute-start(bf16[2,384,1536]{2,1,0:T(8,128)(2,1)} %get-tuple-element.129), channel_id=1, source_target_pairs={{0,4},{4,0},{8,12},{12,8},{16,20},{20,16},{24,28},{28,24},{1,5},{5... | collective-permute-start | bytes 7077896 | tf_op jit(solution)/shard_map/ppermute | solution.py:554
  257.0 38.8 %collective-permute-start.63 = (bf16[2,384,1536]{2,1,0:T(8,128)(2,1)}, bf16[2,384,1536]{2,1,0:T(8,128)(2,1)S(1)}, u32[]{:S(2)}, u32[]{:S(2)}) collective-permute-start(bf16[2,384,1536]{2,1,0:T(8,128)(2,1)} %get-tuple-element.127), channel_id=1, source_target_pairs={{0,4},{4,0},{8,12},{12,8},{16,20},{20,16},{24,28},{28,24},{1,5},{5... | collective-permute-start | bytes 7077896 | tf_op jit(solution)/shard_map/ppermute | solution.py:554
  285.1 61.2 %collective-permute-start.56 = (bf16[96,768]{1,0:T(8,128)(2,1)S(1)}, bf16[96,768]{1,0:T(8,128)(2,1)S(1)}, u32[]{:S(2)}, u32[]{:S(2)}) collective-permute-start(bf16[96,768]{1,0:T(8,128)(2,1)S(1)} %get-tuple-element.188), channel_id=1, source_target_pairs={{0,1},{1,0},{2,3},{3,2},{4,5},{5,4},{6,7},{7,6},{8,9},{9,8},{10,11... | collective-permute-start | bytes 442376 | tf_op jit(solution)/shard_map/ppermute | solution.py:554
  293.6 24.0 %collective-permute-start.71 = (bf16[2,96,1536]{2,1,0:T(8,128)(2,1)S(1)}, bf16[2,96,1536]{2,1,0:T(8,128)(2,1)S(1)}, u32[]{:S(2)}, u32[]{:S(2)}) collective-permute-start(bf16[2,96,1536]{2,1,0:T(8,128)(2,1)S(1)} %get-tuple-element.166), channel_id=1, source_target_pairs={{0,24},{4,28},{8,16},{12,20},{16,8},{20,12},{24,0},{28,4},{1,25},{... | collective-permute-start | bytes 1769480 | tf_op jit(solution)/shard_map/ppermute | solution.py:554
  294.7 24.3 %collective-permute-start.70 = (bf16[2,96,1536]{2,1,0:T(8,128)(2,1)S(1)}, bf16[2,96,1536]{2,1,0:T(8,128)(2,1)S(1)}, u32[]{:S(2)}, u32[]{:S(2)}) collective-permute-start(bf16[2,96,1536]{2,1,0:T(8,128)(2,1)S(1)} %get-tuple-element.167), channel_id=1, source_target_pairs={{0,16},{4,20},{8,24},{12,28},{16,0},{20,4},{24,8},{28,12},{1,17},{... | collective-permute-start | bytes 1769480 | tf_op jit(solution)/shard_map/ppermute | solution.py:554
  295.8 52.4 %collective-permute-start.62 = (bf16[96,768]{1,0:T(8,128)(2,1)S(1)}, bf16[96,768]{1,0:T(8,128)(2,1)S(1)}, u32[]{:S(2)}, u32[]{:S(2)}) collective-permute-start(bf16[96,768]{1,0:T(8,128)(2,1)S(1)} %get-tuple-element.186), channel_id=1, source_target_pairs={{0,3},{1,2},{2,1},{3,0},{4,7},{5,6},{6,5},{7,4},{8,11},{9,10},{10,... | collective-permute-start | bytes 442376 | tf_op jit(solution)/shard_map/ppermute | solution.py:554
  304.9 25.3 %collective-permute-start.64 = (bf16[2,96,1536]{2,1,0:T(8,128)(2,1)S(1)}, bf16[2,96,1536]{2,1,0:T(8,128)(2,1)S(1)}, u32[]{:S(2)}, u32[]{:S(2)}) collective-permute-start(bf16[2,96,1536]{2,1,0:T(8,128)(2,1)S(1)} %get-tuple-element.162), channel_id=1, source_target_pairs={{0,8},{4,12},{8,0},{12,4},{16,24},{20,28},{24,16},{28,20},{1,9},{5... | collective-permute-start | bytes 1769480 | tf_op jit(solution)/shard_map/ppermute | solution.py:554
  317.6 25.3 %collective-permute-start.66 = (bf16[2,96,1536]{2,1,0:T(8,128)(2,1)S(1)}, bf16[2,96,1536]{2,1,0:T(8,128)(2,1)S(1)}, u32[]{:S(2)}, u32[]{:S(2)}) collective-permute-start(bf16[2,96,1536]{2,1,0:T(8,128)(2,1)S(1)} %get-tuple-element.163), channel_id=1, source_target_pairs={{0,24},{4,28},{8,16},{12,20},{16,8},{20,12},{24,0},{28,4},{1,25},{... | collective-permute-start | bytes 1769480 | tf_op jit(solution)/shard_map/ppermute | solution.py:554
  319.0 26.2 %collective-permute-start.65 = (bf16[2,96,1536]{2,1,0:T(8,128)(2,1)S(1)}, bf16[2,96,1536]{2,1,0:T(8,128)(2,1)S(1)}, u32[]{:S(2)}, u32[]{:S(2)}) collective-permute-start(bf16[2,96,1536]{2,1,0:T(8,128)(2,1)S(1)} %get-tuple-element.164), channel_id=1, source_target_pairs={{0,16},{4,20},{8,24},{12,28},{16,0},{20,4},{24,8},{28,12},{1,17},{... | collective-permute-start | bytes 1769480 | tf_op jit(solution)/shard_map/ppermute | solution.py:554
  330.2 18.0 %collective-permute-start.61 = (bf16[96,768]{1,0:T(8,128)(2,1)S(1)}, bf16[96,768]{1,0:T(8,128)(2,1)S(1)}, u32[]{:S(2)}, u32[]{:S(2)}) collective-permute-start(bf16[96,768]{1,0:T(8,128)(2,1)S(1)} %get-tuple-element.187), channel_id=1, source_target_pairs={{0,2},{1,3},{2,0},{3,1},{4,6},{5,7},{6,4},{7,5},{8,10},{9,11},{10,... | collective-permute-start | bytes 442376 | tf_op jit(solution)/shard_map/ppermute | solution.py:554
  343.0 21.1 %collective-permute-start.72 = (bf16[96,1536]{1,0:T(8,128)(2,1)S(1)}, bf16[96,1536]{1,0:T(8,128)(2,1)S(1)}, u32[]{:S(2)}, u32[]{:S(2)}) collective-permute-start(bf16[96,1536]{1,0:T(8,128)(2,1)S(1)} %get-tuple-element.182), channel_id=1, source_target_pairs={{0,2},{1,3},{2,0},{3,1},{4,6},{5,7},{6,4},{7,5},{8,10},{9,11},{10,... | collective-permute-start | bytes 884744 | tf_op jit(solution)/shard_map/ppermute | solution.py:554
  345.2 26.6 %collective-permute-start.73 = (bf16[96,1536]{1,0:T(8,128)(2,1)S(1)}, bf16[96,1536]{1,0:T(8,128)(2,1)S(1)}, u32[]{:S(2)}, u32[]{:S(2)}) collective-permute-start(bf16[96,1536]{1,0:T(8,128)(2,1)S(1)} %get-tuple-element.183), channel_id=1, source_target_pairs={{0,3},{1,2},{2,1},{3,0},{4,7},{5,6},{6,5},{7,4},{8,11},{9,10},{10,... | collective-permute-start | bytes 884744 | tf_op jit(solution)/shard_map/ppermute | solution.py:554
  346.4 25.4 %collective-permute-start.67 = (bf16[96,1536]{1,0:T(8,128)(2,1)S(1)}, bf16[96,1536]{1,0:T(8,128)(2,1)S(1)}, u32[]{:S(2)}, u32[]{:S(2)}) collective-permute-start(bf16[96,1536]{1,0:T(8,128)(2,1)S(1)} %slice_bitcast_fusion.2), channel_id=1, source_target_pairs={{0,1},{1,0},{2,3},{3,2},{4,5},{5,4},{6,7},{7,6},{8,9},{9,8},{10,11... | collective-permute-start | bytes 884744 | tf_op jit(solution)/shard_map/ppermute | solution.py:554
  (82 other events, 1115.1 us)

commit v2 on v1

--- a/solution.py
+++ b/solution.py
@@ -86,16 +86,13 @@
     )(*shards)
 
 
-def prep_kernel(left, tok, right, grad, order, gains, mem, tables, x, tokp, gop, pooled_ref, far):
+def prep_kernel(tok, grad, order, gains, mem, tables, x, tokp, gop, pooled_ref, far):
     turn = order[...]
-    gain = gains[0:1]
-    for base, ref in ((0, left), (BLOCK, tok), (BLOCK + ROWS, right)):
-        v = dot(ref[...], turn)
-        x[base : base + ref.shape[0]] = (v * rsqrt_mean(v) * gain).astype(bf16)
-        if ref is tok:
-            tokp[...] = v.astype(bf16)
+    v = dot(tok[...], turn)
+    x[...] = (v * rsqrt_mean(v) * gains[0:1]).astype(bf16)
+    tokp[...] = v.astype(bf16)
     gop[...] = dot(grad[...], turn).astype(bf16)
-    pooled = dot(mem[...], x[BLOCK : BLOCK + ROWS])
+    pooled = dot(mem[...], x[...])
     pooled_ref[...] = pooled
     rows = (pooled * rsqrt_mean(pooled) * gains[2:3]).astype(bf16)
     at = lax.broadcasted_iota(jnp.int32, rows.shape, 0)
@@ -106,7 +103,7 @@
     return pl.pallas_call(
         prep_kernel,
         out_shape=[
-            shape_of((EXT, D), bf16),
+            shape_of((ROWS, D), bf16),
             shape_of((ROWS, D), bf16),
             shape_of((ROWS, D), bf16),
             shape_of((FAR, D), f32),
@@ -116,13 +113,29 @@
     )(*args)
 
 
+def edge_kernel(left, right, order, gains, edge):
+    for n, ref in enumerate((left, right)):
+        v = dot(ref[...], order[...])
+        edge[n * BLOCK : n * BLOCK + BLOCK] = (v * rsqrt_mean(v) * gains[0:1]).astype(bf16)
+
+
+def edge_rows(*args):
+    return pl.pallas_call(edge_kernel, out_shape=shape_of((2 * BLOCK, D), bf16), name="edge")(*args)
+
+
 def join(w_s, pieces, step):
     for n in range(len(pieces) // 8):
 
         @pl.when(step == n)
         def _(n=n):
-            for k in range(8):
-                w_s[k * 96 : k * 96 + 96, :] = pieces[8 * n + k][...]
+            def rows(i, carry):
+                for k in range(8):
+                    w_s[pl.ds(pl.multiple_of(k * 96 + i * 16, 16), 16), :] = pieces[8 * n + k][
+                        pl.ds(pl.multiple_of(i * 16, 16), 16), :
+                    ]
+                return carry
+
+            lax.fori_loop(0, 6, rows, 0)
 
 
 attn_spec = pl.BlockSpec((96, D), lambda i: (0, 2))
@@ -134,7 +147,10 @@
 
 
 def fill_x(x_s, x, fars):
-    x_s[0:EXT] = x[...]
+    own, edge = x
+    x_s[0:BLOCK] = edge[0:BLOCK]
+    x_s[BLOCK : BLOCK + ROWS] = own[...]
+    x_s[BLOCK + ROWS : EXT] = edge[BLOCK:]
     for n, ref in enumerate(fars):
         x_s[EXT + n * FAR : EXT + n * FAR + FAR] = ref[...]
 
@@ -150,10 +166,10 @@
 
 
 def attn_fwd_kernel(base, last, *refs):
-    x, f0, f1, f2, f3 = refs[:5]
-    pieces = refs[5:21]
-    near_at, far_at, tables, mask = refs[21:25]
-    refs = refs[25:]
+    x, f0, f1, f2, f3 = (refs[:2],) + refs[2:6]
+    pieces = refs[6:22]
+    near_at, far_at, tables, mask = refs[22:26]
+    refs = refs[26:]
     if last:
         before, tok, gains = refs[:3]
         refs = refs[3:]
@@ -217,7 +233,7 @@
             nf[...] = (v * rsqrt_mean(v) * gains[1:2]).astype(bf16)
 
 
-x_specs = [whole_spec((EXT, D))] + [whole_spec((FAR, D))] * 4
+x_specs = [whole_spec((ROWS, D)), whole_spec((2 * BLOCK, D))] + [whole_spec((FAR, D))] * 4
 
 
 def attn_fwd(base, x, fars, pieces, near_at, far_at, tables, mask, *rest):
@@ -249,13 +265,13 @@
         scratch_shapes=([pltpu.VMEM((ROWS, D), f32)] if last else [])
         + [pltpu.VMEM((ALL, D), bf16), pltpu.VMEM((D, D), bf16)],
         name="attn_fwd_b" if last else "attn_fwd_a",
-    )(x, *fars, *pieces, near_at, far_at, tables, mask, *rest)
+    )(*x, *fars, *pieces, near_at, far_at, tables, mask, *rest)
 
 
 def attn_bwd_kernel(slabs, more, last, *refs):
-    x, f0, f1, f2, f3, rl = refs[:6]
-    pieces = refs[6 : 6 + 8 * slabs]
-    refs = refs[6 + 8 * slabs :]
+    x, f0, f1, f2, f3, rl = (refs[:2],) + refs[2:7]
+    pieces = refs[7 : 7 + 8 * slabs]
+    refs = refs[7 + 8 * slabs :]
     r_ref, p_ref, a_ref = refs[:3]
     refs = refs[3:]
     if more:
@@ -382,7 +398,7 @@
         out_shape=[o[1] for o in outs],
         scratch_shapes=([pltpu.VMEM((ALL, D), f32)] if last else [])
         + [pltpu.VMEM((ALL, D), bf16), pltpu.VMEM((D, D), bf16), pltpu.VMEM((ALL, 640), f32)],
-    )(x, *fars, rl, *pieces, r, p, a, *rest)
+    )(*x, *fars, rl, *pieces, r, p, a, *rest)
 
 
 def ff_kernel(last, *refs):
@@ -501,21 +517,21 @@
     far_hot = [
         (jnp.broadcast_to(far_at[a : a + 1], (BUCKETS, 128)) == bucket[:, 0:128]).astype(bf16) for a in range(16)
     ]
-    at = lax.broadcasted_iota(jnp.int32, (16, 3), 0)
-    col = lax.broadcasted_iota(jnp.int32, (16, 3), 1)
-    near_of = (near_0[0], near_1[0], near_b[0], near_b[1])
-    far_of = ((far_0, 0), (far_1, 0), (far_b, 0), (far_b, 1))
-    near_sum = jnp.zeros((16, BUCKETS), f32)
-    far_sum = jnp.zeros((16, BUCKETS), f32)
+    near_grad = jnp.concatenate([near_0[0], near_1[0], near_b[0], near_b[1]], axis=0)
+    far_of = [far_0.at[0], far_1.at[0], far_b.at[0], far_b.at[1]]
+    near_table = sum(dot_nt(part, near_hot) for part in split3(near_grad))
+    far_table = jnp.zeros((HEADS, BUCKETS), f32)
+    for a in range(16):
+        far_grad = jnp.concatenate([ref[:, a] for ref in far_of], axis=0)
+        far_table = far_table + sum(dot_nt(part, far_hot[a]) for part in split3(far_grad))
+    at = lax.broadcasted_iota(jnp.int32, (16, HEADS), 0)
+    col = lax.broadcasted_iota(jnp.int32, (16, HEADS), 1)
+    place = jnp.zeros((16, HEADS), f32)
     for k in range(4):
-        place = (at == col + 3 * (where_ref[2] ^ k)).astype(bf16)
-        near_table = sum(dot_nt(part, near_hot) for part in split3(near_of[k]))
-        far_table = jnp.zeros((3, BUCKETS), f32)
-        for a in range(16):
-            far_grad = far_of[k][0][far_of[k][1], :, a]
-            far_table = far_table + sum(dot_nt(part, far_hot[a]) for part in split3(far_grad))
-        near_sum = near_sum + sum(dot(place, part) for part in split3(near_table))
-        far_sum = far_sum + sum(dot(place, part) for part in split3(far_table))
+        place = jnp.where((col // 3 == k) & (at == col % 3 + 3 * (where_ref[2] ^ k)), 1.0, place)
+    place = place.astype(bf16)
+    near_sum = sum(dot(place, part) for part in split3(near_table))
+    far_sum = sum(dot(place, part) for part in split3(far_table))
     small[8:24] = jnp.zeros((16, D), f32)
     small[8:24, 0:BUCKETS] = near_sum
     small[8:24, 128 : 128 + BUCKETS] = far_sum
@@ -539,14 +555,19 @@
     q[:, 128:192] = wide[:, 384:448]
     v[:, 128:192] = wide[:, 448:512]
     k[:, 128:192] = wide[:, 512:576]
-    o[:, 128:192] = wide[:, 576:640]
-    o[:, 0:128] = wide[:, 640:768]
+    out = jnp.concatenate([wide[:, 640:768], wide[:, 576:640]], axis=1)
+    o[...] = out.T if o.shape[0] == 192 else out
 
 
 def unpack(*slabs):
-    return pl.pallas_call(
-        unpack_kernel, out_shape=[shape_of((slabs[0].shape[0], 192), f32)] * 4, name="unpack"
+    rows = slabs[0].shape[0]
+    turn = rows % 32 == 0
+    q, k, v, o = pl.pallas_call(
+        unpack_kernel,
+        out_shape=[shape_of((rows, 192), f32)] * 3 + [shape_of((192, rows) if turn else (rows, 192), f32)],
+        name="unpack",
     )(*slabs)
+    return q, k, v, o if turn else o.T
 
 
 def swap(x, axis, mask):
@@ -578,7 +599,7 @@
     return got
 
 
-def scatter_pair(sources):
+def scatter_pair(sources, behind=None):
     dtype = sources[0][0].dtype
     came = []
     for _, oth in sources:
@@ -591,13 +612,18 @@
         )
 
     total = piece(0)
+    sends = [piece(n).astype(dtype) for n in (1, 2, 3)]
+    came = []
     for n in (1, 2, 3):
-        total = total + swap(piece(n).astype(dtype), "fsdp", n << 1).astype(f32)
+        came.append(swap(sends[n - 1], "fsdp", n << 1))
+    if behind is not None:
+        came, _ = lax.optimization_barrier((came, behind))
+    total = total + came[0].astype(f32) + came[1].astype(f32) + came[2].astype(f32)
     total = total.astype(dtype)
     for bit in high_bits()[::-1]:
         half = total.shape[1] // 2
         total = total[:, :half] + swap(total[:, half:], "fsdp", 1 << bit)
-    return total
+    return total, sends
 
 
 def scatter_tensor(slabs):
@@ -633,14 +659,17 @@
     tables = jnp.concatenate([table_local.T.reshape(1, -1), table_global.T.reshape(1, -1)], axis=1)
     tables = jnp.pad(tables, ((0, 0), (0, D - tables.shape[1])))
 
+    seg_row, near_hot, tables, gains, f_late = lax.optimization_barrier(
+        (segment[0], local_onehot[0], tables, gains, f)
+    )
+
     true_at = jnp.arange(D, dtype=jnp.int32)
     piece = true_at // 96
     high = (true_at % 96) // width
     relative = (piece // 4) | ((piece & 3) << 1) | (high << 3)
-    source = (f ^ relative) * width + true_at % width
+    source = (f_late ^ relative) * width + true_at % width
     order = (true_at[:, None] == source[None, :]).astype(bf16)
 
-    seg_row = segment[0]
     parts = seg_row.reshape(4, ROWS)
     rel = jnp.arange(4, dtype=jnp.int32) ^ z
     seg_rel = jnp.take(parts, rel, axis=0)
@@ -650,13 +679,15 @@
     )
     triangle = (here[:, None] <= here[None, :]).astype(bf16)
     piece_rel = dot(starts.astype(bf16), triangle).astype(jnp.int32) - 1
+    member = (piece_rel[0] == jnp.arange(FAR, dtype=jnp.int32)[:, None]).astype(bf16)
+    own_hot = lax.dynamic_slice(global_onehot, (z * 16, 0, 0), (16, SLOTS, BUCKETS))
     is_in = piece_rel[:, None, :] == jnp.arange(FAR, dtype=jnp.int32)[:, None]
     slot_rel = rel[:, None] * (ROWS // GBLOCK) + here[None] // GBLOCK
     piece_doc = jnp.max(jnp.where(is_in, seg_rel[:, None, :], -1), axis=2).reshape(4 * FAR)
     piece_slot = jnp.max(jnp.where(is_in, slot_rel[:, None, :], -1), axis=2).reshape(4 * FAR)
-    member = is_in[0].astype(bf16)
-
-    x, tok, go, pooled, far_rows = prep(left, tokens, right, grad_out, order, gains, member, tables)
+
+    x_own, tok, go, pooled, far_rows = prep(tokens, grad_out, order, gains, member, tables)
+    x = (x_own, edge_rows(left, right, order, gains))
     fars = [far_rows] + gather_tensor(far_rows)
 
     tables = jnp.stack([far[FAR - 1, : 6 * BUCKETS] for far in fars])
@@ -671,8 +702,7 @@
     far_ok = seg_own[:, :, None] == piece_doc[None, None, :]
     mask = jnp.where(jnp.concatenate([near_ok, far_ok], axis=2), 0.0, masked_score).astype(f32)
     bucket = jnp.arange(BUCKETS, dtype=jnp.int32)
-    near_at = jnp.sum(local_onehot[0] * bucket, axis=1)[None]
-    own_hot = lax.dynamic_slice(global_onehot, (z * 16, 0, 0), (16, SLOTS, BUCKETS))
+    near_at = jnp.sum(near_hot * bucket, axis=1)[None]
     slot_at = jnp.sum(own_hot * bucket, axis=2)
     slot_is = piece_slot[None, :] == jnp.arange(SLOTS, dtype=jnp.int32)[:, None]
     far_at = dot(slot_at.astype(bf16), slot_is.astype(bf16)).astype(jnp.int32)
@@ -695,14 +725,16 @@
     fo_a, ft_a, output, res_grad, rl, gain_ff = ff_both(
         nf, go, pair_a, out_b, ng_b, residual, gains, order
     )
-    sum_fb = scatter_pair([(fo_b, ft_b)])
-    sum_fa = scatter_pair([(fo_a, ft_a)])
+    sum_fb, _ = scatter_pair([(fo_b, ft_b)])
+    sum_fa, _ = scatter_pair([(fo_a, ft_a)])
     where = jnp.stack([z & 1, ((z == 1) | (z == 2)).astype(jnp.int32), z]).astype(jnp.int32)
     do_b, dt_b, nb_b, fb_b, xg = attn_bwd(x, fars, rl, pair_b, 0, r_b, p_b, at_b)
     do_1, dt_1, nb_1, fb_1, xg = attn_bwd(x, fars, rl, whole[1], 1, r_a, p_a, at_a, xg)
-    do_0, dt_0, nb_0, fb_0, own, f0, s1, s2, s3, s4 = attn_bwd(x, fars, rl, whole[0], 0, r_a, p_a, at_a, xg, where)
-    sum_ab = scatter_pair([(do_b, dt_b)])
-    sum_aa = scatter_pair([(do_0, dt_0), (do_1, dt_1)])
+    do_0, dt_0, nb_0, fb_0, own, f0, s1, s2, s3, s4 = attn_bwd(
+        x, fars, rl, whole[0], 0, r_a, p_a, at_a, xg, where
+    )
+    sum_aa, sends = scatter_pair([(do_0, dt_0), (do_1, dt_1)])
+    sum_ab, _ = scatter_pair([(do_b, dt_b)], sends)
     got = []
     for k, sent in ((1, s1), (2, s2), (3, s3)):
         got.append(swap(sent, "tensor", k))
@@ -723,7 +755,9 @@
 
     parts = scatter_tensor([sum_fa[0], sum_fa[1], sum_fb[0], sum_fb[1]])
     ff_sum = sum(part.astype(f32) for part in parts)
-    grad_query, grad_key, grad_value, grad_out_t = unpack(*scatter_tensor([sum_aa[0], sum_aa[1], sum_ab[0], sum_ab[1]]))
+    grad_query, grad_key, grad_value, grad_w_out = unpack(
+        *scatter_tensor([sum_aa[0], sum_aa[1], sum_ab[0], sum_ab[1]])
+    )
     return (
         output,
         grad_tokens,
@@ -733,7 +767,7 @@
         grad_query,
         grad_key,
         grad_value,
-        grad_out_t.T,
+        grad_w_out,
         ff_sum[:, 0:FFS],
         ff_sum[:, FFS : 2 * FFS],
         ff_sum[:, 2 * FFS : 3 * FFS].T,

time: 379 us -> 390 us (1.029)
  the two profiles are of different devices: /device:TPU:9 before, /device:TPU:0 now
where the time goes in v2:
time: 390 us; the launch traced here: 383 us
  waiting for transfers between devices  160 us (41%)
  Pallas kernels  97.4 us (25%)
  starting transfers between devices  80.2 us (21%)
  local copies, waits for them, and re-layouts  21.4 us (5%)
  other arithmetic  20.9 us (5%)
    ppermute x71, waiting for transfers between devices, swap(): return lax.ppermute(x, axis, [(i, i ^ mask) for i in range(size)])  160 us
    ppermute x71, starting transfers between devices, swap(): return lax.ppermute(x, axis, [(i, i ^ mask) for i in range(size)])  73.4 us
    pallas_call x3, Pallas kernels, attn_bwd(): pl.pallas_call(lambda *refs: attn_bwd_kernel(slabs, more, last, *refs), g...  33.6 us
    pallas_call x2, Pallas kernels, attn_fwd(): pl.pallas_call(lambda *refs: attn_fwd_kernel(base, last, *refs), grid=(2,...  25 us
    pallas_call x2, Pallas kernels, ff_both(): pl.pallas_call(lambda *refs: ff_kernel(last, *refs), grid=(2,), in_specs=...  22.4 us
  transfers between devices with their start and end apart: 74, of which 31 were waited for; matrix products, arithmetic and copies ran while one was open for 10% of the time, Pallas kernels for 6%

profile of v2, /device:TPU:0, one launch (start us, length us, event | category | flops | bytes accessed | tf_op | source)
XLA Modules:
  0.0 382.6 jit_solution(10530132997118279155)
XLA Ops:
  1.4 4.0 %collective-permute-start.2 = (bf16[3,1,96]{2,0,1:T(4,128)(2,1)S(1)}, bf16[3,1,96]{2,0,1:T(4,128)(2,1)S(1)}, u32[]{:S(2)}, u32[]{:S(2)}) collective-permute-start(bf16[3,1,96]{2,0,1:T(4,128)(2,1)S(1)} %get-tuple-element.149), channel_id=1, source_target_pairs={{0,24},{4,28},{8,16},{12,20},{16,8},{20,12},{24,0},{28,4},{1,25},{... | collective-permute-start | bytes 1736 | tf_op jit(solution)/shard_map/ppermute | solution.py:575
  8.3 4.6 %collective-permute-start.4 = (bf16[128,768]{1,0:T(8,128)(2,1)S(1)}, bf16[128,768]{1,0:T(8,128)(2,1)S(1)}, u32[]{:S(2)}, u32[]{:S(2)}) collective-permute-start(bf16[128,768]{1,0:T(8,128)(2,1)S(1)} %get-tuple-element.173), channel_id=1, source_target_pairs={{0,1},{1,2},{2,3},{4,5},{5,6},{6,7},{8,9},{9,10},{10,11},{12,13},{... | collective-permute-start | bytes 589832 | tf_op jit(solution)/shard_map/ppermute | solution.py:654
  24.9 3.2 prep.1
  39.0 3.0 collective-permute-start.31
  48.6 4.5 %collective-permute-done.31.refs_9_.refs_5_.refs_10_ = bf16[96,2304]{1,0:T(8,128)(2,1)S(1)} collective-permute-done((bf16[96,2304]{1,0:T(8,128)(2,1)S(1)}, bf16[96,2304]{1,0:T(8,128)(2,1)S(1)}, u32[]{:S(2)}, u32[]{:S(2)}) %collective-permute-start.31) | collective-permute-done | bytes 442400 | tf_op jit(solution)/shard_map/ppermute | solution.py:575
  54.9 5.8 %collective-permute-done.30.refs_8_.refs_4_.refs_9_ = bf16[96,2304]{1,0:T(8,128)(2,1)S(1)} collective-permute-done((bf16[96,2304]{1,0:T(8,128)(2,1)S(1)}, bf16[96,2304]{1,0:T(8,128)(2,1)S(1)}, u32[]{:S(2)}, u32[]{:S(2)}) %collective-permute-start.30) | collective-permute-done | bytes 442400 | tf_op jit(solution)/shard_map/ppermute | solution.py:575
  61.3 6.0 %collective-permute-done.17.refs_14_.refs_10_.refs_15_ = bf16[96,2304]{1,0:T(8,128)(2,1)S(1)} collective-permute-done((bf16[96,2304]{1,0:T(8,128)(2,1)S(1)}, bf16[96,2304]{1,0:T(8,128)(2,1)S(1)}, u32[]{:S(2)}, u32[]{:S(2)}) %collective-permute-start.17) | collective-permute-done | bytes 442400 | tf_op jit(solution)/shard_map/ppermute | solution.py:575
  74.5 9.1 %collective-permute-done.9.refs_6_.refs_2_.refs_7_ = bf16[96,2304]{1,0:T(8,128)(2,1)} collective-permute-done((bf16[96,2304]{1,0:T(8,128)(2,1)S(1)}, bf16[96,2304]{1,0:T(8,128)(2,1)}, u32[]{:S(2)}, u32[]{:S(2)}) %collective-permute-start.9) | collective-permute-done | bytes 442400 | tf_op jit(solution)/shard_map/ppermute | solution.py:575
  90.4 13.4 %collective-permute-done.27.refs_16_.refs_12_.refs_9_ = bf16[96,2304]{1,0:T(8,128)(2,1)S(1)} collective-permute-done((bf16[96,2304]{1,0:T(8,128)(2,1)S(1)}, bf16[96,2304]{1,0:T(8,128)(2,1)S(1)}, u32[]{:S(2)}, u32[]{:S(2)}) %collective-permute-start.27) | collective-permute-done | bytes 442400 | tf_op jit(solution)/shard_map/ppermute | solution.py:575
  109.2 12.4 %collective-permute-done.19.refs_16_.refs_12_.refs_17_ = bf16[96,2304]{1,0:T(8,128)(2,1)} collective-permute-done((bf16[96,2304]{1,0:T(8,128)(2,1)}, bf16[96,2304]{1,0:T(8,128)(2,1)}, u32[]{:S(2)}, u32[]{:S(2)}) %collective-permute-start.19) | collective-permute-done | bytes 442400 | tf_op jit(solution)/shard_map/ppermute | solution.py:575
  138.7 12.3 %attn_fwd_a.1 = (f32[256,768]{1,0:T(8,128)}, bf16[2,6,128,512]{3,2,1,0:T(8,128)(2,1)}, bf16[2,640,640]{2,1,0:T(8,128)(2,1)}, bf16[2,256,256]{2,1,0:T(8,128)(2,1)}) custom-call(bf16[256,768]{1,0:T(8,128)(2,1)} %get-tuple-element.84.refs_0_, bf16[256,768]{1,0:T(8,128)(2,1)} %edge.1.refs_1_, bf16[32,768]{1,0:T(8,128)(2,1)} %get-tuple-element.85.refs_2_, ...), custom_call_target="tpu_custom_call" | custom-call | tf_op jit(solution)/shard_map/attn_fwd_a/pallas_call | solution.py:251
  151.0 12.7 %attn_fwd_b.1 = (f32[256,768]{1,0:T(8,128)}, bf16[256,768]{1,0:T(8,128)(2,1)}, bf16[2,6,128,512]{3,2,1,0:T(8,128)(2,1)}, bf16[2,640,640]{2,1,0:T(8,128)(2,1)}, bf16[2,256,256]{2,1,0:T(8,128)(2,1)}) custom-call(bf16[256,768]{1,0:T(8,128)(2,1)} %get-tuple-element.84.refs_0_, bf16[256,768]{1,0:T(8,128)(2,1)} %edge.1.refs_1_, ...), custom_call_target="tpu_custom_call" | custom-call | tf_op jit(solution)/shard_map/attn_fwd_b/pallas_call | solution.py:251
  163.8 9.7 %ff_b.1 = (bf16[2,384,1536]{2,1,0:T(8,128)(2,1)}, bf16[2,384,1536]{2,1,0:T(8,128)(2,1)}, f32[256,768]{1,0:T(8,128)}, f32[256,768]{1,0:T(8,128)}) custom-call(bf16[256,768]{1,0:T(8,128)(2,1)} %get-tuple-element.97.refs_0_, bf16[256,768]{1,0:T(8,128)(2,1)} %get-tuple-element.98.refs_1_, bf16[96,2304]{1,0:T(8,128)(2,1)} %collective-permute-done.9.refs_6_.refs_2_.refs_7_, ...), custom_call_target="tpu_custom_call" | custom-call | tf_op jit(solution)/shard_map/ff_b/pallas_call | solution.py:464
  173.4 12.7 %ff_a.1 = (bf16[2,384,1536]{2,1,0:T(8,128)(2,1)}, bf16[2,384,1536]{2,1,0:T(8,128)(2,1)}, bf16[256,768]{1,0:T(8,128)(2,1)}, f32[256,768]{1,0:T(8,128)}, bf16[256,768]{1,0:T(8,128)(2,1)}, /*index=5*/f32[1,768]{1,0:T(1,128)}) custom-call(bf16[256,768]{1,0:T(8,128)(2,1)} %get-tuple-element.97.refs_0_, bf16[256,768]{1,0:T(8,128)(2,1)} %get-tuple-element.98.refs_1_, ...), custom_call_target="tpu_custom_call" | custom-call | tf_op jit(solution)/shard_map/ff_a/pallas_call | solution.py:464
  186.2 15.6 %shard_map.272 = (bf16[2,384,768]{2,1,0:T(8,128)(2,1)}, bf16[2,384,768]{2,1,0:T(8,128)(2,1)}, f32[2,3,384]{2,1,0:T(4,128)}, f32[2,3,16,128]{3,2,1,0:T(8,128)}, f32[640,768]{1,0:T(8,128)}) custom-call(bf16[256,768]{1,0:T(8,128)(2,1)} %get-tuple-element.84.refs_0_, bf16[256,768]{1,0:T(8,128)(2,1)} %edge.1.refs_1_, bf16[32,768]{1,0:T(8,128)(2,1)} %get-tuple-element.85.refs_2_, ...), custom_call_target="tpu_custom_call" | custom-call | tf_op jit(solution)/shard_map/pallas_call | solution.py:388
  201.8 9.3 %shard_map.273 = (bf16[1,384,768]{2,1,0:T(8,128)(2,1)}, bf16[1,384,768]{2,1,0:T(8,128)(2,1)}, f32[1,3,384]{2,1,0:T(4,128)}, f32[1,3,16,128]{3,2,1,0:T(8,128)}, f32[640,768]{1,0:T(8,128)}) custom-call(bf16[256,768]{1,0:T(8,128)(2,1)} %get-tuple-element.84.refs_0_, bf16[256,768]{1,0:T(8,128)(2,1)} %edge.1.refs_1_, bf16[32,768]{1,0:T(8,128)(2,1)} %get-tuple-element.85.refs_2_, ...), custom_call_target="tpu_custom_call" | custom-call | tf_op jit(solution)/shard_map/pallas_call | solution.py:388
  211.1 8.6 %shard_map.274 = (bf16[1,384,768]{2,1,0:T(8,128)(2,1)}, bf16[1,384,768]{2,1,0:T(8,128)(2,1)}, f32[1,3,384]{2,1,0:T(4,128)}, f32[1,3,16,128]{3,2,1,0:T(8,128)}, f...) custom-call(bf16[256,768]{1,0:T(8,128)(2,1)} %get-tuple-element.84.r, ...), custom_call_target="tpu_custom_call" | custom-call | tf_op jit(solution)/shard_map/pallas_call | solution.py:388
  219.8 3.5 collective-permute-start.40
  224.1 4.8 %collective-permute-start.41 = (bf16[32,768]{1,0:T(8,128)(2,1)}, bf16[32,768]{1,0:T(8,128)(2,1)S(1)}, u32[]{:S(2)}, u32[]{:S(2)}) collective-permute-start(bf16[32,768]{1,0:T(8,128)(2,1)} %get-tuple-element.115), channel_id=1, source_target_pairs={{0,2},{1,3},{2,0},{3,1},{4,6},{5,7},{6,4},{7,5},{8,10},{9,11},{10,... | collective-permute-start | bytes 147464 | tf_op jit(solution)/shard_map/ppermute | solution.py:575
  228.9 2.9 collective-permute-start.42
  231.8 5.9 %collective-permute-done.41.r2 = bf16[32,768]{1,0:T(8,128)(2,1)S(1)} collective-permute-done((bf16[32,768]{1,0:T(8,128)(2,1)}, bf16[32,768]{1,0:T(8,128)(2,1)S(1)}, u32[]{:S(2)}, u32[]{:S(2)}) %collective-permute-start.41) | collective-permute-done | bytes 49184 | tf_op jit(solution)/shard_map/ppermute | solution.py:575
  238.5 6.3 %post.1 = (f32[256,768]{1,0:T(8,128)}, f32[24,768]{1,0:T(8,128)}) custom-call(s32[3]{0:T(128)} %pad_add_fusion.1.refs_19_.where_ref, f32[256,768]{1,0:T(8,128)} %get-tuple-element.112.own, f32[32,768]{1,0:T(8,128)} %get-tuple-element.113.f0, bf16[160,768]{1,0:T(8,128)(2,1)} %copy-done.24, bf16[32,768]{1,0:T(8,128)(2,1)} %copy-done.31, ...), custom_call_target="tpu_custom_call" | custom-call | tf_op jit(solution)/shard_map/post/pallas_call | solution.py:542
  259.3 3.6 collective-permute-done.50
  264.4 4.0 %collective-permute-done.48 = f32[24,768]{1,0:T(8,128)} collective-permute-done((f32[24,768]{1,0:T(8,128)}, f32[24,768]{1,0:T(8,128)}, u32[]{:S(2)}, u32[]{:S(2)}) %collective-permute-start.48) | collective-permute-done | bytes 73760 | tf_op jit(solution)/shard_map/ppermute | solution.py:575
  276.4 11.7 %collective-permute-done.54 = bf16[2,96,768]{2,1,0:T(8,128)(2,1)S(1)} collective-permute-done((bf16[2,96,768]{2,1,0:T(8,128)(2,1)S(1)}, bf16[2,96,768]{2,1,0:T(8,128)(2,1)S(1)}, u32[]{:S(2)}, u32[]{:S(2)}) %collective-permute-start.54) | collective-permute-done | bytes 294944 | tf_op jit(solution)/shard_map/ppermute | solution.py:575
  292.4 6.5 %collective-permute-done.60 = bf16[2,96,768]{2,1,0:T(8,128)(2,1)S(1)} collective-permute-done((bf16[2,96,768]{2,1,0:T(8,128)(2,1)S(1)}, bf16[2,96,768]{2,1,0:T(8,128)(2,1)S(1)}, u32[]{:S(2)}, u32[]{:S(2)}) %collective-permute-start.60) | collective-permute-done | bytes 294944 | tf_op jit(solution)/shard_map/ppermute | solution.py:575
  298.9 4.9 %collective-permute-done.59 = bf16[2,96,768]{2,1,0:T(8,128)(2,1)S(1)} collective-permute-done((bf16[2,96,768]{2,1,0:T(8,128)(2,1)S(1)}, bf16[2,96,768]{2,1,0:T(8,128)(2,1)S(1)}, u32[]{:S(2)}, u32[]{:S(2)}) %collective-permute-start.59) | collective-permute-done | bytes 294944 | tf_op jit(solution)/shard_map/ppermute | solution.py:575
  310.8 10.0 %collective-permute-done.69 = bf16[2,96,1536]{2,1,0:T(8,128)(2,1)S(1)} collective-permute-done((bf16[2,96,1536]{2,1,0:T(8,128)(2,1)S(1)}, bf16[2,96,1536]{2,1,0:T(8,128)(2,1)S(1)}, u32[]{:S(2)}, u32[]{:S(2)}) %collective-permute-start.69) | collective-permute-done | bytes 589856 | tf_op jit(solution)/shard_map/ppermute | solution.py:575
  321.5 12.1 %collective-permute-done.71 = bf16[2,96,1536]{2,1,0:T(8,128)(2,1)S(1)} collective-permute-done((bf16[2,96,1536]{2,1,0:T(8,128)(2,1)S(1)}, bf16[2,96,1536]{2,1,0:T(8,128)(2,1)S(1)}, u32[]{:S(2)}, u32[]{:S(2)}) %collective-permute-start.71) | collective-permute-done | bytes 589856 | tf_op jit(solution)/shard_map/ppermute | solution.py:575
  336.6 9.6 %collective-permute-done.64 = bf16[2,96,1536]{2,1,0:T(8,128)(2,1)S(1)} collective-permute-done((bf16[2,96,1536]{2,1,0:T(8,128)(2,1)S(1)}, bf16[2,96,1536]{2,1,0:T(8,128)(2,1)S(1)}, u32[]{:S(2)}, u32[]{:S(2)}) %collective-permute-start.64) | collective-permute-done | bytes 589856 | tf_op jit(solution)/shard_map/ppermute | solution.py:575
  346.8 11.2 %collective-permute-done.66 = bf16[2,96,1536]{2,1,0:T(8,128)(2,1)S(1)} collective-permute-done((bf16[2,96,1536]{2,1,0:T(8,128)(2,1)S(1)}, bf16[2,96,1536]{2,1,0:T(8,128)(2,1)S(1)}, u32[]{:S(2)}, u32[]{:S(2)}) %collective-permute-start.66) | collective-permute-done | bytes 589856 | tf_op jit(solution)/shard_map/ppermute | solution.py:575
  367.9 11.0 %collective-permute-done.72 = bf16[96,1536]{1,0:T(8,128)(2,1)S(1)} collective-permute-done((bf16[96,1536]{1,0:T(8,128)(2,1)S(1)}, bf16[96,1536]{1,0:T(8,128)(2,1)S(1)}, u32[]{:S(2)}, u32[]{:S(2)}) %collective-permute-start.72) | collective-permute-done | bytes 294944 | tf_op jit(solution)/shard_map/ppermute | solution.py:575
  (279 shorter events, 126.2 us)
Async XLA Ops:
  7.0 35.5 %collective-permute-start.5 = (bf16[128,768]{1,0:T(8,128)(2,1)S(1)}, bf16[128,768]{1,0:T(8,128)(2,1)}, u32[]{:S(2)}, u32[]{:S(2)}) collective-permute-start(bf16[128,768]{1,0:T(8,128)(2,1)S(1)} %get-tuple-element.172), channel_id=1, source_target_pairs={{1,0},{2,1},{3,2},{5,4},{6,5},{7,6},{9,8},{10,9},{11,10},{13,12},{... | collective-permute-start | bytes 589832 | tf_op jit(solution)/shard_map/ppermute | solution.py:655
  8.3 34.4 %collective-permute-start.4 = (bf16[128,768]{1,0:T(8,128)(2,1)S(1)}, bf16[128,768]{1,0:T(8,128)(2,1)S(1)}, u32[]{:S(2)}, u32[]{:S(2)}) collective-permute-start(bf16[128,768]{1,0:T(8,128)(2,1)S(1)} %get-tuple-element.173), channel_id=1, source_target_pairs={{0,1},{1,2},{2,3},{4,5},{5,6},{6,7},{8,9},{9,10},{10,11},{12,13},{... | collective-permute-start | bytes 589832 | tf_op jit(solution)/shard_map/ppermute | solution.py:654
  18.1 25.9 %collective-permute-start.32 = (bf16[96,2304]{1,0:T(8,128)(2,1)}, bf16[96,2304]{1,0:T(8,128)(2,1)S(1)}, u32[]{:S(2)}, u32[]{:S(2)}) collective-permute-start(bf16[96,2304]{1,0:T(8,128)(2,1)} %pack.1.refs_6_.refs_2_.refs_7_), channel_id=1, source_target_pairs={{0,4},{4,0},{8,12},{12,8},{16,20},{20,16},{24,28},{28,24},{1,5},{5... | collective-permute-start | bytes 1327112 | tf_op jit(solution)/shard_map/ppermute | solution.py:575
  42.0 18.7 %collective-permute-start.30 = (bf16[96,2304]{1,0:T(8,128)(2,1)S(1)}, bf16[96,2304]{1,0:T(8,128)(2,1)S(1)}, u32[]{:S(2)}, u32[]{:S(2)}) collective-permute-start(bf16[96,2304]{1,0:T(8,128)(2,1)S(1)} %copy-done), channel_id=1, source_target_pairs={{0,16},{4,20},{8,24},{12,28},{16,0},{20,4},{24,8},{28,12},{1,17},{... | collective-permute-start | bytes 1327112 | tf_op jit(solution)/shard_map/ppermute | solution.py:575
  42.7 18.5 %collective-permute-start.25 = (bf16[96,2304]{1,0:T(8,128)(2,1)S(1)}, bf16[96,2304]{1,0:T(8,128)(2,1)S(1)}, u32[]{:S(2)}, u32[]{:S(2)}) collective-permute-start(bf16[96,2304]{1,0:T(8,128)(2,1)S(1)} %copy-done), channel_id=1, source_target_pairs={{0,1},{1,0},{2,3},{3,2},{4,5},{5,4},{6,7},{7,6},{8,9},{9,8},{10,11... | collective-permute-start | bytes 1327112 | tf_op jit(solution)/shard_map/ppermute | solution.py:575
  44.0 23.4 %collective-permute-start.17 = (bf16[96,2304]{1,0:T(8,128)(2,1)S(1)}, bf16[96,2304]{1,0:T(8,128)(2,1)S(1)}, u32[]{:S(2)}, u32[]{:S(2)}) collective-permute-start(bf16[96,2304]{1,0:T(8,128)(2,1)S(1)} %copy-done), channel_id=1, source_target_pairs={{0,3},{1,2},{2,1},{3,0},{4,7},{5,6},{6,5},{7,4},{8,11},{9,10},{10,... | collective-permute-start | bytes 1327112 | tf_op jit(solution)/shard_map/ppermute | solution.py:575
  53.1 30.5 %collective-permute-start.9 = (bf16[96,2304]{1,0:T(8,128)(2,1)S(1)}, bf16[96,2304]{1,0:T(8,128)(2,1)}, u32[]{:S(2)}, u32[]{:S(2)}) collective-permute-start(bf16[96,2304]{1,0:T(8,128)(2,1)S(1)} %copy-done), channel_id=1, source_target_pairs={{0,2},{1,3},{2,0},{3,1},{4,6},{5,7},{6,4},{7,5},{8,10},{9,11},{10,... | collective-permute-start | bytes 1327112 | tf_op jit(solution)/shard_map/ppermute | solution.py:575
  60.7 24.3 %collective-permute-start.35 = (bf16[96,2304]{1,0:T(8,128)(2,1)S(1)}, bf16[96,2304]{1,0:T(8,128)(2,1)S(1)}, u32[]{:S(2)}, u32[]{:S(2)}) collective-permute-start(bf16[96,2304]{1,0:T(8,128)(2,1)S(1)} %collective-permute-done.31.refs_9_.refs_5_.refs_10_), channel_id=1, source_target_pairs={{0,4},{4,0},{8,12},{12,8},{16,20},{20,16},{24,28},{28,24},{1,5},{5... | collective-permute-start | bytes 1327112 | tf_op jit(solution)/shard_map/ppermute | solution.py:575
  60.7 25.9 %collective-permute-start.34 = (bf16[96,2304]{1,0:T(8,128)(2,1)S(1)}, bf16[96,2304]{1,0:T(8,128)(2,1)S(1)}, u32[]{:S(2)}, u32[]{:S(2)}) collective-permute-start(bf16[96,2304]{1,0:T(8,128)(2,1)S(1)} %collective-permute-done.30.refs_8_.refs_4_.refs_9_), channel_id=1, source_target_pairs={{0,4},{4,0},{8,12},{12,8},{16,20},{20,16},{24,28},{28,24},{1,5},{5... | collective-permute-start | bytes 1327112 | tf_op jit(solution)/shard_map/ppermute | solution.py:575
  61.2 25.4 %collective-permute-start.33 = (bf16[96,2304]{1,0:T(8,128)(2,1)S(1)}, bf16[96,2304]{1,0:T(8,128)(2,1)}, u32[]{:S(2)}, u32[]{:S(2)}) collective-permute-start(bf16[96,2304]{1,0:T(8,128)(2,1)S(1)} %collective-permute-done.29.refs_7_.refs_3_.refs_8_), channel_id=1, source_target_pairs={{0,4},{4,0},{8,12},{12,8},{16,20},{20,16},{24,28},{28,24},{1,5},{5... | collective-permute-start | bytes 1327112 | tf_op jit(solution)/shard_map/ppermute | solution.py:575
  68.1 19.1 %collective-permute-start.28 = (bf16[96,2304]{1,0:T(8,128)(2,1)S(1)}, bf16[96,2304]{1,0:T(8,128)(2,1)S(1)}, u32[]{:S(2)}, u32[]{:S(2)}) collective-permute-start(bf16[96,2304]{1,0:T(8,128)(2,1)S(1)} %collective-permute-done.25.refs_14_.refs_10_.refs_7_), channel_id=1, source_target_pairs={{0,24},{4,28},{8,16},{12,20},{16,8},{20,12},{24,0},{28,4},{1,25},{... | collective-permute-start | bytes 1327112 | tf_op jit(solution)/shard_map/ppermute | solution.py:575
  83.6 20.2 %collective-permute-start.27 = (bf16[96,2304]{1,0:T(8,128)(2,1)S(1)}, bf16[96,2304]{1,0:T(8,128)(2,1)S(1)}, u32[]{:S(2)}, u32[]{:S(2)}) collective-permute-start(bf16[96,2304]{1,0:T(8,128)(2,1)S(1)} %collective-permute-done.25.refs_14_.refs_10_.refs_7_), channel_id=1, source_target_pairs={{0,16},{4,20},{8,24},{12,28},{16,0},{20,4},{24,8},{28,12},{1,17},{... | collective-permute-start | bytes 1327112 | tf_op jit(solution)/shard_map/ppermute | solution.py:575
  85.0 20.9 %collective-permute-start.26 = (bf16[96,2304]{1,0:T(8,128)(2,1)S(1)}, bf16[96,2304]{1,0:T(8,128)(2,1)S(1)}, u32[]{:S(2)}, u32[]{:S(2)}) collective-permute-start(bf16[96,2304]{1,0:T(8,128)(2,1)S(1)} %collective-permute-done.25.refs_14_.refs_10_.refs_7_), channel_id=1, source_target_pairs={{0,8},{4,12},{8,0},{12,4},{16,24},{20,28},{24,16},{28,20},{1,9},{5... | collective-permute-start | bytes 1327112 | tf_op jit(solution)/shard_map/ppermute | solution.py:575
  86.6 19.4 %collective-permute-start.21 = (bf16[96,2304]{1,0:T(8,128)(2,1)}, bf16[96,2304]{1,0:T(8,128)(2,1)}, u32[]{:S(2)}, u32[]{:S(2)}) collective-permute-start(bf16[96,2304]{1,0:T(8,128)(2,1)} %copy-done.15), channel_id=1, source_target_pairs={{0,4},{4,0},{8,12},{12,8},{16,20},{20,16},{24,28},{28,24},{1,5},{5... | collective-permute-start | bytes 1327112 | tf_op jit(solution)/shard_map/ppermute | solution.py:575
  86.6 21.1 %collective-permute-start.20 = (bf16[96,2304]{1,0:T(8,128)(2,1)}, bf16[96,2304]{1,0:T(8,128)(2,1)}, u32[]{:S(2)}, u32[]{:S(2)}) collective-permute-start(bf16[96,2304]{1,0:T(8,128)(2,1)} %copy-done.15), channel_id=1, source_target_pairs={{0,24},{4,28},{8,16},{12,20},{16,8},{20,12},{24,0},{28,4},{1,25},{... | collective-permute-start | bytes 1327112 | tf_op jit(solution)/shard_map/ppermute | solution.py:575
  87.2 34.4 %collective-permute-start.19 = (bf16[96,2304]{1,0:T(8,128)(2,1)}, bf16[96,2304]{1,0:T(8,128)(2,1)}, u32[]{:S(2)}, u32[]{:S(2)}) collective-permute-start(bf16[96,2304]{1,0:T(8,128)(2,1)} %copy-done.15), channel_id=1, source_target_pairs={{0,16},{4,20},{8,24},{12,28},{16,0},{20,4},{24,8},{28,12},{1,17},{... | collective-permute-start | bytes 1327112 | tf_op jit(solution)/shard_map/ppermute | solution.py:575
  103.8 27.0 %collective-permute-start.18 = (bf16[96,2304]{1,0:T(8,128)(2,1)}, bf16[96,2304]{1,0:T(8,128)(2,1)}, u32[]{:S(2)}, u32[]{:S(2)}) collective-permute-start(bf16[96,2304]{1,0:T(8,128)(2,1)} %copy-done.15), channel_id=1, source_target_pairs={{0,8},{4,12},{8,0},{12,4},{16,24},{20,28},{24,16},{28,20},{1,9},{5... | collective-permute-start | bytes 1327112 | tf_op jit(solution)/shard_map/ppermute | solution.py:575
  105.9 24.9 %collective-permute-start.13 = (bf16[96,2304]{1,0:T(8,128)(2,1)}, bf16[96,2304]{1,0:T(8,128)(2,1)}, u32[]{:S(2)}, u32[]{:S(2)}) collective-permute-start(bf16[96,2304]{1,0:T(8,128)(2,1)} %collective-permute-done.9.refs_6_.refs_2_.refs_7_), channel_id=1, source_target_pairs={{0,4},{4,0},{8,12},{12,8},{16,20},{20,16},{24,28},{28,24},{1,5},{5... | collective-permute-start | bytes 1327112 | tf_op jit(solution)/shard_map/ppermute | solution.py:575
  106.0 25.3 %collective-permute-start.12 = (bf16[96,2304]{1,0:T(8,128)(2,1)}, bf16[96,2304]{1,0:T(8,128)(2,1)}, u32[]{:S(2)}, u32[]{:S(2)}) collective-permute-start(bf16[96,2304]{1,0:T(8,128)(2,1)} %collective-permute-done.9.refs_6_.refs_2_.refs_7_), channel_id=1, source_target_pairs={{0,24},{4,28},{8,16},{12,20},{16,8},{20,12},{24,0},{28,4},{1,25},{... | collective-permute-start | bytes 1327112 | tf_op jit(solution)/shard_map/ppermute | solution.py:575
  107.7 23.7 %collective-permute-start.11 = (bf16[96,2304]{1,0:T(8,128)(2,1)}, bf16[96,2304]{1,0:T(8,128)(2,1)}, u32[]{:S(2)}, u32[]{:S(2)}) collective-permute-start(bf16[96,2304]{1,0:T(8,128)(2,1)} %collective-permute-done.9.refs_6_.refs_2_.refs_7_), channel_id=1, source_target_pairs={{0,16},{4,20},{8,24},{12,28},{16,0},{20,4},{24,8},{28,12},{1,17},{... | collective-permute-start | bytes 1327112 | tf_op jit(solution)/shard_map/ppermute | solution.py:575
  249.2 20.3 %collective-permute-start.51 = (bf16[1,384,768]{2,1,0:T(8,128)(2,1)}, bf16[1,384,768]{2,1,0:T(8,128)(2,1)}, u32[]{:S(2)}, u32[]{:S(2)}) collective-permute-start(bf16[1,384,768]{2,1,0:T(8,128)(2,1)} %get-tuple-element.130), channel_id=1, source_target_pairs={{0,4},{4,0},{8,12},{12,8},{16,20},{20,16},{24,28},{28,24},{1,5},{5... | collective-permute-start | bytes 1769480 | tf_op jit(solution)/shard_map/ppermute | solution.py:575
  258.8 45.2 %collective-permute-start.68 = (bf16[2,384,1536]{2,1,0:T(8,128)(2,1)}, bf16[2,384,1536]{2,1,0:T(8,128)(2,1)S(1)}, u32[]{:S(2)}, u32[]{:S(2)}) collective-permute-start(bf16[2,384,1536]{2,1,0:T(8,128)(2,1)} %get-tuple-element.145), channel_id=1, source_target_pairs={{0,4},{4,0},{8,12},{12,8},{16,20},{20,16},{24,28},{28,24},{1,5},{5... | collective-permute-start | bytes 7077896 | tf_op jit(solution)/shard_map/ppermute | solution.py:575
  268.5 39.6 %collective-permute-start.63 = (bf16[2,384,1536]{2,1,0:T(8,128)(2,1)}, bf16[2,384,1536]{2,1,0:T(8,128)(2,1)S(1)}, u32[]{:S(2)}, u32[]{:S(2)}) collective-permute-start(bf16[2,384,1536]{2,1,0:T(8,128)(2,1)} %get-tuple-element.143), channel_id=1, source_target_pairs={{0,4},{4,0},{8,12},{12,8},{16,20},{20,16},{24,28},{28,24},{1,5},{5... | collective-permute-start | bytes 7077896 | tf_op jit(solution)/shard_map/ppermute | solution.py:575
  298.9 64.5 %collective-permute-start.56 = (bf16[96,768]{1,0:T(8,128)(2,1)S(1)}, bf16[96,768]{1,0:T(8,128)(2,1)S(1)}, u32[]{:S(2)}, u32[]{:S(2)}) collective-permute-start(bf16[96,768]{1,0:T(8,128)(2,1)S(1)} %get-tuple-element.176), channel_id=1, source_target_pairs={{0,1},{1,0},{2,3},{3,2},{4,5},{5,4},{6,7},{7,6},{8,9},{9,8},{10,11... | collective-permute-start | bytes 442376 | tf_op jit(solution)/shard_map/ppermute | solution.py:575
  305.3 28.3 %collective-permute-start.71 = (bf16[2,96,1536]{2,1,0:T(8,128)(2,1)S(1)}, bf16[2,96,1536]{2,1,0:T(8,128)(2,1)S(1)}, u32[]{:S(2)}, u32[]{:S(2)}) collective-permute-start(bf16[2,96,1536]{2,1,0:T(8,128)(2,1)S(1)} %get-tuple-element.154), channel_id=1, source_target_pairs={{0,24},{4,28},{8,16},{12,20},{16,8},{20,12},{24,0},{28,4},{1,25},{... | collective-permute-start | bytes 1769480 | tf_op jit(solution)/shard_map/ppermute | solution.py:575
  306.8 28.3 %collective-permute-start.70 = (bf16[2,96,1536]{2,1,0:T(8,128)(2,1)S(1)}, bf16[2,96,1536]{2,1,0:T(8,128)(2,1)S(1)}, u32[]{:S(2)}, u32[]{:S(2)}) collective-permute-start(bf16[2,96,1536]{2,1,0:T(8,128)(2,1)S(1)} %get-tuple-element.155), channel_id=1, source_target_pairs={{0,16},{4,20},{8,24},{12,28},{16,0},{20,4},{24,8},{28,12},{1,17},{... | collective-permute-start | bytes 1769480 | tf_op jit(solution)/shard_map/ppermute | solution.py:575
  308.1 57.1 %collective-permute-start.62 = (bf16[96,768]{1,0:T(8,128)(2,1)S(1)}, bf16[96,768]{1,0:T(8,128)(2,1)S(1)}, u32[]{:S(2)}, u32[]{:S(2)}) collective-permute-start(bf16[96,768]{1,0:T(8,128)(2,1)S(1)} %get-tuple-element.174), channel_id=1, source_target_pairs={{0,3},{1,2},{2,1},{3,0},{4,7},{5,6},{6,5},{7,4},{8,11},{9,10},{10,... | collective-permute-start | bytes 442376 | tf_op jit(solution)/shard_map/ppermute | solution.py:575
  320.8 25.3 %collective-permute-start.64 = (bf16[2,96,1536]{2,1,0:T(8,128)(2,1)S(1)}, bf16[2,96,1536]{2,1,0:T(8,128)(2,1)S(1)}, u32[]{:S(2)}, u32[]{:S(2)}) collective-permute-start(bf16[2,96,1536]{2,1,0:T(8,128)(2,1)S(1)} %get-tuple-element.150), channel_id=1, source_target_pairs={{0,8},{4,12},{8,0},{12,4},{16,24},{20,28},{24,16},{28,20},{1,9},{5... | collective-permute-start | bytes 1769480 | tf_op jit(solution)/shard_map/ppermute | solution.py:575
  333.6 24.4 %collective-permute-start.66 = (bf16[2,96,1536]{2,1,0:T(8,128)(2,1)S(1)}, bf16[2,96,1536]{2,1,0:T(8,128)(2,1)S(1)}, u32[]{:S(2)}, u32[]{:S(2)}) collective-permute-start(bf16[2,96,1536]{2,1,0:T(8,128)(2,1)S(1)} %get-tuple-element.151), channel_id=1, source_target_pairs={{0,24},{4,28},{8,16},{12,20},{16,8},{20,12},{24,0},{28,4},{1,25},{... | collective-permute-start | bytes 1769480 | tf_op jit(solution)/shard_map/ppermute | solution.py:575
  335.1 25.8 %collective-permute-start.65 = (bf16[2,96,1536]{2,1,0:T(8,128)(2,1)S(1)}, bf16[2,96,1536]{2,1,0:T(8,128)(2,1)S(1)}, u32[]{:S(2)}, u32[]{:S(2)}) collective-permute-start(bf16[2,96,1536]{2,1,0:T(8,128)(2,1)S(1)} %get-tuple-element.152), channel_id=1, source_target_pairs={{0,16},{4,20},{8,24},{12,28},{16,0},{20,4},{24,8},{28,12},{1,17},{... | collective-permute-start | bytes 1769480 | tf_op jit(solution)/shard_map/ppermute | solution.py:575
  346.1 19.1 %collective-permute-start.61 = (bf16[96,768]{1,0:T(8,128)(2,1)S(1)}, bf16[96,768]{1,0:T(8,128)(2,1)S(1)}, u32[]{:S(2)}, u32[]{:S(2)}) collective-permute-start(bf16[96,768]{1,0:T(8,128)(2,1)S(1)} %get-tuple-element.175), channel_id=1, source_target_pairs={{0,2},{1,3},{2,0},{3,1},{4,6},{5,7},{6,4},{7,5},{8,10},{9,11},{10,... | collective-permute-start | bytes 442376 | tf_op jit(solution)/shard_map/ppermute | solution.py:575
  358.0 20.9 %collective-permute-start.72 = (bf16[96,1536]{1,0:T(8,128)(2,1)S(1)}, bf16[96,1536]{1,0:T(8,128)(2,1)S(1)}, u32[]{:S(2)}, u32[]{:S(2)}) collective-permute-start(bf16[96,1536]{1,0:T(8,128)(2,1)S(1)} %get-tuple-element.170), channel_id=1, source_target_pairs={{0,2},{1,3},{2,0},{3,1},{4,6},{5,7},{6,4},{7,5},{8,10},{9,11},{10,... | collective-permute-start | bytes 884744 | tf_op jit(solution)/shard_map/ppermute | solution.py:575
  (77 other events, 1056.5 us)

commit v3 on v2

--- a/solution.py
+++ b/solution.py
@@ -744,6 +744,7 @@
         nb_0, nb_1, nb_b, fb_0, fb_1, fb_b, near_at, far_at,
     )
     got = [small] + gather_tensor(small)
+    got, _ = lax.optimization_barrier((got, sum_aa))
     small = (got[0] + got[1]) + (got[2] + got[3])
     small = small + swap(small, "fsdp", 1)
     got = near_swaps(small)
@@ -755,9 +756,8 @@
 
     parts = scatter_tensor([sum_fa[0], sum_fa[1], sum_fb[0], sum_fb[1]])
     ff_sum = sum(part.astype(f32) for part in parts)
-    grad_query, grad_key, grad_value, grad_w_out = unpack(
-        *scatter_tensor([sum_aa[0], sum_aa[1], sum_ab[0], sum_ab[1]])
-    )
+    last_sums = scatter_tensor([sum_aa[0], sum_aa[1], sum_ab[0], sum_ab[1]])
+    grad_query, grad_key, grad_value, grad_w_out = unpack(*last_sums)
     return (
         output,
         grad_tokens,

time: 390 us -> 390 us (level)
  transfers between devices with their start and end apart: 74 -> 74, of which waited for: 31 -> 32; matrix products, arithmetic and copies ran while one was open for 10% -> 11% of each run, Pallas kernels for 6% -> 7%
where the time goes in v3:
time: 390 us; the launch traced here: 383 us
  waiting for transfers between devices  157 us (40%)
  Pallas kernels  97.4 us (25%)
  starting transfers between devices  80.5 us (21%)
  other arithmetic  24.4 us (6%)
  local copies, waits for them, and re-layouts  20.7 us (5%)
    ppermute x71, waiting for transfers between devices, swap(): return lax.ppermute(x, axis, [(i, i ^ mask) for i in range(size)])  157 us
    ppermute x71, starting transfers between devices, swap(): return lax.ppermute(x, axis, [(i, i ^ mask) for i in range(size)])  73.8 us
    pallas_call x3, Pallas kernels, attn_bwd(): pl.pallas_call(lambda *refs: attn_bwd_kernel(slabs, more, last, *refs), g...  33.6 us
    pallas_call x2, Pallas kernels, attn_fwd(): pl.pallas_call(lambda *refs: attn_fwd_kernel(base, last, *refs), grid=(2,...  24.9 us
    pallas_call x2, Pallas kernels, ff_both(): pl.pallas_call(lambda *refs: ff_kernel(last, *refs), grid=(2,), in_specs=...  22.4 us
  transfers between devices with their start and end apart: 74, of which 32 were waited for; matrix products, arithmetic and copies ran while one was open for 11% of the time, Pallas kernels for 7%

profile of v3, /device:TPU:0, one launch (start us, length us, event | category | flops | bytes accessed | tf_op | source)
XLA Modules:
  0.0 382.9 jit_solution(8376958761396374966)
XLA Ops:
  1.4 4.0 %collective-permute-start.2 = (bf16[3,1,96]{2,0,1:T(4,128)(2,1)S(1)}, bf16[3,1,96]{2,0,1:T(4,128)(2,1)S(1)}, u32[]{:S(2)}, u32[]{:S(2)}) collective-permute-start(bf16[3,1,96]{2,0,1:T(4,128)(2,1)S(1)} %get-tuple-element.157), channel_id=1, source_target_pairs={{0,24},{4,28},{8,16},{12,20},{16,8},{20,12},{24,0},{28,4},{1,25},{... | collective-permute-start | bytes 1736 | tf_op jit(solution)/shard_map/ppermute | solution.py:575
  8.3 4.6 %collective-permute-start.4 = (bf16[128,768]{1,0:T(8,128)(2,1)S(1)}, bf16[128,768]{1,0:T(8,128)(2,1)S(1)}, u32[]{:S(2)}, u32[]{:S(2)}) collective-permute-start(bf16[128,768]{1,0:T(8,128)(2,1)S(1)} %get-tuple-element.181), channel_id=1, source_target_pairs={{0,1},{1,2},{2,3},{4,5},{5,6},{6,7},{8,9},{9,10},{10,11},{12,13},{... | collective-permute-start | bytes 589832 | tf_op jit(solution)/shard_map/ppermute | solution.py:654
  25.0 3.2 prep.1
  39.1 3.0 collective-permute-start.31
  44.0 2.8 collective-permute-start.17
  48.8 4.4 %collective-permute-done.31.refs_9_.refs_5_.refs_10_ = bf16[96,2304]{1,0:T(8,128)(2,1)S(1)} collective-permute-done((bf16[96,2304]{1,0:T(8,128)(2,1)S(1)}, bf16[96,2304]{1,0:T(8,128)(2,1)S(1)}, u32[]{:S(2)}, u32[]{:S(2)}) %collective-permute-start.31) | collective-permute-done | bytes 442400 | tf_op jit(solution)/shard_map/ppermute | solution.py:575
  55.0 5.8 %collective-permute-done.30.refs_8_.refs_4_.refs_9_ = bf16[96,2304]{1,0:T(8,128)(2,1)S(1)} collective-permute-done((bf16[96,2304]{1,0:T(8,128)(2,1)S(1)}, bf16[96,2304]{1,0:T(8,128)(2,1)S(1)}, u32[]{:S(2)}, u32[]{:S(2)}) %collective-permute-start.30) | collective-permute-done | bytes 442400 | tf_op jit(solution)/shard_map/ppermute | solution.py:575
  61.4 6.1 %collective-permute-done.17.refs_14_.refs_10_.refs_15_ = bf16[96,2304]{1,0:T(8,128)(2,1)S(1)} collective-permute-done((bf16[96,2304]{1,0:T(8,128)(2,1)S(1)}, bf16[96,2304]{1,0:T(8,128)(2,1)S(1)}, u32[]{:S(2)}, u32[]{:S(2)}) %collective-permute-start.17) | collective-permute-done | bytes 442400 | tf_op jit(solution)/shard_map/ppermute | solution.py:575
  74.6 9.1 %collective-permute-done.9.refs_6_.refs_2_.refs_7_ = bf16[96,2304]{1,0:T(8,128)(2,1)} collective-permute-done((bf16[96,2304]{1,0:T(8,128)(2,1)S(1)}, bf16[96,2304]{1,0:T(8,128)(2,1)}, u32[]{:S(2)}, u32[]{:S(2)}) %collective-permute-start.9) | collective-permute-done | bytes 442400 | tf_op jit(solution)/shard_map/ppermute | solution.py:575
  90.5 13.4 %collective-permute-done.27.refs_16_.refs_12_.refs_9_ = bf16[96,2304]{1,0:T(8,128)(2,1)S(1)} collective-permute-done((bf16[96,2304]{1,0:T(8,128)(2,1)S(1)}, bf16[96,2304]{1,0:T(8,128)(2,1)S(1)}, u32[]{:S(2)}, u32[]{:S(2)}) %collective-permute-start.27) | collective-permute-done | bytes 442400 | tf_op jit(solution)/shard_map/ppermute | solution.py:575
  109.3 12.4 %collective-permute-done.19.refs_16_.refs_12_.refs_17_ = bf16[96,2304]{1,0:T(8,128)(2,1)} collective-permute-done((bf16[96,2304]{1,0:T(8,128)(2,1)}, bf16[96,2304]{1,0:T(8,128)(2,1)}, u32[]{:S(2)}, u32[]{:S(2)}) %collective-permute-start.19) | collective-permute-done | bytes 442400 | tf_op jit(solution)/shard_map/ppermute | solution.py:575
  138.9 12.3 %attn_fwd_a.1 = (f32[256,768]{1,0:T(8,128)}, bf16[2,6,128,512]{3,2,1,0:T(8,128)(2,1)}, bf16[2,640,640]{2,1,0:T(8,128)(2,1)}, bf16[2,256,256]{2,1,0:T(8,128)(2,1)}) custom-call(bf16[256,768]{1,0:T(8,128)(2,1)} %get-tuple-element.88.refs_0_, bf16[256,768]{1,0:T(8,128)(2,1)} %edge.1.refs_1_, bf16[32,768]{1,0:T(8,128)(2,1)} %get-tuple-element.89.refs_2_, ...), custom_call_target="tpu_custom_call" | custom-call | tf_op jit(solution)/shard_map/attn_fwd_a/pallas_call | solution.py:251
  151.2 12.7 %attn_fwd_b.1 = (f32[256,768]{1,0:T(8,128)}, bf16[256,768]{1,0:T(8,128)(2,1)}, bf16[2,6,128,512]{3,2,1,0:T(8,128)(2,1)}, bf16[2,640,640]{2,1,0:T(8,128)(2,1)}, bf16[2,256,256]{2,1,0:T(8,128)(2,1)}) custom-call(bf16[256,768]{1,0:T(8,128)(2,1)} %get-tuple-element.88.refs_0_, bf16[256,768]{1,0:T(8,128)(2,1)} %edge.1.refs_1_, ...), custom_call_target="tpu_custom_call" | custom-call | tf_op jit(solution)/shard_map/attn_fwd_b/pallas_call | solution.py:251
  163.9 9.7 %ff_b.1 = (bf16[2,384,1536]{2,1,0:T(8,128)(2,1)}, bf16[2,384,1536]{2,1,0:T(8,128)(2,1)}, f32[256,768]{1,0:T(8,128)}, f32[256,768]{1,0:T(8,128)}) custom-call(bf16[256,768]{1,0:T(8,128)(2,1)} %get-tuple-element.101.refs_0_, bf16[256,768]{1,0:T(8,128)(2,1)} %get-tuple-element.102.refs_1_, bf16[96,2304]{1,0:T(8,128)(2,1)} %collective-permute-done.9.refs_6_.refs_2_.refs_7_, ...), custom_call_target="tpu_custom_call" | custom-call | tf_op jit(solution)/shard_map/ff_b/pallas_call | solution.py:464
  173.5 12.7 %ff_a.1 = (bf16[2,384,1536]{2,1,0:T(8,128)(2,1)}, bf16[2,384,1536]{2,1,0:T(8,128)(2,1)}, bf16[256,768]{1,0:T(8,128)(2,1)}, f32[256,768]{1,0:T(8,128)}, bf16[256,768]{1,0:T(8,128)(2,1)}, /*index=5*/f32[1,768]{1,0:T(1,128)}) custom-call(bf16[256,768]{1,0:T(8,128)(2,1)} %get-tuple-element.101.refs_0_, bf16[256,768]{1,0:T(8,128)(2,1)} %get-tuple-element.102.refs_1_, ...), custom_call_target="tpu_custom_call" | custom-call | tf_op jit(solution)/shard_map/ff_a/pallas_call | solution.py:464
  186.3 15.6 %shard_map.272 = (bf16[2,384,768]{2,1,0:T(8,128)(2,1)}, bf16[2,384,768]{2,1,0:T(8,128)(2,1)}, f32[2,3,384]{2,1,0:T(4,128)}, f32[2,3,16,128]{3,2,1,0:T(8,128)}, f32[640,768]{1,0:T(8,128)}) custom-call(bf16[256,768]{1,0:T(8,128)(2,1)} %get-tuple-element.88.refs_0_, bf16[256,768]{1,0:T(8,128)(2,1)} %edge.1.refs_1_, bf16[32,768]{1,0:T(8,128)(2,1)} %get-tuple-element.89.refs_2_, ...), custom_call_target="tpu_custom_call" | custom-call | tf_op jit(solution)/shard_map/pallas_call | solution.py:388
  201.9 9.3 %shard_map.273 = (bf16[1,384,768]{2,1,0:T(8,128)(2,1)}, bf16[1,384,768]{2,1,0:T(8,128)(2,1)}, f32[1,3,384]{2,1,0:T(4,128)}, f32[1,3,16,128]{3,2,1,0:T(8,128)}, f32[640,768]{1,0:T(8,128)}) custom-call(bf16[256,768]{1,0:T(8,128)(2,1)} %get-tuple-element.88.refs_0_, bf16[256,768]{1,0:T(8,128)(2,1)} %edge.1.refs_1_, bf16[32,768]{1,0:T(8,128)(2,1)} %get-tuple-element.89.refs_2_, ...), custom_call_target="tpu_custom_call" | custom-call | tf_op jit(solution)/shard_map/pallas_call | solution.py:388
  211.2 8.6 %shard_map.274 = (bf16[1,384,768]{2,1,0:T(8,128)(2,1)}, bf16[1,384,768]{2,1,0:T(8,128)(2,1)}, f32[1,3,384]{2,1,0:T(4,128)}, f32[1,3,16,128]{3,2,1,0:T(8,128)}, f...) custom-call(bf16[256,768]{1,0:T(8,128)(2,1)} %get-tuple-element.88.r, ...), custom_call_target="tpu_custom_call" | custom-call | tf_op jit(solution)/shard_map/pallas_call | solution.py:388
  220.4 3.3 collective-permute-start.40
  224.7 4.8 %collective-permute-start.41 = (bf16[32,768]{1,0:T(8,128)(2,1)}, bf16[32,768]{1,0:T(8,128)(2,1)S(1)}, u32[]{:S(2)}, u32[]{:S(2)}) collective-permute-start(bf16[32,768]{1,0:T(8,128)(2,1)} %get-tuple-element.119), channel_id=1, source_target_pairs={{0,2},{1,3},{2,0},{3,1},{4,6},{5,7},{6,4},{7,5},{8,10},{9,11},{10,... | collective-permute-start | bytes 147464 | tf_op jit(solution)/shard_map/ppermute | solution.py:575
  229.4 7.5 %collective-permute-done.41.r2 = bf16[32,768]{1,0:T(8,128)(2,1)S(1)} collective-permute-done((bf16[32,768]{1,0:T(8,128)(2,1)}, bf16[32,768]{1,0:T(8,128)(2,1)S(1)}, u32[]{:S(2)}, u32[]{:S(2)}) %collective-permute-start.41) | collective-permute-done | bytes 49184 | tf_op jit(solution)/shard_map/ppermute | solution.py:575
  239.5 3.5 collective-permute-done.42.r3
  244.2 6.3 %post.1 = (f32[256,768]{1,0:T(8,128)}, f32[24,768]{1,0:T(8,128)}) custom-call(s32[3]{0:T(128)} %pad_add_fusion.1.refs_19_.where_ref, f32[256,768]{1,0:T(8,128)} %get-tuple-element.116.own, f32[32,768]{1,0:T(8,128)} %get-tuple-element.117.f0, bf16[160,768]{1,0:T(8,128)(2,1)} %collective-permute-done.40.r1, bf16[32,768]{1,0:T(8,128)(2,1)} %copy-done.30, ...), custom_call_target="tpu_custom_call" | custom-call | tf_op jit(solution)/shard_map/post/pallas_call | solution.py:542
  263.2 10.3 %collective-permute-done.50 = bf16[2,96,768]{2,1,0:T(8,128)(2,1)} collective-permute-done((bf16[2,96,768]{2,1,0:T(8,128)(2,1)}, bf16[2,96,768]{2,1,0:T(8,128)(2,1)}, u32[]{:S(2)}, u32[]{:S(2)}) %collective-permute-start.50) | collective-permute-done | bytes 294944 | tf_op jit(solution)/shard_map/ppermute | solution.py:575
  292.1 7.2 %collective-permute-done.60 = bf16[2,96,768]{2,1,0:T(8,128)(2,1)S(1)} collective-permute-done((bf16[2,96,768]{2,1,0:T(8,128)(2,1)S(1)}, bf16[2,96,768]{2,1,0:T(8,128)(2,1)S(1)}, u32[]{:S(2)}, u32[]{:S(2)}) %collective-permute-start.60) | collective-permute-done | bytes 294944 | tf_op jit(solution)/shard_map/ppermute | solution.py:575
  299.3 3.6 collective-permute-done.59
  310.4 9.5 %collective-permute-done.69 = bf16[2,96,1536]{2,1,0:T(8,128)(2,1)S(1)} collective-permute-done((bf16[2,96,1536]{2,1,0:T(8,128)(2,1)S(1)}, bf16[2,96,1536]{2,1,0:T(8,128)(2,1)S(1)}, u32[]{:S(2)}, u32[]{:S(2)}) %collective-permute-start.69) | collective-permute-done | bytes 589856 | tf_op jit(solution)/shard_map/ppermute | solution.py:575
  320.0 12.7 %collective-permute-done.71 = bf16[2,96,1536]{2,1,0:T(8,128)(2,1)S(1)} collective-permute-done((bf16[2,96,1536]{2,1,0:T(8,128)(2,1)S(1)}, bf16[2,96,1536]{2,1,0:T(8,128)(2,1)S(1)}, u32[]{:S(2)}, u32[]{:S(2)}) %collective-permute-start.71) | collective-permute-done | bytes 589856 | tf_op jit(solution)/shard_map/ppermute | solution.py:575
  335.5 9.8 %collective-permute-done.64 = bf16[2,96,1536]{2,1,0:T(8,128)(2,1)S(1)} collective-permute-done((bf16[2,96,1536]{2,1,0:T(8,128)(2,1)S(1)}, bf16[2,96,1536]{2,1,0:T(8,128)(2,1)S(1)}, u32[]{:S(2)}, u32[]{:S(2)}) %collective-permute-start.64) | collective-permute-done | bytes 589856 | tf_op jit(solution)/shard_map/ppermute | solution.py:575
  346.2 10.8 %collective-permute-done.66 = bf16[2,96,1536]{2,1,0:T(8,128)(2,1)S(1)} collective-permute-done((bf16[2,96,1536]{2,1,0:T(8,128)(2,1)S(1)}, bf16[2,96,1536]{2,1,0:T(8,128)(2,1)S(1)}, u32[]{:S(2)}, u32[]{:S(2)}) %collective-permute-start.66) | collective-permute-done | bytes 589856 | tf_op jit(solution)/shard_map/ppermute | solution.py:575
  367.3 10.7 %collective-permute-done.72 = bf16[96,1536]{1,0:T(8,128)(2,1)S(1)} collective-permute-done((bf16[96,1536]{1,0:T(8,128)(2,1)S(1)}, bf16[96,1536]{1,0:T(8,128)(2,1)S(1)}, u32[]{:S(2)}, u32[]{:S(2)}) %collective-permute-start.72) | collective-permute-done | bytes 294944 | tf_op jit(solution)/shard_map/ppermute | solution.py:575
  378.1 3.6 collective-permute-done.67
  (277 shorter events, 128.2 us)
Async XLA Ops:
  7.0 35.6 %collective-permute-start.5 = (bf16[128,768]{1,0:T(8,128)(2,1)S(1)}, bf16[128,768]{1,0:T(8,128)(2,1)}, u32[]{:S(2)}, u32[]{:S(2)}) collective-permute-start(bf16[128,768]{1,0:T(8,128)(2,1)S(1)} %get-tuple-element.180), channel_id=1, source_target_pairs={{1,0},{2,1},{3,2},{5,4},{6,5},{7,6},{9,8},{10,9},{11,10},{13,12},{... | collective-permute-start | bytes 589832 | tf_op jit(solution)/shard_map/ppermute | solution.py:655
  8.3 34.5 %collective-permute-start.4 = (bf16[128,768]{1,0:T(8,128)(2,1)S(1)}, bf16[128,768]{1,0:T(8,128)(2,1)S(1)}, u32[]{:S(2)}, u32[]{:S(2)}) collective-permute-start(bf16[128,768]{1,0:T(8,128)(2,1)S(1)} %get-tuple-element.181), channel_id=1, source_target_pairs={{0,1},{1,2},{2,3},{4,5},{5,6},{6,7},{8,9},{9,10},{10,11},{12,13},{... | collective-permute-start | bytes 589832 | tf_op jit(solution)/shard_map/ppermute | solution.py:654
  18.1 25.9 %collective-permute-start.32 = (bf16[96,2304]{1,0:T(8,128)(2,1)}, bf16[96,2304]{1,0:T(8,128)(2,1)S(1)}, u32[]{:S(2)}, u32[]{:S(2)}) collective-permute-start(bf16[96,2304]{1,0:T(8,128)(2,1)} %pack.1.refs_6_.refs_2_.refs_7_), channel_id=1, source_target_pairs={{0,4},{4,0},{8,12},{12,8},{16,20},{20,16},{24,28},{28,24},{1,5},{5... | collective-permute-start | bytes 1327112 | tf_op jit(solution)/shard_map/ppermute | solution.py:575
  44.0 23.4 %collective-permute-start.17 = (bf16[96,2304]{1,0:T(8,128)(2,1)S(1)}, bf16[96,2304]{1,0:T(8,128)(2,1)S(1)}, u32[]{:S(2)}, u32[]{:S(2)}) collective-permute-start(bf16[96,2304]{1,0:T(8,128)(2,1)S(1)} %copy-done), channel_id=1, source_target_pairs={{0,3},{1,2},{2,1},{3,0},{4,7},{5,6},{6,5},{7,4},{8,11},{9,10},{10,... | collective-permute-start | bytes 1327112 | tf_op jit(solution)/shard_map/ppermute | solution.py:575
  53.2 30.5 %collective-permute-start.9 = (bf16[96,2304]{1,0:T(8,128)(2,1)S(1)}, bf16[96,2304]{1,0:T(8,128)(2,1)}, u32[]{:S(2)}, u32[]{:S(2)}) collective-permute-start(bf16[96,2304]{1,0:T(8,128)(2,1)S(1)} %copy-done), channel_id=1, source_target_pairs={{0,2},{1,3},{2,0},{3,1},{4,6},{5,7},{6,4},{7,5},{8,10},{9,11},{10,... | collective-permute-start | bytes 1327112 | tf_op jit(solution)/shard_map/ppermute | solution.py:575
  60.8 24.4 %collective-permute-start.35 = (bf16[96,2304]{1,0:T(8,128)(2,1)S(1)}, bf16[96,2304]{1,0:T(8,128)(2,1)S(1)}, u32[]{:S(2)}, u32[]{:S(2)}) collective-permute-start(bf16[96,2304]{1,0:T(8,128)(2,1)S(1)} %collective-permute-done.31.refs_9_.refs_5_.refs_10_), channel_id=1, source_target_pairs={{0,4},{4,0},{8,12},{12,8},{16,20},{20,16},{24,28},{28,24},{1,5},{5... | collective-permute-start | bytes 1327112 | tf_op jit(solution)/shard_map/ppermute | solution.py:575
  60.8 25.9 %collective-permute-start.34 = (bf16[96,2304]{1,0:T(8,128)(2,1)S(1)}, bf16[96,2304]{1,0:T(8,128)(2,1)S(1)}, u32[]{:S(2)}, u32[]{:S(2)}) collective-permute-start(bf16[96,2304]{1,0:T(8,128)(2,1)S(1)} %collective-permute-done.30.refs_8_.refs_4_.refs_9_), channel_id=1, source_target_pairs={{0,4},{4,0},{8,12},{12,8},{16,20},{20,16},{24,28},{28,24},{1,5},{5... | collective-permute-start | bytes 1327112 | tf_op jit(solution)/shard_map/ppermute | solution.py:575
  61.3 25.4 %collective-permute-start.33 = (bf16[96,2304]{1,0:T(8,128)(2,1)S(1)}, bf16[96,2304]{1,0:T(8,128)(2,1)}, u32[]{:S(2)}, u32[]{:S(2)}) collective-permute-start(bf16[96,2304]{1,0:T(8,128)(2,1)S(1)} %collective-permute-done.29.refs_7_.refs_3_.refs_8_), channel_id=1, source_target_pairs={{0,4},{4,0},{8,12},{12,8},{16,20},{20,16},{24,28},{28,24},{1,5},{5... | collective-permute-start | bytes 1327112 | tf_op jit(solution)/shard_map/ppermute | solution.py:575
  83.7 20.2 %collective-permute-start.27 = (bf16[96,2304]{1,0:T(8,128)(2,1)S(1)}, bf16[96,2304]{1,0:T(8,128)(2,1)S(1)}, u32[]{:S(2)}, u32[]{:S(2)}) collective-permute-start(bf16[96,2304]{1,0:T(8,128)(2,1)S(1)} %collective-permute-done.25.refs_14_.refs_10_.refs_7_), channel_id=1, source_target_pairs={{0,16},{4,20},{8,24},{12,28},{16,0},{20,4},{24,8},{28,12},{1,17},{... | collective-permute-start | bytes 1327112 | tf_op jit(solution)/shard_map/ppermute | solution.py:575
  85.1 20.9 %collective-permute-start.26 = (bf16[96,2304]{1,0:T(8,128)(2,1)S(1)}, bf16[96,2304]{1,0:T(8,128)(2,1)S(1)}, u32[]{:S(2)}, u32[]{:S(2)}) collective-permute-start(bf16[96,2304]{1,0:T(8,128)(2,1)S(1)} %collective-permute-done.25.refs_14_.refs_10_.refs_7_), channel_id=1, source_target_pairs={{0,8},{4,12},{8,0},{12,4},{16,24},{20,28},{24,16},{28,20},{1,9},{5... | collective-permute-start | bytes 1327112 | tf_op jit(solution)/shard_map/ppermute | solution.py:575
  86.7 19.4 %collective-permute-start.21 = (bf16[96,2304]{1,0:T(8,128)(2,1)}, bf16[96,2304]{1,0:T(8,128)(2,1)}, u32[]{:S(2)}, u32[]{:S(2)}) collective-permute-start(bf16[96,2304]{1,0:T(8,128)(2,1)} %copy-done.15), channel_id=1, source_target_pairs={{0,4},{4,0},{8,12},{12,8},{16,20},{20,16},{24,28},{28,24},{1,5},{5... | collective-permute-start | bytes 1327112 | tf_op jit(solution)/shard_map/ppermute | solution.py:575
  86.7 21.1 %collective-permute-start.20 = (bf16[96,2304]{1,0:T(8,128)(2,1)}, bf16[96,2304]{1,0:T(8,128)(2,1)}, u32[]{:S(2)}, u32[]{:S(2)}) collective-permute-start(bf16[96,2304]{1,0:T(8,128)(2,1)} %copy-done.15), channel_id=1, source_target_pairs={{0,24},{4,28},{8,16},{12,20},{16,8},{20,12},{24,0},{28,4},{1,25},{... | collective-permute-start | bytes 1327112 | tf_op jit(solution)/shard_map/ppermute | solution.py:575
  87.3 34.4 %collective-permute-start.19 = (bf16[96,2304]{1,0:T(8,128)(2,1)}, bf16[96,2304]{1,0:T(8,128)(2,1)}, u32[]{:S(2)}, u32[]{:S(2)}) collective-permute-start(bf16[96,2304]{1,0:T(8,128)(2,1)} %copy-done.15), channel_id=1, source_target_pairs={{0,16},{4,20},{8,24},{12,28},{16,0},{20,4},{24,8},{28,12},{1,17},{... | collective-permute-start | bytes 1327112 | tf_op jit(solution)/shard_map/ppermute | solution.py:575
  103.9 27.0 %collective-permute-start.18 = (bf16[96,2304]{1,0:T(8,128)(2,1)}, bf16[96,2304]{1,0:T(8,128)(2,1)}, u32[]{:S(2)}, u32[]{:S(2)}) collective-permute-start(bf16[96,2304]{1,0:T(8,128)(2,1)} %copy-done.15), channel_id=1, source_target_pairs={{0,8},{4,12},{8,0},{12,4},{16,24},{20,28},{24,16},{28,20},{1,9},{5... | collective-permute-start | bytes 1327112 | tf_op jit(solution)/shard_map/ppermute | solution.py:575
  106.0 24.9 %collective-permute-start.13 = (bf16[96,2304]{1,0:T(8,128)(2,1)}, bf16[96,2304]{1,0:T(8,128)(2,1)}, u32[]{:S(2)}, u32[]{:S(2)}) collective-permute-start(bf16[96,2304]{1,0:T(8,128)(2,1)} %collective-permute-done.9.refs_6_.refs_2_.refs_7_), channel_id=1, source_target_pairs={{0,4},{4,0},{8,12},{12,8},{16,20},{20,16},{24,28},{28,24},{1,5},{5... | collective-permute-start | bytes 1327112 | tf_op jit(solution)/shard_map/ppermute | solution.py:575
  106.1 25.4 %collective-permute-start.12 = (bf16[96,2304]{1,0:T(8,128)(2,1)}, bf16[96,2304]{1,0:T(8,128)(2,1)}, u32[]{:S(2)}, u32[]{:S(2)}) collective-permute-start(bf16[96,2304]{1,0:T(8,128)(2,1)} %collective-permute-done.9.refs_6_.refs_2_.refs_7_), channel_id=1, source_target_pairs={{0,24},{4,28},{8,16},{12,20},{16,8},{20,12},{24,0},{28,4},{1,25},{... | collective-permute-start | bytes 1327112 | tf_op jit(solution)/shard_map/ppermute | solution.py:575
  107.8 23.7 %collective-permute-start.11 = (bf16[96,2304]{1,0:T(8,128)(2,1)}, bf16[96,2304]{1,0:T(8,128)(2,1)}, u32[]{:S(2)}, u32[]{:S(2)}) collective-permute-start(bf16[96,2304]{1,0:T(8,128)(2,1)} %collective-permute-done.9.refs_6_.refs_2_.refs_7_), channel_id=1, source_target_pairs={{0,16},{4,20},{8,24},{12,28},{16,0},{20,4},{24,8},{28,12},{1,17},{... | collective-permute-start | bytes 1327112 | tf_op jit(solution)/shard_map/ppermute | solution.py:575
  219.9 33.4 %collective-permute-start.47 = (bf16[1,384,768]{2,1,0:T(8,128)(2,1)}, bf16[1,384,768]{2,1,0:T(8,128)(2,1)}, u32[]{:S(2)}, u32[]{:S(2)}) collective-permute-start(bf16[1,384,768]{2,1,0:T(8,128)(2,1)} %get-tuple-element.134), channel_id=1, source_target_pairs={{0,4},{4,0},{8,12},{12,8},{16,20},{20,16},{24,28},{28,24},{1,5},{5... | collective-permute-start | bytes 1769480 | tf_op jit(solution)/shard_map/ppermute | solution.py:575
  220.3 35.1 %collective-permute-start.48 = (bf16[1,384,768]{2,1,0:T(8,128)(2,1)}, bf16[1,384,768]{2,1,0:T(8,128)(2,1)}, u32[]{:S(2)}, u32[]{:S(2)}) collective-permute-start(bf16[1,384,768]{2,1,0:T(8,128)(2,1)} %get-tuple-element.136), channel_id=1, source_target_pairs={{0,4},{4,0},{8,12},{12,8},{16,20},{20,16},{24,28},{28,24},{1,5},{5... | collective-permute-start | bytes 1769480 | tf_op jit(solution)/shard_map/ppermute | solution.py:575
  220.4 23.7 %collective-permute-start.40 = (bf16[160,768]{1,0:T(8,128)(2,1)}, bf16[160,768]{1,0:T(8,128)(2,1)}, u32[]{:S(2)}, u32[]{:S(2)}) collective-permute-start(bf16[160,768]{1,0:T(8,128)(2,1)} %get-tuple-element.118), channel_id=1, source_target_pairs={{0,1},{1,0},{2,3},{3,2},{4,5},{5,4},{6,7},{7,6},{8,9},{9,8},{10,11... | collective-permute-start | bytes 737288 | tf_op jit(solution)/shard_map/ppermute | solution.py:575
  243.0 60.1 %collective-permute-start.68 = (bf16[2,384,1536]{2,1,0:T(8,128)(2,1)}, bf16[2,384,1536]{2,1,0:T(8,128)(2,1)S(1)}, u32[]{:S(2)}, u32[]{:S(2)}) collective-permute-start(bf16[2,384,1536]{2,1,0:T(8,128)(2,1)} %get-tuple-element.153), channel_id=1, source_target_pairs={{0,4},{4,0},{8,12},{12,8},{16,20},{20,16},{24,28},{28,24},{1,5},{5... | collective-permute-start | bytes 7077896 | tf_op jit(solution)/shard_map/ppermute | solution.py:575
  243.7 40.3 %collective-permute-start.57 = (bf16[2,384,768]{2,1,0:T(8,128)(2,1)}, bf16[2,384,768]{2,1,0:T(8,128)(2,1)S(1)}, u32[]{:S(2)}, u32[]{:S(2)}) collective-permute-start(bf16[2,384,768]{2,1,0:T(8,128)(2,1)} %get-tuple-element.142), channel_id=1, source_target_pairs={{0,4},{4,0},{8,12},{12,8},{16,20},{20,16},{24,28},{28,24},{1,5},{5... | collective-permute-start | bytes 3538952 | tf_op jit(solution)/shard_map/ppermute | solution.py:575
  273.5 33.8 %collective-permute-start.63 = (bf16[2,384,1536]{2,1,0:T(8,128)(2,1)}, bf16[2,384,1536]{2,1,0:T(8,128)(2,1)S(1)}, u32[]{:S(2)}, u32[]{:S(2)}) collective-permute-start(bf16[2,384,1536]{2,1,0:T(8,128)(2,1)} %get-tuple-element.151), channel_id=1, source_target_pairs={{0,4},{4,0},{8,12},{12,8},{16,20},{20,16},{24,28},{28,24},{1,5},{5... | collective-permute-start | bytes 7077896 | tf_op jit(solution)/shard_map/ppermute | solution.py:575
  299.3 63.5 %collective-permute-start.56 = (bf16[96,768]{1,0:T(8,128)(2,1)S(1)}, bf16[96,768]{1,0:T(8,128)(2,1)S(1)}, u32[]{:S(2)}, u32[]{:S(2)}) collective-permute-start(bf16[96,768]{1,0:T(8,128)(2,1)S(1)} %get-tuple-element.184), channel_id=1, source_target_pairs={{0,1},{1,0},{2,3},{3,2},{4,5},{5,4},{6,7},{7,6},{8,9},{9,8},{10,11... | collective-permute-start | bytes 442376 | tf_op jit(solution)/shard_map/ppermute | solution.py:575
  303.8 28.9 %collective-permute-start.71 = (bf16[2,96,1536]{2,1,0:T(8,128)(2,1)S(1)}, bf16[2,96,1536]{2,1,0:T(8,128)(2,1)S(1)}, u32[]{:S(2)}, u32[]{:S(2)}) collective-permute-start(bf16[2,96,1536]{2,1,0:T(8,128)(2,1)S(1)} %get-tuple-element.162), channel_id=1, source_target_pairs={{0,24},{4,28},{8,16},{12,20},{16,8},{20,12},{24,0},{28,4},{1,25},{... | collective-permute-start | bytes 1769480 | tf_op jit(solution)/shard_map/ppermute | solution.py:575
  305.9 27.8 %collective-permute-start.70 = (bf16[2,96,1536]{2,1,0:T(8,128)(2,1)S(1)}, bf16[2,96,1536]{2,1,0:T(8,128)(2,1)S(1)}, u32[]{:S(2)}, u32[]{:S(2)}) collective-permute-start(bf16[2,96,1536]{2,1,0:T(8,128)(2,1)S(1)} %get-tuple-element.163), channel_id=1, source_target_pairs={{0,16},{4,20},{8,24},{12,28},{16,0},{20,4},{24,8},{28,12},{1,17},{... | collective-permute-start | bytes 1769480 | tf_op jit(solution)/shard_map/ppermute | solution.py:575
  307.3 57.4 %collective-permute-start.62 = (bf16[96,768]{1,0:T(8,128)(2,1)S(1)}, bf16[96,768]{1,0:T(8,128)(2,1)S(1)}, u32[]{:S(2)}, u32[]{:S(2)}) collective-permute-start(bf16[96,768]{1,0:T(8,128)(2,1)S(1)} %get-tuple-element.182), channel_id=1, source_target_pairs={{0,3},{1,2},{2,1},{3,0},{4,7},{5,6},{6,5},{7,4},{8,11},{9,10},{10,... | collective-permute-start | bytes 442376 | tf_op jit(solution)/shard_map/ppermute | solution.py:575
  319.9 25.3 %collective-permute-start.64 = (bf16[2,96,1536]{2,1,0:T(8,128)(2,1)S(1)}, bf16[2,96,1536]{2,1,0:T(8,128)(2,1)S(1)}, u32[]{:S(2)}, u32[]{:S(2)}) collective-permute-start(bf16[2,96,1536]{2,1,0:T(8,128)(2,1)S(1)} %get-tuple-element.158), channel_id=1, source_target_pairs={{0,8},{4,12},{8,0},{12,4},{16,24},{20,28},{24,16},{28,20},{1,9},{5... | collective-permute-start | bytes 1769480 | tf_op jit(solution)/shard_map/ppermute | solution.py:575
  332.7 24.3 %collective-permute-start.66 = (bf16[2,96,1536]{2,1,0:T(8,128)(2,1)S(1)}, bf16[2,96,1536]{2,1,0:T(8,128)(2,1)S(1)}, u32[]{:S(2)}, u32[]{:S(2)}) collective-permute-start(bf16[2,96,1536]{2,1,0:T(8,128)(2,1)S(1)} %get-tuple-element.159), channel_id=1, source_target_pairs={{0,24},{4,28},{8,16},{12,20},{16,8},{20,12},{24,0},{28,4},{1,25},{... | collective-permute-start | bytes 1769480 | tf_op jit(solution)/shard_map/ppermute | solution.py:575
  333.6 26.0 %collective-permute-start.65 = (bf16[2,96,1536]{2,1,0:T(8,128)(2,1)S(1)}, bf16[2,96,1536]{2,1,0:T(8,128)(2,1)S(1)}, u32[]{:S(2)}, u32[]{:S(2)}) collective-permute-start(bf16[2,96,1536]{2,1,0:T(8,128)(2,1)S(1)} %get-tuple-element.160), channel_id=1, source_target_pairs={{0,16},{4,20},{8,24},{12,28},{16,0},{20,4},{24,8},{28,12},{1,17},{... | collective-permute-start | bytes 1769480 | tf_op jit(solution)/shard_map/ppermute | solution.py:575
  345.3 19.4 %collective-permute-start.61 = (bf16[96,768]{1,0:T(8,128)(2,1)S(1)}, bf16[96,768]{1,0:T(8,128)(2,1)S(1)}, u32[]{:S(2)}, u32[]{:S(2)}) collective-permute-start(bf16[96,768]{1,0:T(8,128)(2,1)S(1)} %get-tuple-element.183), channel_id=1, source_target_pairs={{0,2},{1,3},{2,0},{3,1},{4,6},{5,7},{6,4},{7,5},{8,10},{9,11},{10,... | collective-permute-start | bytes 442376 | tf_op jit(solution)/shard_map/ppermute | solution.py:575
  357.0 21.1 %collective-permute-start.72 = (bf16[96,1536]{1,0:T(8,128)(2,1)S(1)}, bf16[96,1536]{1,0:T(8,128)(2,1)S(1)}, u32[]{:S(2)}, u32[]{:S(2)}) collective-permute-start(bf16[96,1536]{1,0:T(8,128)(2,1)S(1)} %get-tuple-element.178), channel_id=1, source_target_pairs={{0,2},{1,3},{2,0},{3,1},{4,6},{5,7},{6,4},{7,5},{8,10},{9,11},{10,... | collective-permute-start | bytes 884744 | tf_op jit(solution)/shard_map/ppermute | solution.py:575
  (76 other events, 1103.3 us)
